TPU v7x, 32 devices: a whole 2x2x4 slice. The times are simulated.
32 devices in a mesh: dp: 8 (over y, x, core), seq: 4 (over z).
Axes of the slice: x: 2, y: 2, z: 4, core: 2. Of those that a mesh axis runs over, the one named last changes fastest.
Arguments:
- block_input: bfloat16 [24, 1024, 1024], P('dp', 'seq'), may hold values from -6 to 6
- seg_start: int32 [24, 1024], P('dp'), may hold values from 0 to 1023, as said below
- ln1_gain: float32 [1024], replicated, may hold values from 0.5 to 1.5
- ln1_bias: float32 [1024], replicated, may hold values from -1.75 to 1.75
- qkv_weight: bfloat16 [1024, 3072], P('dp'), may hold values from -0.1875 to 0.1875
- query_bias: float32 [1024], replicated, may hold values from -1.75 to 1.75
- value_bias: float32 [1024], replicated, may hold values from -1.75 to 1.75
- query_adapter_reduce: bfloat16 [1024, 4], replicated, may hold values from -0.1875 to 0.1875
- query_up: bfloat16 [4, 1024], replicated, may hold values from -0.1875 to 0.1875
- value_adapter_reduce: bfloat16 [1024, 4], replicated, may hold values from -0.1875 to 0.1875
- value_up: bfloat16 [4, 1024], replicated, may hold values from -0.1875 to 0.1875
- out_weight: bfloat16 [1024, 1024], P('dp'), may hold values from -0.75 to 0.75
- out_bias: float32 [1024], replicated, may hold values from -1.75 to 1.75
- ln2_gain: float32 [1024], replicated, may hold values from 0.5 to 1.5
- ln2_bias: float32 [1024], replicated, may hold values from -1.75 to 1.75
- fc_weight: bfloat16 [1024, 4096], P('dp'), may hold values from -0.1875 to 0.1875
- fc_bias: float32 [4096], replicated, may hold values from -1.75 to 1.75
- proj_weight: bfloat16 [4096, 1024], P('dp'), may hold values from -0.09375 to 0.09375
- proj_bias: float32 [1024], replicated, may hold values from -1.75 to 1.75
- grad_out: bfloat16 [24, 1024, 1024], P('dp', 'seq'), may hold values from -6 to 6
Outputs:
- block_output: bfloat16 [24, 1024, 1024], P('dp', 'seq')
- grad_input: float32 [24, 1024, 1024], P('dp', 'seq')
- grad_query_down: float32 [1024, 4], replicated
- grad_query_up: float32 [4, 1024], replicated
- grad_value_down: float32 [1024, 4], replicated
- grad_value_up: float32 [4, 1024], replicated
Inputs may be any that keep to these rules, and one draw needn't show every extreme that they name: `seg_start`: each entry is the first position of its token's document within the row: it is at most the token's own position, position 0 has 0, and equal entries form runs of consecutive tokens whose start is the entry itself. The last position of every row starts its own document. In every row one document begins within the row's first 1 / N of positions and ends within its last 1 / N, N being the number of devices along seq.
All inputs are finite; a program needn't handle non-finite values.
Results may differ from a plain program's by a relative error of at most 0.014.
Values may be sent and summed in bfloat16 or wider, within the bound.
A program may use at most 192 MiB of HBM per device.

v0:
```python
from functools import partial

import jax
import jax.numpy as jnp
from jax import lax
from jax.sharding import PartitionSpec as P

HEAD = 64


NORM_EPSILON = 1e-05
ADAPTER_SCALE = 8.0
MASKED = -1e30


def for_sending(value):

    def short(part):
        return part.astype(jnp.bfloat16) if part.dtype == jnp.float32 else part

    return jax.tree.map(short, value)


def norm_forward(row_values, norm_gain, norm_shift):
    average = jnp.mean(row_values, axis=-1, keepdims=True)
    centered = row_values - average
    inverse = lax.rsqrt(jnp.mean(centered * centered, axis=-1, keepdims=True) + NORM_EPSILON)
    normed = centered * inverse
    return (normed * norm_gain + norm_shift, normed, inverse)


def norm_backward(gradient, normed, inverse, norm_gain):
    scaled = gradient * norm_gain
    return inverse * (
        scaled
        - jnp.mean(scaled, axis=-1, keepdims=True)
        - normed * jnp.mean(scaled * normed, axis=-1, keepdims=True)
    )


def fold_with(left_side, total_sum, weight_piece):
    columns = lax.slice_in_dim(left_side, 0, weight_piece.shape[0], axis=1)
    return total_sum + jnp.dot(columns, weight_piece, preferred_element_type=jnp.float32)


def times_transposed(left_side, right_side):
    return lax.dot_general(
        left_side, right_side, (((1,), (1,)), ((), ())), preferred_element_type=jnp.float32
    )


def across_token_rows(left_side, right_side):
    return lax.dot_general(
        left_side, right_side, (((0,), (0,)), ((), ())), preferred_element_type=jnp.float32
    )


def map_with(left_side, weight_piece):
    return times_transposed(left_side, weight_piece)


def mask_for(document_starts, offset, block_rows, length):
    query_pos = offset + jnp.arange(block_rows, dtype=jnp.int32)
    key_pos = jnp.arange(length, dtype=jnp.int32)
    query_start = document_starts[offset : offset + block_rows]
    return (key_pos[None, :] <= query_pos[:, None]) & (key_pos[None, :] >= query_start[:, None])


def split_heads(head_layout):
    length = head_layout.shape[0]
    head_count = head_layout.shape[2] // HEAD
    return (
        head_layout[:, 0].reshape(length, head_count, HEAD),
        head_layout[:, 1].reshape(length, head_count, HEAD),
        head_layout[:, 2].reshape(length, head_count, HEAD),
    )


def attend_row(row_entry):
    head_layout, document_starts = row_entry
    query_heads, key_heads, value_heads = split_heads(head_layout)
    length = head_layout.shape[0]
    block_rows = min(512, length)
    score_scale = HEAD ** (-0.5)
    mixed_parts = []
    total_parts = []
    for offset in range(0, length, block_rows):
        allowed = mask_for(document_starts, offset, block_rows, length)
        scores = (
            jnp.einsum(
                "qhd,khd->hqk",
                query_heads[offset : offset + block_rows],
                key_heads,
                preferred_element_type=jnp.float32,
            )
            * score_scale
        )
        scores = jnp.where(allowed[None], scores, MASKED)
        highest = jnp.max(scores, axis=-1, keepdims=True)
        weights = jnp.exp(scores - highest)
        denominator = jnp.sum(weights, axis=-1, keepdims=True)
        probabilities = (weights / denominator).astype(jnp.bfloat16)
        mixed_rows = jnp.einsum(
            "hqk,khd->qhd", probabilities, value_heads, preferred_element_type=jnp.float32
        )
        mixed_parts.append(mixed_rows.reshape(block_rows, -1))
        total_parts.append((highest + jnp.log(denominator))[:, :, 0])
    return (jnp.concatenate(mixed_parts, 0).astype(jnp.bfloat16), jnp.concatenate(total_parts, 1))


def attend_back(row_entry):
    head_layout, grad_mixed, log_total, document_starts = row_entry
    query_heads, key_heads, value_heads = split_heads(head_layout)
    length = head_layout.shape[0]
    head_count = query_heads.shape[1]
    grad_heads = grad_mixed.reshape(length, head_count, HEAD)
    block_rows = min(512, length)
    score_scale = HEAD ** (-0.5)
    grad_keys = jnp.zeros(key_heads.shape, jnp.float32)
    grad_values = jnp.zeros(value_heads.shape, jnp.float32)
    query_parts = []
    for offset in range(0, length, block_rows):
        allowed = mask_for(document_starts, offset, block_rows, length)
        query_block = query_heads[offset : offset + block_rows]
        grad_block = grad_heads[offset : offset + block_rows]
        scores = (
            jnp.einsum("qhd,khd->hqk", query_block, key_heads, preferred_element_type=jnp.float32)
            * score_scale
        )
        scores = jnp.where(allowed[None], scores, MASKED)
        probabilities = jnp.exp(scores - log_total[:, offset : offset + block_rows, None])
        grad_probs = jnp.einsum(
            "qhd,khd->hqk", grad_block, value_heads, preferred_element_type=jnp.float32
        )
        inner_sum = jnp.sum(probabilities * grad_probs, axis=-1, keepdims=True)
        grad_scores = (probabilities * (grad_probs - inner_sum)).astype(jnp.bfloat16)
        query_parts.append(
            jnp.einsum("hqk,khd->qhd", grad_scores, key_heads, preferred_element_type=jnp.float32)
            * score_scale
        )
        grad_keys = (
            grad_keys
            + jnp.einsum(
                "hqk,qhd->khd", grad_scores, query_block, preferred_element_type=jnp.float32
            )
            * score_scale
        )
        grad_values = grad_values + jnp.einsum(
            "hqk,qhd->khd",
            probabilities.astype(jnp.bfloat16),
            grad_block,
            preferred_element_type=jnp.float32,
        )
    grad_query = jnp.concatenate(query_parts, 0)
    return jnp.stack(
        [
            grad_query.reshape(length, -1),
            grad_keys.reshape(length, -1),
            grad_values.reshape(length, -1),
        ],
        axis=1,
    ).astype(jnp.bfloat16)


def on_device(
    block_input,
    seg_start,
    ln1_gain,
    ln1_bias,
    qkv_weight,
    query_bias,
    value_bias,
    query_adapter_reduce,
    query_up,
    value_adapter_reduce,
    value_up,
    out_weight,
    out_bias,
    ln2_gain,
    ln2_bias,
    fc_weight,
    fc_bias,
    proj_weight,
    proj_bias,
    grad_out,
):
    groups = block_input.shape[0]
    row_span = block_input.shape[1]
    model_width = block_input.shape[2]
    tokens = groups * row_span
    hidden_units = fc_weight.shape[1]
    row_values = block_input.reshape(tokens, model_width).astype(jnp.float32)
    normed_first, unit_first, inverse_first = norm_forward(row_values, ln1_gain, ln1_bias)
    first_hidden_layer = normed_first.astype(jnp.bfloat16)
    projected = fold_with(
        first_hidden_layer,
        jnp.zeros((tokens, 3 * model_width), jnp.float32),
        lax.all_gather(qkv_weight, "dp", axis=0, tiled=True),
    )
    query_reduce = (
        jnp.dot(first_hidden_layer, query_adapter_reduce, preferred_element_type=jnp.float32)
        * ADAPTER_SCALE
    ).astype(jnp.bfloat16)
    value_reduce = (
        jnp.dot(first_hidden_layer, value_adapter_reduce, preferred_element_type=jnp.float32)
        * ADAPTER_SCALE
    ).astype(jnp.bfloat16)
    split_parts = projected.reshape(tokens, 3, model_width)
    queries = (
        split_parts[:, 0]
        + query_bias
        + jnp.dot(query_reduce, query_up, preferred_element_type=jnp.float32)
    )
    valued = (
        split_parts[:, 2]
        + value_bias
        + jnp.dot(value_reduce, value_up, preferred_element_type=jnp.float32)
    )
    token_layout = jnp.stack([queries, split_parts[:, 1], valued], axis=1).astype(jnp.bfloat16)
    token_layout = token_layout.reshape(groups, row_span, 3, model_width)
    head_layout = lax.all_to_all(token_layout, "seq", split_axis=3, concat_axis=1, tiled=True)
    attended, log_totals = lax.map(attend_row, (head_layout, seg_start))
    mixed_tokens = jax.tree.map(
        lambda part, own: part.astype(own.dtype),
        lax.all_to_all(for_sending(attended), "seq", split_axis=1, concat_axis=2, tiled=True),
        attended,
    ).reshape(tokens, model_width)
    attention_out = fold_with(
        mixed_tokens,
        jnp.zeros((tokens, model_width), jnp.float32),
        lax.all_gather(out_weight, "dp", axis=0, tiled=True),
    )
    middle = row_values + attention_out + out_bias
    normed_second, unit_second, inverse_second = norm_forward(middle, ln2_gain, ln2_bias)
    hidden_second = normed_second.astype(jnp.bfloat16)
    before = (
        fold_with(
            hidden_second,
            jnp.zeros((tokens, hidden_units), jnp.float32),
            lax.all_gather(fc_weight, "dp", axis=0, tiled=True),
        )
        + fc_bias
    )
    gelu_value, gelu_pull = jax.vjp(partial(jax.nn.gelu, approximate=True), before)
    activated = gelu_value.astype(jnp.bfloat16)
    feed_out = fold_with(
        activated,
        jnp.zeros((tokens, model_width), jnp.float32),
        lax.all_gather(proj_weight, "dp", axis=0, tiled=True),
    )
    result_rows = middle + feed_out + proj_bias
    block_output = result_rows.astype(jnp.bfloat16).reshape(groups, row_span, model_width)
    gradient_row_list = grad_out.reshape(tokens, model_width)
    grad_act = map_with(gradient_row_list, lax.all_gather(proj_weight, "dp", axis=0, tiled=True))
    grad_before = gelu_pull(grad_act)[0].astype(jnp.bfloat16)
    grad_second = map_with(grad_before, lax.all_gather(fc_weight, "dp", axis=0, tiled=True))
    grad_middle = gradient_row_list.astype(jnp.float32) + norm_backward(
        grad_second, unit_second, inverse_second, ln2_gain
    )
    grad_attended = grad_middle.astype(jnp.bfloat16)
    grad_mixed = map_with(grad_attended, lax.all_gather(out_weight, "dp", axis=0, tiled=True))
    grad_mixed = grad_mixed.astype(jnp.bfloat16).reshape(groups, row_span, model_width)
    grad_head_layout = lax.all_to_all(grad_mixed, "seq", split_axis=2, concat_axis=1, tiled=True)
    grad_projected = lax.map(attend_back, (head_layout, grad_head_layout, log_totals, seg_start))
    grad_tokens = lax.all_to_all(
        grad_projected, "seq", split_axis=1, concat_axis=3, tiled=True
    ).reshape(tokens, 3 * model_width)
    grad_first = map_with(grad_tokens, lax.all_gather(qkv_weight, "dp", axis=0, tiled=True))
    grad_query = grad_tokens[:, :model_width]
    grad_value = grad_tokens[:, 2 * model_width :]
    gradient_query_reduce = times_transposed(grad_query, query_up).astype(jnp.bfloat16)
    gradient_value_reduce = times_transposed(grad_value, value_up).astype(jnp.bfloat16)
    grad_first = (
        grad_first
        + (
            times_transposed(gradient_query_reduce, query_adapter_reduce)
            + times_transposed(gradient_value_reduce, value_adapter_reduce)
        )
        * ADAPTER_SCALE
    )
    grad_input = grad_middle + norm_backward(grad_first, unit_first, inverse_first, ln1_gain)
    shard_query_reduce = (
        across_token_rows(first_hidden_layer, gradient_query_reduce) * ADAPTER_SCALE
    )
    local_query_up = across_token_rows(query_reduce, grad_query)
    shard_value_reduce = (
        across_token_rows(first_hidden_layer, gradient_value_reduce) * ADAPTER_SCALE
    )
    local_value_up = across_token_rows(value_reduce, grad_value)
    summed = lax.psum(
        (shard_query_reduce, local_query_up, shard_value_reduce, local_value_up), ("dp", "seq")
    )
    return (
        block_output,
        grad_input.reshape(groups, row_span, model_width),
        summed[0],
        summed[1],
        summed[2],
        summed[3],
    )


def solution(mesh):
    return jax.shard_map(
        on_device,
        mesh=mesh,
        in_specs=(
            P("dp", "seq", None),
            P("dp", None),
            P(),
            P(),
            P("dp", None),
            P(),
            P(),
            P(),
            P(),
            P(),
            P(),
            P("dp", None),
            P(),
            P(),
            P(),
            P("dp", None),
            P(),
            P("dp", None),
            P(),
            P("dp", "seq", None),
        ),
        out_specs=(P("dp", "seq", None), P("dp", "seq", None), P(), P(), P(), P()),
        check_vma=False,
    )
```

profile of v0, /device:TPU:0, one launch (start us, length us, event | category | flops | bytes accessed | tf_op | source)
XLA Modules:
  0.0 918.0 jit_solution(9611403195169453674)
XLA Ops:
  14.8 43.4 %all-gather.5.cloned.1.call-done = bf16[1024,3072]{1,0:T(8,128)(2,1)} async-done(((bf16[128,3072]{1,0:T(8,128)(2,1)}), bf16[1024,3072]{1,0:T(8,128)(2,1)}) %all-gather.5.cloned.1.call-update) | async-done | bytes 6291472 | tf_op jit(solution)/shard_map/all_gather | solution.py:198
  58.2 8.6 copy.34
  66.8 7.4 fusion.118
  93.8 8.3 pad_maximum_fusion.1
  108.0 138.2 %all-to-all-done = bf16[3,256,3,1024]{1,0,2,3:T(4,128)(2,1)} async-done(((bf16[3,256,3,1024]{1,0,2,3:T(4,128)(2,1)}), bf16[3,256,3,1024]{1,0,2,3:T(4,128)(2,1)}, u32[]{:S(2)}, u32[]{:S(2)}) %all-to-all-start) | async-done | bytes 4718624 | tf_op jit(solution)/shard_map/all_to_all | solution.py:221
  246.2 9.4 %copy.38 = bf16[3,4,256,3,256]{2,1,4,3,0:T(4,128)(2,1)} copy(bf16[3,4,256,3,256]{2,0,3,4,1:T(4,128)(2,1)} %bitcast.40) | data formatting | bytes 9437184 | tf_op jit(solution)/shard_map/all_to_all | solution.py:221
  255.6 8.7 all_to_all.51
  264.4 51.6 %while.22 = (s32[]{:T(128)}, bf16[3,1024,256]{1,2,0:T(8,128)(2,1)S(1)}, f32[3,4,1024]{2,1,0:T(4,128)S(1)}, bf16[3,1024,3,256]{1,3,2,0:T(8,128)(2,1)}, s32[3,1024]{1,0:T(4,128)S(1)}, /*index=5*/s32[]{:T(128)}, s32[]{:T(128)}, s32[]{}) while((s32[]{:T(128)}, bf16[3,1024,256]{1,2,0:T(8,128)(2,1)S(1)}, f32[3,4,1024]{2,1,0:T(4,128)S(1)}, ...), condition=%wide.region_7.8_spmd, body=%wide.region_2.7_spmd.sunk | while | flops 1128530432 | bytes 65192060 | solution.py:222
  320.1 51.0 %all_to_all.66 = bf16[3,1024,256]{2,0,1:T(4,128)(2,1)S(1)} all-to-all(bf16[3,1024,256]{2,0,1:T(4,128)(2,1)S(1)} %copy.39), channel_id=1, replica_groups=mesh['dp'=8,'seq'=4] {'seq'}, dimensions={1} | all-to-all | bytes 3145728 | tf_op jit(solution)/shard_map/all_to_all | solution.py:225
  378.7 13.8 %fusion.74 = f32[768,4096]{1,0:T(8,128)} fusion(bf16[1024,4096]{1,0:T(8,128)(2,1)} %all-gather.9.cloned.1.call-done, f32[768,1024]{1,0:T(8,128)} %copy-done.6, f32[1024]{0:T(1024)S(1)} %copy-done.38, f32[1024]{0:T(1024)S(1)} %copy-done.31, f32[768]{0:T(1024)S(1)} %add_rsqrt_fusion, f32[768]{0:T(1024)S(1)} %broadcast_multiply_fusion.4), kind=kOutput, calls=%fused_computation.126 | convolution fusion | flops 6446383104 | bytes 24131584 | tf_op jit(solution)/shard_map/dot_general | solution.py:43
  392.6 27.2 %multiply_reduce_fusion.4 = (f32[768]{0:T(1024)S(1)}, f32[768]{0:T(1024)S(1)}, f32[768,1024]{1,0:T(8,128)}) fusion(f32[1024]{0:T(1024)S(1)} %copy-done.31, f32[768]{0:T(1024)S(1)} %add_rsqrt_fusion, f32[768,1024]{1,0:T(8,128)S(1)} %copy-done.7, f32[768]{0:T(1024)S(1)} %broadcast_multiply_fusion.4, bf16[1024,4096]{1,0:T(8,128)(2,1)} %all-gather.9.cloned.1.call-done, ...), kind=kOutput, calls=%fused_computation.124 | convolution fusion | flops 12955678720 | bytes 37257216 | tf_op jit(solution)/shard_map/dot_general | solution.py:47
  431.0 47.2 %all-to-all-done.2 = bf16[3,256,1024]{1,0,2:T(4,128)(2,1)S(1)} async-done(((bf16[3,256,1024]{1,0,2:T(4,128)(2,1)}), bf16[3,256,1024]{1,0,2:T(4,128)(2,1)S(1)}, u32[]{:S(2)}, u32[]{:S(2)}) %all-to-all-start.2) | async-done | bytes 1572896 | tf_op jit(solution)/shard_map/all_to_all | solution.py:263
  483.6 106.4 %while.23 = (s32[]{:T(128)}, bf16[3,1024,3,256]{1,3,2,0:T(8,128)(2,1)}, bf16[3,1024,3,256]{1,3,2,0:T(8,128)(2,1)}, s32[3,1024]{1,0:T(4,128)S(1)}, f32[3,4,1024]{...) while((s32[]{:T(128)}, bf16[3,1024,3,256]{1,3,2,0:T(8,128)(2,1)}, ...), condition=%wide.region_15.16_spmd, body=%wide.region_12.15_spmd.sunk | while | flops 2758013440 | bytes 152731792 | solution.py:264
  505.1 8.3 multiply_convert_fusion.7
  540.4 8.3 multiply_convert_fusion.7
  575.7 8.3 multiply_convert_fusion.7
  590.0 10.3 %copy.43 = bf16[3,1024,3,256]{3,2,0,1:T(4,128)(2,1)} copy(bf16[3,1024,3,256]{1,3,2,0:T(8,128)(2,1)} %get-tuple-element.68) | data formatting | bytes 9437184 | tf_op jit(solution)/shard_map/while | solution.py:264
  600.3 5.5 all-to-all-start.3
  605.9 14.5 %add_convert_fusion = bf16[768,1024]{1,0:T(8,128)(2,1)} fusion(f32[768,1024]{1,0:T(8,128)S(1)} %copy-done.8, bf16[4096,1024]{1,0:T(8,128)(2,1)} %all-gather.11.cloned.1.call-done, f32[768,4096]{1,0:T(8,128)} %fusion.74, f32[4096]{0:T(1024)S(1)} %copy-done.36, f32[1024]{0:T(1024)S(1)} %copy-done.39), kind=kOutput, calls=%fused_computation.120 | convolution fusion | flops 6476267520 | bytes 25710592 | tf_op jit(solution)/shard_map/dot_general | solution.py:43
  620.4 123.1 %all-to-all-done.3 = bf16[3,1024,3,256]{3,2,0,1:T(4,128)(2,1)} async-done(((bf16[3,1024,3,256]{3,2,0,1:T(4,128)(2,1)}), bf16[3,1024,3,256]{3,2,0,1:T(4,128)(2,1)}, u32[]{:S(2)}, u32[]{:S(2)}) %all-to-all-start.3) | async-done | bytes 4718624 | tf_op jit(solution)/shard_map/all_to_all | solution.py:265
  743.5 11.0 %copy.47 = bf16[3,4,256,3,256]{4,1,3,2,0:T(4,128)(2,1)} copy(bf16[3,4,256,3,256]{4,3,0,2,1:T(4,128)(2,1)} %bitcast.48) | data formatting | bytes 9437184 | tf_op jit(solution)/shard_map/all_to_all | solution.py:265
  754.5 9.5 %reshape.412 = bf16[768,3072]{1,0:T(8,128)(2,1)} reshape(bf16[3,256,3,4,256]{4,3,2,1,0:T(4,128)(2,1)} %bitcast.288) | data formatting | bytes 9437184 | tf_op jit(solution)/shard_map/reshape | solution.py:267
  776.9 8.7 fusion.119
  794.1 111.9 %all-reduce.3.cloned.1.call-done = (f32[1024,4]{0,1:T(4,128)}, f32[4,1024]{1,0:T(4,128)}, f32[1024,4]{0,1:T(4,128)}, f32[4,1024]{1,0:T(4,128)}) async-done(((f32[1024,4]{0,1:T(4,128)}, f32[4,1024]{1,0:T(4,128)}, f32[1024,4]{0,1:T(4,128)}, f32[4,1024]{1,0:T(4,128)}), (f32[1024,4]{0,1:T(4,128)}, f32[4,1024]{1,0:T(4,128)}, f32[1024,4]{0,1:T(4,128)}, f32[4,1024]{1,0:T(4,128)})) %all-reduce.3.cloned.1.call-update) | async-done | bytes 65552 | tf_op jit(solution)/shard_map/psum | solution.py:290
  (256 shorter events, 219.5 us)
Async XLA Ops:
  7.2 51.0 %all-gather.5.cloned.1.call-start = ((), (), s32[]{:S(2)}) async-start(), calls=%async_computation.4 | async-start | bytes 7077888 | tf_op jit(solution)/shard_map/all_gather | solution.py:198
  7.9 365.0 %all-gather.7.cloned.1.call-start = ((), (), s32[]{:S(2)}) async-start(), calls=%async_computation.5 | async-start | bytes 2359296 | tf_op jit(solution)/shard_map/all_gather | solution.py:231
  8.7 370.0 %all-gather.9.cloned.1.call-start = ((), (), s32[]{:S(2)}) async-start(), calls=%async_computation.6 | async-start | bytes 9437184 | tf_op jit(solution)/shard_map/all_gather | solution.py:240
  13.6 62.2 %copy-start.18 = (bf16[768,4]{0,1:T(4,128)(2,1)}, bf16[768,4]{0,1:T(4,128)(2,1)S(1)}, u32[]{:S(2)}) copy-start(bf16[768,4]{0,1:T(4,128)(2,1)S(1)} %fusion.89) | copy-start | bytes 18436
  14.1 71.8 %copy-start.20 = (bf16[768,4]{0,1:T(4,128)(2,1)}, bf16[768,4]{0,1:T(4,128)(2,1)S(1)}, u32[]{:S(2)}) copy-start(bf16[768,4]{0,1:T(4,128)(2,1)S(1)} %fusion.88) | copy-start | bytes 18436
  66.8 9.0 copy-start.27
  66.8 9.0 copy-start.32
  102.2 144.1 %all-to-all-start = ((bf16[3,256,3,1024]{1,0,2,3:T(4,128)(2,1)}), bf16[3,256,3,1024]{1,0,2,3:T(4,128)(2,1)}, u32[]{:S(2)}, u32[]{:S(2)}) async-start(bf16[3,256,3,1024]{1,0,2,3:T(4,128)(2,1)} %pad_maximum_fusion.1), calls=%async_computation | async-start | bytes 12582912 | tf_op jit(solution)/shard_map/all_to_all | solution.py:221
  107.4 285.2 %all-gather.11.cloned.1.call-start = ((), (), s32[]{:S(2)}) async-start(), calls=%async_computation.7 | async-start | bytes 9437184 | tf_op jit(solution)/shard_map/all_gather | solution.py:249
  255.6 8.7 copy-start.13
  378.7 13.9 %copy-start.7 = (f32[768,1024]{1,0:T(8,128)S(1)}, f32[768,1024]{1,0:T(8,128)}, u32[]{:S(2)}) copy-start(f32[768,1024]{1,0:T(8,128)} %copy-done.6) | copy-start | bytes 9437188
  378.7 13.9 %copy-start.35 = (f32[4096]{0:T(1024)S(1)}, f32[4096]{0:T(1024)}, u32[]{:S(2)}) copy-start(f32[4096]{0:T(1024)} %param.40) | copy-start | bytes 49156
  427.3 50.8 %all-to-all-start.2 = ((bf16[3,256,1024]{1,0,2:T(4,128)(2,1)}), bf16[3,256,1024]{1,0,2:T(4,128)(2,1)S(1)}, u32[]{:S(2)}, u32[]{:S(2)}) async-start(bf16[3,256,1024]{1,0,2:T(4,128)(2,1)} %copy.41), calls=%async_computation.2 | async-start | bytes 4194304 | tf_op jit(solution)/shard_map/all_to_all | solution.py:263
  600.3 143.1 %all-to-all-start.3 = ((bf16[3,1024,3,256]{3,2,0,1:T(4,128)(2,1)}), bf16[3,1024,3,256]{3,2,0,1:T(4,128)(2,1)}, u32[]{:S(2)}, u32[]{:S(2)}) async-start(bf16[3,1024,3,256]{3,2,0,1:T(4,128)(2,1)} %copy.43), calls=%async_computation.3 | async-start | bytes 12582912 | tf_op jit(solution)/shard_map/all_to_all | solution.py:265
  605.9 300.1 %all-reduce.3.cloned.1.call-start = ((), (), s32[]{:S(2)}) async-start(), calls=%async_computation.8 | async-start | bytes 131072 | tf_op jit(solution)/shard_map/psum | solution.py:290
  754.5 9.5 %copy-start.28 = (bf16[4,1024]{1,0:T(4,128)(2,1)S(1)}, bf16[4,1024]{1,0:T(4,128)(2,1)}, u32[]{:S(2)}) copy-start(bf16[4,1024]{1,0:T(4,128)(2,1)} %param.34) | copy-start | bytes 24580
  754.5 11.6 %copy-start.30 = (bf16[4,1024]{1,0:T(4,128)(2,1)S(1)}, bf16[4,1024]{1,0:T(4,128)(2,1)}, u32[]{:S(2)}) copy-start(bf16[4,1024]{1,0:T(4,128)(2,1)} %param.32) | copy-start | bytes 24580
  754.5 13.5 %copy-start.21 = (bf16[768,4]{0,1:T(4,128)(2,1)S(1)}, bf16[768,4]{0,1:T(4,128)(2,1)}, u32[]{:S(2)}) copy-start(bf16[768,4]{0,1:T(4,128)(2,1)} %copy-done.20) | copy-start | bytes 18436
  764.1 9.6 %copy-start.25 = (bf16[1024,4]{0,1:T(4,128)(2,1)S(1)}, bf16[1024,4]{0,1:T(4,128)(2,1)}, u32[]{:S(2)}) copy-start(bf16[1024,4]{0,1:T(4,128)(2,1)} %param.31) | copy-start | bytes 24580
  776.9 8.8 copy-start.3
  776.9 8.8 copy-start.10
  776.9 8.8 copy-start.15
  776.9 8.8 copy-start.17
  776.9 8.8 copy-start.23
  (24 other events, 100.4 us)
Sparse Core Ops, SparseCore 0:
  9.9 48.2 all-gather.4
  60.1 27.8 all-gather.6
  89.9 54.3 all-gather.8
  146.1 54.3 all-gather.10
  788.7 117.1 all-reduce.2
where the time goes:
time: 928 us; the launch traced here: 918 us
  waiting for transfers between devices  466 us (50%)
  matrix products  197 us (21%)
  local copies, waits for them, and re-layouts  103 us (11%)
  other arithmetic  70 us (8%)
  blocking collectives  51 us (5%)
  starting transfers between devices  14.8 us (2%)
  between operations  14.6 us (2%)
    all_to_all x1, waiting for transfers between devices, on_device(): lax.all_to_all(token_layout, 'seq', split_axis=3, concat_axis=1, tiled=True)  138 us
    all_to_all x1, waiting for transfers between devices, on_device(): lax.all_to_all(grad_projected, 'seq', split_axis=1, concat_axis=3, tiled=...  123 us
    psum x1, waiting for transfers between devices, on_device(): lax.psum((shard_query_reduce, local_query_up, shard_value_reduce, local_v...  112 us
    all_to_all x1, blocking collectives, on_device(): lax.all_to_all(for_sending(attended), 'seq', split_axis=1, concat_axis=2,...  51 us
    all_to_all x1, waiting for transfers between devices, on_device(): lax.all_to_all(grad_mixed, 'seq', split_axis=2, concat_axis=1, tiled=True)  47.2 us
    dot_general x7, matrix products, times_transposed(): lax.dot_general(left_side, right_side, (((1,), (1,)), ((), ())), preferre...  46.9 us
    all_gather x1, waiting for transfers between devices, on_device(): lax.all_gather(qkv_weight, 'dp', axis=0, tiled=True)  43.4 us
    dot_general x4, matrix products, fold_with(): jnp.dot(columns, weight_piece, preferred_element_type=jnp.float32)  39.2 us
  transfers between devices with their start and end apart: 8, of which 5 were waited for; matrix products, arithmetic and copies ran while one was open for 16% of the time, Pallas kernels for 0%

commit v1 on v0

v1 whole, which is shorter than its diff:
```python
from functools import partial

import jax
import jax.numpy as jnp
from jax import lax
from jax.experimental import pallas as pl
from jax.experimental.pallas import tpu as pltpu
from jax.sharding import PartitionSpec as P

HEAD = 64
QUAD = 256
PAIR = 128
NORM_EPSILON = 1e-05
ADAPTER_SCALE = 8.0
MASKED = -1e30
GELU_A = 0.7978845608028654
GELU_B = 0.044715

F32 = jnp.float32
BF16 = jnp.bfloat16
VMEM_BYTES = 56 * 1024 * 1024


def dot_nn(left, right):
    return lax.dot_general(left, right, (((1,), (0,)), ((), ())), preferred_element_type=F32)


def dot_nt(left, right):
    return lax.dot_general(left, right, (((1,), (1,)), ((), ())), preferred_element_type=F32)


def norm_parts(values):
    average = jnp.mean(values, axis=-1, keepdims=True)
    centered = values - average
    inverse = lax.rsqrt(jnp.mean(centered * centered, axis=-1, keepdims=True) + NORM_EPSILON)
    return centered * inverse, inverse


def norm_backward(gradient, normed, inverse, gain):
    scaled = gradient * gain
    return inverse * (
        scaled
        - jnp.mean(scaled, axis=-1, keepdims=True)
        - normed * jnp.mean(scaled * normed, axis=-1, keepdims=True)
    )


def head_lanes(rows, dtype):
    lane = lax.broadcasted_iota(jnp.int32, (rows, PAIR), 1)
    return lane < HEAD


def forward_kernel(chunks, place_ref, start_ref, *refs):
    hidden = refs[:chunks]
    wq, wk, wv, bias_q, bias_v, reduce_ref = refs[chunks : chunks + 6]
    q_out, k_out, v_out, mix_out, lse_out, down_out, mask_ref = refs[chunks + 6 :]
    tokens = hidden[0].shape[0]
    quad = pl.program_id(0)

    @pl.when(quad == 0)
    def _():
        place = place_ref[0]
        query = place * tokens + lax.broadcasted_iota(jnp.int32, (tokens, tokens), 0)
        start = start_ref[...]
        for s in range(chunks):
            key = (place - s) * tokens + lax.broadcasted_iota(jnp.int32, (tokens, tokens), 1)
            allowed = key >= start
            if s == 0:
                allowed = allowed & (key <= query)
            mask_ref[:, s * tokens : (s + 1) * tokens] = jnp.where(allowed, 0.0, MASKED)
            down = dot_nn(hidden[s][...], reduce_ref[...]) * ADAPTER_SCALE
            down_out[:, s * tokens : (s + 1) * tokens] = down.T[:8].astype(BF16)

    q_out[...] = ((dot_nn(hidden[0][...], wq[...]) + bias_q[...]).astype(BF16) * (HEAD**-0.5)).astype(BF16)
    for s in range(chunks):
        span = slice(s * tokens, (s + 1) * tokens)
        k_out[span, :] = dot_nn(hidden[s][...], wk[...]).astype(BF16)
        v_out[span, :] = (dot_nn(hidden[s][...], wv[...]) + bias_v[...]).astype(BF16)
    low = head_lanes(tokens, BF16)
    lane = lax.broadcasted_iota(jnp.int32, (tokens, PAIR), 1)
    totals = jnp.zeros((tokens, PAIR), F32)
    for pair in range(QUAD // PAIR):
        span = slice(pair * PAIR, (pair + 1) * PAIR)
        q_pair = q_out[:, span]
        mixed = []
        for half in range(2):
            own = low if half == 0 else jnp.logical_not(low)
            q_head = jnp.where(own, q_pair, jnp.zeros_like(q_pair))
            score = dot_nt(q_head, k_out[:, span]) + mask_ref[...]
            highest = jnp.max(score, axis=-1, keepdims=True)
            weight = jnp.exp(score - highest)
            total = jnp.sum(weight, axis=-1, keepdims=True)
            mixed.append(dot_nn(weight.astype(BF16), v_out[:, span]) * (1.0 / total))
            totals = jnp.where(lane == pair * 2 + half, highest + jnp.log(total), totals)
        mix_out[:, span] = jnp.where(low, mixed[0], mixed[1]).astype(BF16)
    lse_out[0] = totals.T[:8]


def feed_kernel(
    mix_ref, x_ref, gout_ref, wo_ref, out_bias, gain, shift, proj_bias, fc_ref, fc_bias, proj_ref,
    out_ref, gmid_ref, gmix_ref, middle_ref, hidden_ref, acc_ref, grad_ref,
):
    step = pl.program_id(0)

    @pl.when(step == 0)
    def _():
        middle = x_ref[...].astype(F32) + dot_nn(mix_ref[...], wo_ref[...]) + out_bias[...]
        middle_ref[...] = middle
        normed, _ = norm_parts(middle)
        hidden_ref[...] = (normed * gain[...] + shift[...]).astype(BF16)

    before = dot_nn(hidden_ref[...], fc_ref[...]) + fc_bias[...]
    square = before * before
    bend = jnp.tanh(GELU_A * before * (1.0 + GELU_B * square))
    half = 0.5 * (1.0 + bend)
    slope = half + 0.5 * before * (1.0 - bend * bend) * (GELU_A * (1.0 + 3.0 * GELU_B * square))
    act = (before * half).astype(BF16)
    g_before = (dot_nt(gout_ref[...], proj_ref[...]) * slope).astype(BF16)
    fed = dot_nn(act, proj_ref[...])
    back = dot_nt(g_before, fc_ref[...])

    @pl.when(step == 0)
    def _():
        acc_ref[...] = fed
        grad_ref[...] = back

    @pl.when(step > 0)
    def _():
        acc_ref[...] += fed
        grad_ref[...] += back

    @pl.when(step == pl.num_programs(0) - 1)
    def _():
        middle = middle_ref[...]
        out_ref[...] = (middle + acc_ref[...] + proj_bias[...]).astype(BF16)
        normed, inverse = norm_parts(middle)
        g_middle = gout_ref[...].astype(F32) + norm_backward(grad_ref[...], normed, inverse, gain[...])
        gmid_ref[...] = g_middle
        gmix_ref[...] = dot_nt(g_middle.astype(BF16), wo_ref[...]).astype(BF16)


def backward_kernel(chunks, place_ref, start_ref, *refs):
    hidden = refs[:chunks]
    q_ref, k_ref, v_ref, mix_ref, g_ref, lse_ref, down_ref, up_ref, w_ref = refs[chunks : chunks + 9]
    grads = refs[chunks + 9 : 2 * chunks + 9]
    reduce_out, up_out, mask_ref, dq_ref, dkv_ref, w_held, w_sem = refs[2 * chunks + 9 :]
    tokens = hidden[0].shape[0]
    width = hidden[0].shape[1]
    quad = pl.program_id(0)

    @pl.when(quad == 0)
    def _():
        pltpu.make_async_copy(w_ref, w_held, w_sem).start()
        place = place_ref[0]
        query = place * tokens + lax.broadcasted_iota(jnp.int32, (tokens, tokens), 1)
        start = start_ref[...]
        for s in range(chunks):
            key = (place - s) * tokens + lax.broadcasted_iota(jnp.int32, (tokens, tokens), 0)
            allowed = key >= start
            if s == 0:
                allowed = allowed & (key <= query)
            mask_ref[s * tokens : (s + 1) * tokens, :] = jnp.where(allowed, 0.0, MASKED)

    low = head_lanes(tokens, BF16)
    for pair in range(QUAD // PAIR):
        span = slice(pair * PAIR, (pair + 1) * PAIR)
        q_pair = q_ref[:, span]
        g_pair = g_ref[:, span]
        product = (g_pair.astype(F32) * mix_ref[:, span].astype(F32)).T
        heads = []
        for half in range(2):
            own = low if half == 0 else jnp.logical_not(low)
            inner = jnp.sum(product[half * HEAD : (half + 1) * HEAD], axis=0, keepdims=True)
            row = pair * 2 + half
            heads.append(
                (
                    jnp.where(own, q_pair, jnp.zeros_like(q_pair)),
                    jnp.where(own, g_pair, jnp.zeros_like(g_pair)),
                    inner,
                    lse_ref[0, row : row + 1, :],
                )
            )
        dq_parts = [jnp.zeros((HEAD, tokens), F32)] * 2
        for s in range(chunks):
            rows = slice(s * tokens, (s + 1) * tokens)
            k_pair = k_ref[rows, span]
            v_pair = v_ref[rows, span]
            k_turned = k_pair.astype(F32).T.astype(BF16)
            dk = None
            for half, (q_head, g_head, inner, lse) in enumerate(heads):
                score = dot_nt(k_pair, q_head) + mask_ref[rows, :]
                prob = jnp.exp(score - lse)
                g_score = (prob * (dot_nt(v_pair, g_head) - inner)).astype(BF16)
                part_v = dot_nn(prob.astype(BF16), g_head)
                part_k = dot_nn(g_score, q_head)
                dk = part_k if dk is None else dk + part_k
                dv = part_v if half == 0 else dv + part_v
                dq_parts[half] = dq_parts[half] + dot_nn(k_turned[half * HEAD : (half + 1) * HEAD], g_score)
            columns = pl.ds(pl.multiple_of(quad * QUAD, QUAD) + pair * PAIR, PAIR)
            dkv_ref[rows, columns] = dk.astype(BF16)
            columns = pl.ds(pl.multiple_of(quad * QUAD, QUAD) + (width + pair * PAIR), PAIR)
            dkv_ref[rows, columns] = dv.astype(BF16)
        dq = jnp.concatenate(dq_parts, axis=0).T * (HEAD**-0.5)
        dq_ref[:, pl.ds(pl.multiple_of(quad * QUAD, QUAD) + pair * PAIR, PAIR)] = dq.astype(BF16)

    @pl.when(quad == pl.num_programs(0) - 1)
    def _():
        pltpu.make_async_copy(w_ref, w_held, w_sem).wait()
        rank_row = lax.broadcasted_iota(jnp.int32, (8, width), 0) < 4
        up_grad = jnp.zeros((8, width), F32)
        reduce_grad = jnp.zeros((8, width), F32)
        for s in range(chunks - 1, -1, -1):
            rows = slice(s * tokens, (s + 1) * tokens)
            dkv = dkv_ref[rows, :]
            grad = dot_nt(dkv, w_held[:, width:])
            if s == 0:
                grad = grad + dot_nt(dq_ref[...], w_held[:, :width])
            grads[s][...] = grad.astype(grads[s].dtype)
            dv = dkv_ref[rows, width:]
            down = down_ref[:, rows]
            up_grad = up_grad + dot_nn(down, dv)
            g_down = dot_nt(dv, up_ref[...]).T[:8].astype(BF16)
            reduce_grad = reduce_grad + dot_nn(g_down, hidden[s][...])
        dq = dq_ref[...]
        g_down = dot_nt(dq, up_ref[...]).T[:8].astype(BF16)
        up_out[...] = jnp.where(rank_row, dot_nn(down_ref[:, :tokens], dq), up_grad)
        reduce_out[...] = jnp.where(rank_row, dot_nn(g_down, hidden[0][...]), reduce_grad)


def whole(shape):
    return pl.BlockSpec(shape, lambda i: (0,) * len(shape))


def run_forward(place, start, hidden, weight, query_bias, value_bias, reduce_wide):
    chunks = len(hidden)
    tokens, width = hidden[0].shape
    length = chunks * tokens
    quads = width // QUAD
    flops = 2 * width * width * (tokens + 2 * length) + 4 * tokens * length * width
    return pl.pallas_call(
        partial(forward_kernel, chunks),
        grid=(quads,),
        in_specs=[pl.BlockSpec(memory_space=pltpu.SMEM), whole((tokens, 1))]
        + [whole((tokens, width))] * chunks
        + [
            pl.BlockSpec((width, QUAD), lambda i: (0, i)),
            pl.BlockSpec((width, QUAD), lambda i: (0, i + quads)),
            pl.BlockSpec((width, QUAD), lambda i: (0, i + 2 * quads)),
            pl.BlockSpec((1, QUAD), lambda i: (0, i)),
            pl.BlockSpec((1, QUAD), lambda i: (0, i)),
            whole((width, PAIR)),
        ],
        out_specs=[
            pl.BlockSpec((tokens, QUAD), lambda i: (0, i)),
            pl.BlockSpec((length, QUAD), lambda i: (0, i)),
            pl.BlockSpec((length, QUAD), lambda i: (0, i)),
            pl.BlockSpec((tokens, QUAD), lambda i: (0, i)),
            pl.BlockSpec((1, 8, tokens), lambda i: (i, 0, 0)),
            whole((8, length)),
        ],
        out_shape=[
            jax.ShapeDtypeStruct((tokens, width), BF16),
            jax.ShapeDtypeStruct((length, width), BF16),
            jax.ShapeDtypeStruct((length, width), BF16),
            jax.ShapeDtypeStruct((tokens, width), BF16),
            jax.ShapeDtypeStruct((quads, 8, tokens), F32),
            jax.ShapeDtypeStruct((8, length), BF16),
        ],
        scratch_shapes=[pltpu.VMEM((tokens, length), F32)],
        compiler_params=pltpu.CompilerParams(vmem_limit_bytes=VMEM_BYTES),
        cost_estimate=pl.CostEstimate(
            flops=flops, bytes_accessed=8 * width * width + 10 * length * width,
            transcendentals=tokens * length * width // HEAD,
        ),
        name="attend_forward",
    )(place, start, *hidden, weight, weight, weight, query_bias, value_bias, reduce_wide)


def run_feed(mixed, x, grad_out, out_weight, vectors, fc_weight, fc_bias, proj_weight):
    tokens, width = x.shape
    hidden_units = fc_weight.shape[1]
    block = 1024
    out_bias, gain, shift, proj_bias = vectors
    return pl.pallas_call(
        feed_kernel,
        grid=(hidden_units // block,),
        in_specs=[whole((tokens, width))] * 3
        + [whole((width, width))]
        + [whole((1, width))] * 4
        + [
            pl.BlockSpec((width, block), lambda i: (0, i)),
            pl.BlockSpec((1, block), lambda i: (0, i)),
            pl.BlockSpec((block, width), lambda i: (i, 0)),
        ],
        out_specs=[whole((tokens, width))] * 3,
        out_shape=[
            jax.ShapeDtypeStruct((tokens, width), BF16),
            jax.ShapeDtypeStruct((tokens, width), F32),
            jax.ShapeDtypeStruct((tokens, width), BF16),
        ],
        scratch_shapes=[
            pltpu.VMEM((tokens, width), F32),
            pltpu.VMEM((tokens, width), BF16),
            pltpu.VMEM((tokens, width), F32),
            pltpu.VMEM((tokens, width), F32),
        ],
        compiler_params=pltpu.CompilerParams(vmem_limit_bytes=VMEM_BYTES),
        cost_estimate=pl.CostEstimate(
            flops=2 * tokens * width * (4 * hidden_units + 2 * width),
            bytes_accessed=2 * width * (2 * hidden_units + width) + 16 * tokens * width,
            transcendentals=tokens * hidden_units,
        ),
        name="feed",
    )(mixed, x, grad_out, out_weight, out_bias, gain, shift, proj_bias, fc_weight, fc_bias, proj_weight)


def run_backward(place, start, hidden, q, k, v, mixed, g_mixed, lse, down, up_wide, weight):
    chunks = len(hidden)
    tokens, width = hidden[0].shape
    length = chunks * tokens
    quads = width // QUAD
    flops = 2 * width * width * (tokens + 2 * length) + 10 * tokens * length * width
    own = pl.BlockSpec((tokens, QUAD), lambda i: (0, i))
    every = pl.BlockSpec((length, QUAD), lambda i: (0, i))
    return pl.pallas_call(
        partial(backward_kernel, chunks),
        grid=(quads,),
        in_specs=[pl.BlockSpec(memory_space=pltpu.SMEM), whole((1, tokens))]
        + [whole((tokens, width))] * chunks
        + [
            own, every, every, own, own,
            pl.BlockSpec((1, 8, tokens), lambda i: (i, 0, 0)),
            whole((8, length)),
            whole((PAIR, width)),
            pl.BlockSpec(memory_space=pl.ANY),
        ],
        out_specs=[whole((tokens, width))] * chunks + [whole((8, width))] * 2,
        out_shape=[jax.ShapeDtypeStruct((tokens, width), F32 if s == 0 else BF16) for s in range(chunks)]
        + [jax.ShapeDtypeStruct((8, width), F32)] * 2,
        scratch_shapes=[
            pltpu.VMEM((length, tokens), F32),
            pltpu.VMEM((tokens, width), BF16),
            pltpu.VMEM((length, 2 * width), BF16),
            pltpu.VMEM((width, 3 * width), BF16),
            pltpu.SemaphoreType.DMA,
        ],
        compiler_params=pltpu.CompilerParams(vmem_limit_bytes=VMEM_BYTES),
        cost_estimate=pl.CostEstimate(
            flops=flops, bytes_accessed=6 * width * width + 14 * length * width,
            transcendentals=tokens * length * width // HEAD,
        ),
        name="attend_backward",
    )(place, start, *hidden, q, k, v, mixed, g_mixed, lse, down, up_wide, weight)


def on_device(
    seq,
    block_input,
    seg_start,
    ln1_gain,
    ln1_bias,
    qkv_weight,
    query_bias,
    value_bias,
    query_adapter_reduce,
    query_up,
    value_adapter_reduce,
    value_up,
    out_weight,
    out_bias,
    ln2_gain,
    ln2_bias,
    fc_weight,
    fc_bias,
    proj_weight,
    proj_bias,
    grad_out,
):
    rows, tokens, width = block_input.shape
    rank = query_up.shape[0]
    shard = qkv_weight.shape[0]
    place = lax.axis_index("seq")
    upward = [(i, i + 1) for i in range(seq - 1)]
    downward = [(i + 1, i) for i in range(seq - 1)]

    def own_rows(reduce):
        return lax.dynamic_slice(reduce, (lax.axis_index("dp") * shard, 0), (shard, rank))

    def folded(part, reduce, up):
        change = jnp.dot(own_rows(reduce), up, preferred_element_type=F32) * ADAPTER_SCALE
        return (part.astype(F32) + change).astype(BF16)

    weight_shard = jnp.concatenate(
        [
            folded(qkv_weight[:, :width], query_adapter_reduce, query_up),
            qkv_weight[:, width : 2 * width],
            folded(qkv_weight[:, 2 * width :], value_adapter_reduce, value_up),
        ],
        axis=1,
    )
    weight = lax.all_gather(weight_shard, "dp", axis=0, tiled=True)
    whole_out = lax.all_gather(out_weight, "dp", axis=0, tiled=True)
    whole_fc = lax.all_gather(fc_weight, "dp", axis=0, tiled=True)
    whole_proj = lax.all_gather(proj_weight, "dp", axis=0, tiled=True)

    pad = jnp.zeros((width, PAIR - 2 * rank), BF16)
    reduce_wide = jnp.concatenate([query_adapter_reduce, value_adapter_reduce, pad], axis=1)
    up_wide = jnp.concatenate([query_up, value_up, pad.T], axis=0)
    starts = lax.dynamic_slice(seg_start, (0, place * tokens), (rows, tokens))
    place_ref = place.astype(jnp.int32).reshape(1)

    def as_row(vector):
        return vector.reshape(1, -1)

    vectors = tuple(as_row(a) for a in (out_bias, ln2_gain, ln2_bias, proj_bias))

    hidden_rows = []
    for r in range(rows):
        normed, _ = norm_parts(block_input[r].astype(F32))
        first = (normed * ln1_gain + ln1_bias).astype(BF16)
        hidden = [first]
        for _ in range(seq - 1):
            hidden.append(lax.ppermute(hidden[-1], "seq", upward))
        hidden_rows.append(hidden)

    outs, grads, reduce_sum, up_sum = [], [], 0.0, 0.0
    for r in range(rows):
        hidden = hidden_rows[r]
        q, k, v, mixed, lse, down = run_forward(
            place_ref, starts[r].reshape(tokens, 1), hidden, weight, as_row(query_bias), as_row(value_bias), reduce_wide
        )
        out, g_middle, g_mixed = run_feed(
            mixed, block_input[r], grad_out[r], whole_out, vectors, whole_fc, as_row(fc_bias), whole_proj
        )
        outs.append(out)
        result = run_backward(
            place_ref, starts[r].reshape(1, tokens), hidden, q, k, v, mixed, g_mixed, lse, down, up_wide, weight
        )
        reduce_sum = reduce_sum + result[seq]
        up_sum = up_sum + result[seq + 1]
        moving = result[seq - 1]
        for s in range(seq - 2, -1, -1):
            arrived = lax.ppermute(moving, "seq", downward)
            total = result[s].astype(F32) + arrived.astype(F32)
            moving = total.astype(BF16)
        normed, inverse = norm_parts(block_input[r].astype(F32))
        grads.append(g_middle + norm_backward(total, normed, inverse, ln1_gain))

    summed = lax.psum(jnp.concatenate([reduce_sum * ADAPTER_SCALE, up_sum], axis=0), ("dp", "seq"))
    return (
        jnp.stack(outs),
        jnp.stack(grads),
        summed[:rank].T,
        summed[8 : 8 + rank],
        summed[rank : 2 * rank].T,
        summed[8 + rank : 8 + 2 * rank],
    )


def solution(mesh):
    return jax.shard_map(
        partial(on_device, mesh.shape["seq"]),
        mesh=mesh,
        in_specs=(
            P("dp", "seq", None),
            P("dp", None),
            P(),
            P(),
            P("dp", None),
            P(),
            P(),
            P(),
            P(),
            P(),
            P(),
            P("dp", None),
            P(),
            P(),
            P(),
            P("dp", None),
            P(),
            P("dp", None),
            P(),
            P("dp", "seq", None),
        ),
        out_specs=(P("dp", "seq", None), P("dp", "seq", None), P(), P(), P(), P()),
        check_vma=False,
    )
```

time: 928 us -> 541 us (0.58)
  waiting for transfers between devices: 466 us -> 241 us
  matrix products: 197 us -> 2.56 us
  Pallas kernels: 0 us -> 190 us
  local copies, waits for them, and re-layouts: 103 us -> 10.5 us
  blocking collectives: 51 us -> 0 us
  other arithmetic: 70 us -> 22.6 us
  starting transfers between devices: 14.8 us -> 54.7 us
    all_to_all x3 -> x0, waiting for transfers between devices: 309 us -> none  [the longest x1 138 us: on_device(): lax.all_to_all(token_layout, 'seq', split_axis=3, concat_axis=1, tiled=True)]
    dot_general x61 -> x2, matrix products: 197 us -> 2.56 us  [folded(): jnp.dot(own_rows(reduce), up, preferred_element_type=F32) * ADAPTER_SCALE]
    pallas_call x0 -> x9, Pallas kernels: none -> 190 us  [the longest x3 83 us: run_backward(): pl.pallas_call(partial(backward_kernel, chunks), grid=(quads,), in_specs=...]
    ppermute x0 -> x18, waiting for transfers between devices: none -> 77.9 us  [the longest x9 40.6 us: on_device(): arrived = lax.ppermute(moving, 'seq', downward)]
    ppermute x0 -> x18, starting transfers between devices: none -> 54.6 us  [the longest x9 42.6 us: on_device(): hidden.append(lax.ppermute(hidden[-1], 'seq', upward))]
    all_to_all x1 -> x0, blocking collectives: 51 us -> none  [on_device(): lax.all_to_all(for_sending(attended), 'seq', split_axis=1, concat_axis=2,...]
    all_to_all x6 -> x0, local copies, waits for them, and re-layouts: 36.1 us -> none  [the longest x2 18.1 us: on_device(): lax.all_to_all(token_layout, 'seq', split_axis=3, concat_axis=1, tiled=True)]
    convert_element_type x5 -> x7, other arithmetic: 26.2 us -> 5.14 us  [the longest x6 3.55 us: on_device(): moving = total.astype(BF16)]
  transfers between devices with their start and end apart: 8 -> 23, of which waited for: 5 -> 14; matrix products, arithmetic and copies ran while one was open for 16% -> 4% of each run, Pallas kernels for 0% -> 27%
where the time goes in v1:
time: 541 us; the launch traced here: 536 us
  waiting for transfers between devices  241 us (45%)
  Pallas kernels  190 us (35%)
  starting transfers between devices  54.7 us (10%)
  other arithmetic  22.6 us (4%)
  between operations  14.8 us (3%)
  local copies, waits for them, and re-layouts  10.5 us (2%)
    psum x1, waiting for transfers between devices, on_device(): lax.psum(jnp.concatenate([reduce_sum * ADAPTER_SCALE, up_sum], axis=0), (...  118 us
    pallas_call x3, Pallas kernels, run_backward(): pl.pallas_call(partial(backward_kernel, chunks), grid=(quads,), in_specs=...  83 us
    pallas_call x3, Pallas kernels, run_feed(): pl.pallas_call(feed_kernel, grid=(hidden_units // block,), in_specs=[whol...  54.4 us
    pallas_call x3, Pallas kernels, run_forward(): pl.pallas_call(partial(forward_kernel, chunks), grid=(quads,), in_specs=[...  52.3 us
    ppermute x9, starting transfers between devices, on_device(): hidden.append(lax.ppermute(hidden[-1], 'seq', upward))  42.6 us
    all_gather x1, waiting for transfers between devices, on_device(): whole_proj = lax.all_gather(proj_weight, 'dp', axis=0, tiled=True)  42.4 us
    ppermute x9, waiting for transfers between devices, on_device(): arrived = lax.ppermute(moving, 'seq', downward)  40.6 us
    ppermute x9, waiting for transfers between devices, on_device(): hidden.append(lax.ppermute(hidden[-1], 'seq', upward))  37.2 us
  transfers between devices with their start and end apart: 23, of which 14 were waited for; matrix products, arithmetic and copies ran while one was open for 4% of the time, Pallas kernels for 27%

profile of v1, /device:TPU:0, one launch (start us, length us, event | category | flops | bytes accessed | tf_op | source)
XLA Modules:
  0.0 535.6 jit_solution(16820085578519462451)
XLA Ops:
  16.4 5.7 %collective-permute-start.6 = (bf16[256,1024]{1,0:T(8,128)(2,1)S(1)}, bf16[256,1024]{1,0:T(8,128)(2,1)}, u32[]{:S(2)}, u32[]{:S(2)}) collective-permute-start(bf16[256,1024]{1,0:T(8,128)(2,1)S(1)} %get-tuple-element.109.refs_0_), channel_id=1, source_target_pairs={{0,1},{1,2},{2,3},{4,5},{5,6},{6,7},{8,9},{9,10},{10,11},{12,13},{... | collective-permute-start | bytes 1572872 | tf_op jit(solution)/shard_map/ppermute | solution.py:423
  33.7 5.3 collective-permute-start.7
  45.0 5.2 collective-permute-start.1
  50.2 6.1 %collective-permute-done.3.refs_1_ = bf16[256,1024]{1,0:T(8,128)(2,1)} collective-permute-done((bf16[256,1024]{1,0:T(8,128)(2,1)}, bf16[256,1024]{1,0:T(8,128)(2,1)}, u32[]{:S(2)}, u32[]{:S(2)}) %collective-permute-start.3) | collective-permute-done | bytes 524320 | tf_op jit(solution)/shard_map/ppermute | solution.py:423
  56.2 5.2 collective-permute-start.4
  61.4 6.1 %collective-permute-done.7.refs_2_ = bf16[256,1024]{1,0:T(8,128)(2,1)} collective-permute-done((bf16[256,1024]{1,0:T(8,128)(2,1)}, bf16[256,1024]{1,0:T(8,128)(2,1)}, u32[]{:S(2)}, u32[]{:S(2)}) %collective-permute-start.7) | collective-permute-done | bytes 524320 | tf_op jit(solution)/shard_map/ppermute | solution.py:423
  67.5 5.2 collective-permute-start.8
  83.1 6.8 %collective-permute-done.4.refs_2_ = bf16[256,1024]{1,0:T(8,128)(2,1)} collective-permute-done((bf16[256,1024]{1,0:T(8,128)(2,1)}, bf16[256,1024]{1,0:T(8,128)(2,1)}, u32[]{:S(2)}, u32[]{:S(2)}) %collective-permute-start.4) | collective-permute-done | bytes 524320 | tf_op jit(solution)/shard_map/ppermute | solution.py:423
  94.6 6.6 %collective-permute-done.8.refs_3_ = bf16[256,1024]{1,0:T(8,128)(2,1)} collective-permute-done((bf16[256,1024]{1,0:T(8,128)(2,1)}, bf16[256,1024]{1,0:T(8,128)(2,1)}, u32[]{:S(2)}, u32[]{:S(2)}) %collective-permute-start.8) | collective-permute-done | bytes 524320 | tf_op jit(solution)/shard_map/ppermute | solution.py:423
  101.2 17.4 %attend_forward.5 = (bf16[256,1024]{1,0:T(8,128)(2,1)}, bf16[1024,1024]{1,0:T(8,128)(2,1)}, bf16[1024,1024]{1,0:T(8,128)(2,1)}, bf16[256,1024]{1,0:T(8,128)(2,1)...) custom-call(s32[1]{0:T(128)} %bitcast.place_ref, s32[256,1]{1,0:T(8,128)} %copy.32.start_ref, ...), custom_call_target="tpu_custom_call" | custom-call | flops 5905580032 | bytes 18874368 | tf_op jit(solution)/shard_map/attend_forward/pallas_call | solution.py:240
  123.3 17.5 %attend_forward.4 = (bf16[256,1024]{1,0:T(8,128)(2,1)}, bf16[1024,1024]{1,0:T(8,128)(2,1)}, bf16[1024,1024]{1,0:T(8,128)(2,1)}, bf16[256,1024]{1,0:T(8,128)(2,1)...) custom-call(s32[1]{0:T(128)} %bitcast.place_ref, s32[256,1]{1,0:T(8,128)} %copy.31.start_ref, ...), custom_call_target="tpu_custom_call" | custom-call | flops 5905580032 | bytes 18874368 | tf_op jit(solution)/shard_map/attend_forward/pallas_call | solution.py:240
  141.6 17.4 %attend_forward.3 = (bf16[256,1024]{1,0:T(8,128)(2,1)}, bf16[1024,1024]{1,0:T(8,128)(2,1)}, bf16[1024,1024]{1,0:T(8,128)(2,1)}, bf16[256,1024]{1,0:T(8,128)(2,1)...) custom-call(s32[1]{0:T(128)} %bitcast.place_ref, s32[256,1]{1,0:T(8,128)} %copy.30.start_ref, ...), custom_call_target="tpu_custom_call" | custom-call | flops 5905580032 | bytes 18874368 | tf_op jit(solution)/shard_map/attend_forward/pallas_call | solution.py:240
  159.1 42.4 %all-gather.11.cloned.1.call-done.proj_ref = bf16[4096,1024]{1,0:T(8,128)(2,1)} async-done(((bf16[512,1024]{1,0:T(8,128)(2,1)}), bf16[4096,1024]{1,0:T(8,128)(2,1)}) %all-gather.11.cloned.1.call-update) | async-done | bytes 8388624 | tf_op jit(solution)/shard_map/all_gather | solution.py:404
  201.5 18.3 %feed.5 = (bf16[256,1024]{1,0:T(8,128)(2,1)}, f32[256,1024]{1,0:T(8,128)}, bf16[256,1024]{1,0:T(8,128)(2,1)}) custom-call(bf16[256,1024]{1,0:T(8,128)(2,1)} %get-tuple-element.55.mix_ref.refs_7_, bf16[256,1024]{1,0:T(8,128)(2,1)} %get-tuple-element.128.x_ref, bf16[256,1024]{1,0:T(8,128)(2,1)} %get-tuple-element.113.gout_ref, ...), custom_call_target="tpu_custom_call" | custom-call | flops 9663676416 | bytes 23068672 | tf_op jit(solution)/shard_map/feed/pallas_call | solution.py:284
  219.8 27.6 %attend_backward.5 = (f32[256,1024]{1,0:T(8,128)}, bf16[256,1024]{1,0:T(8,128)(2,1)}, bf16[256,1024]{1,0:T(8,128)(2,1)}, bf16[256,1024]{1,0:T(8,128)(2,1)}, f32[8,1024]{1,0:T(8,128)}, /*index=5*/f32[8,1024]{1,0:T(8,128)}) custom-call(s32[1]{0:T(128)} %bitcast.place_ref, s32[1,256]{1,0:T(1,128)} %copy-done.28, bf16[256,1024]{1,0:T(8,128)(2,1)} %copy-done.14, ...), custom_call_target="tpu_custom_call" | custom-call | flops 7516192768 | bytes 20971520 | tf_op jit(solution)/shard_map/attend_backward/pallas_call | solution.py:325
  248.7 18.0 %feed.4 = (bf16[256,1024]{1,0:T(8,128)(2,1)}, f32[256,1024]{1,0:T(8,128)}, bf16[256,1024]{1,0:T(8,128)(2,1)}) custom-call(bf16[256,1024]{1,0:T(8,128)(2,1)} %get-tuple-element.53.mix_ref.refs_7_, bf16[256,1024]{1,0:T(8,128)(2,1)} %get-tuple-element.127.x_ref, bf16[256,1024]{1,0:T(8,128)(2,1)} %get-tuple-element.114.gout_ref, ...), custom_call_target="tpu_custom_call" | custom-call | flops 9663676416 | bytes 23068672 | tf_op jit(solution)/shard_map/feed/pallas_call | solution.py:284
  266.7 27.7 %attend_backward.4 = (f32[256,1024]{1,0:T(8,128)}, bf16[256,1024]{1,0:T(8,128)(2,1)}, bf16[256,1024]{1,0:T(8,128)(2,1)}, bf16[256,1024]{1,0:T(8,128)(2,1)}, f32[8,1024]{1,0:T(8,128)}, /*index=5*/f32[8,1024]{1,0:T(8,128)}) custom-call(s32[1]{0:T(128)} %bitcast.place_ref, s32[1,256]{1,0:T(1,128)} %copy-done.27, bf16[256,1024]{1,0:T(8,128)(2,1)} %get-tuple-element.108.refs_0_, ...), custom_call_target="tpu_custom_call" | custom-call | flops 7516192768 | bytes 20971520 | tf_op jit(solution)/shard_map/attend_backward/pallas_call | solution.py:325
  295.7 18.1 %feed.3 = (bf16[256,1024]{1,0:T(8,128)(2,1)}, f32[256,1024]{1,0:T(8,128)}, bf16[256,1024]{1,0:T(8,128)(2,1)}) custom-call(bf16[256,1024]{1,0:T(8,128)(2,1)} %get-tuple-element.51.mix_ref.refs_7_, bf16[256,1024]{1,0:T(8,128)(2,1)} %get-tuple-element.129.x_ref, bf16[256,1024]{1,0:T(8,128)(2,1)} %get-tuple-element.112.gout_ref, ...), custom_call_target="tpu_custom_call" | custom-call | flops 9663676416 | bytes 23068672 | tf_op jit(solution)/shard_map/feed/pallas_call | solution.py:284
  313.8 27.7 %attend_backward.3 = (f32[256,1024]{1,0:T(8,128)}, bf16[256,1024]{1,0:T(8,128)(2,1)}, bf16[256,1024]{1,0:T(8,128)(2,1)}, bf16[256,1024]{1,0:T(8,128)(2,1)}, f32[8,1024]{1,0:T(8,128)}, /*index=5*/f32[8,1024]{1,0:T(8,128)}) custom-call(s32[1]{0:T(128)} %bitcast.place_ref, s32[1,256]{1,0:T(1,128)} %copy-done.26, bf16[256,1024]{1,0:T(8,128)(2,1)} %get-tuple-element.107.refs_0_, ...), custom_call_target="tpu_custom_call" | custom-call | flops 7516192768 | bytes 20971520 | tf_op jit(solution)/shard_map/attend_backward/pallas_call | solution.py:325
  346.8 13.0 %collective-permute-done.9 = bf16[256,1024]{1,0:T(8,128)(2,1)S(1)} collective-permute-done((bf16[256,1024]{1,0:T(8,128)(2,1)}, bf16[256,1024]{1,0:T(8,128)(2,1)S(1)}, u32[]{:S(2)}, u32[]{:S(2)}) %collective-permute-start.9) | collective-permute-done | bytes 524320 | tf_op jit(solution)/shard_map/ppermute | solution.py:443
  361.3 9.7 %collective-permute-done.16 = bf16[256,1024]{1,0:T(8,128)(2,1)S(1)} collective-permute-done((bf16[256,1024]{1,0:T(8,128)(2,1)S(1)}, bf16[256,1024]{1,0:T(8,128)(2,1)S(1)}, u32[]{:S(2)}, u32[]{:S(2)}) %collective-permute-start.16) | collective-permute-done | bytes 524320 | tf_op jit(solution)/shard_map/ppermute | solution.py:443
  373.3 9.0 %collective-permute-done.13 = bf16[256,1024]{1,0:T(8,128)(2,1)S(1)} collective-permute-done((bf16[256,1024]{1,0:T(8,128)(2,1)S(1)}, bf16[256,1024]{1,0:T(8,128)(2,1)S(1)}, u32[]{:S(2)}, u32[]{:S(2)}) %collective-permute-start.13) | collective-permute-done | bytes 524320 | tf_op jit(solution)/shard_map/ppermute | solution.py:443
  384.5 9.0 %collective-permute-done.10 = bf16[256,1024]{1,0:T(8,128)(2,1)S(1)} collective-permute-done((bf16[256,1024]{1,0:T(8,128)(2,1)S(1)}, bf16[256,1024]{1,0:T(8,128)(2,1)S(1)}, u32[]{:S(2)}, u32[]{:S(2)}) %collective-permute-start.10) | collective-permute-done | bytes 524320 | tf_op jit(solution)/shard_map/ppermute | solution.py:443
  399.5 118.4 %all-reduce.2.cloned.1.call-done = f32[16,1024]{1,0:T(8,128)} async-done(((f32[16,1024]{1,0:T(8,128)}), f32[16,1024]{1,0:T(8,128)}) %all-reduce.2.cloned.1.call-update) | async-done | bytes 65552 | tf_op jit(solution)/shard_map/psum | solution.py:449
  (144 shorter events, 77.5 us)
Async XLA Ops:
  7.2 94.0 %all-gather.5.cloned.1.call-start = ((), (), s32[]{:S(2)}) async-start(), calls=%async_computation | async-start | bytes 7077888 | tf_op jit(solution)/shard_map/all_gather | solution.py:401
  10.8 148.3 %all-gather.7.cloned.1.call-start = ((), (), s32[]{:S(2)}) async-start(), calls=%async_computation.1 | async-start | bytes 2359296 | tf_op jit(solution)/shard_map/all_gather | solution.py:402
  11.5 147.6 %all-gather.9.cloned.1.call-start = ((), (), s32[]{:S(2)}) async-start(), calls=%async_computation.2 | async-start | bytes 9437184 | tf_op jit(solution)/shard_map/all_gather | solution.py:403
  12.3 189.2 %all-gather.11.cloned.1.call-start = ((), (), s32[]{:S(2)}) async-start(), calls=%async_computation.3 | async-start | bytes 9437184 | tf_op jit(solution)/shard_map/all_gather | solution.py:404
  12.9 505.1 %all-reduce.2.cloned.1.call-start = ((), (), s32[]{:S(2)}) async-start(), calls=%async_computation.4 | async-start | bytes 131072 | tf_op jit(solution)/shard_map/psum | solution.py:449
  16.4 17.2 %collective-permute-start.6 = (bf16[256,1024]{1,0:T(8,128)(2,1)S(1)}, bf16[256,1024]{1,0:T(8,128)(2,1)}, u32[]{:S(2)}, u32[]{:S(2)}) collective-permute-start(bf16[256,1024]{1,0:T(8,128)(2,1)S(1)} %get-tuple-element.109.refs_0_), channel_id=1, source_target_pairs={{0,1},{1,2},{2,3},{4,5},{5,6},{6,7},{8,9},{9,10},{10,11},{12,13},{... | collective-permute-start | bytes 1572872 | tf_op jit(solution)/shard_map/ppermute | solution.py:423
  22.2 22.8 %collective-permute-start = (bf16[256,1024]{1,0:T(8,128)(2,1)}, bf16[256,1024]{1,0:T(8,128)(2,1)}, u32[]{:S(2)}, u32[]{:S(2)}) collective-permute-start(bf16[256,1024]{1,0:T(8,128)(2,1)} %get-tuple-element.107.refs_0_), channel_id=1, source_target_pairs={{0,1},{1,2},{2,3},{4,5},{5,6},{6,7},{8,9},{9,10},{10,11},{12,13},{... | collective-permute-start | bytes 1572872 | tf_op jit(solution)/shard_map/ppermute | solution.py:423
  25.6 30.6 %collective-permute-start.3 = (bf16[256,1024]{1,0:T(8,128)(2,1)}, bf16[256,1024]{1,0:T(8,128)(2,1)}, u32[]{:S(2)}, u32[]{:S(2)}) collective-permute-start(bf16[256,1024]{1,0:T(8,128)(2,1)} %get-tuple-element.108.refs_0_), channel_id=1, source_target_pairs={{0,1},{1,2},{2,3},{4,5},{5,6},{6,7},{8,9},{9,10},{10,11},{12,13},{... | collective-permute-start | bytes 1572872 | tf_op jit(solution)/shard_map/ppermute | solution.py:423
  33.7 33.8 %collective-permute-start.7 = (bf16[256,1024]{1,0:T(8,128)(2,1)}, bf16[256,1024]{1,0:T(8,128)(2,1)}, u32[]{:S(2)}, u32[]{:S(2)}) collective-permute-start(bf16[256,1024]{1,0:T(8,128)(2,1)} %collective-permute-done.6.refs_1_), channel_id=1, source_target_pairs={{0,1},{1,2},{2,3},{4,5},{5,6},{6,7},{8,9},{9,10},{10,11},{12,13},{... | collective-permute-start | bytes 1572872 | tf_op jit(solution)/shard_map/ppermute | solution.py:423
  45.0 33.7 %collective-permute-start.1 = (bf16[256,1024]{1,0:T(8,128)(2,1)}, bf16[256,1024]{1,0:T(8,128)(2,1)}, u32[]{:S(2)}, u32[]{:S(2)}) collective-permute-start(bf16[256,1024]{1,0:T(8,128)(2,1)} %collective-permute-done.refs_1_), channel_id=1, source_target_pairs={{0,1},{1,2},{2,3},{4,5},{5,6},{6,7},{8,9},{9,10},{10,11},{12,13},{... | collective-permute-start | bytes 1572872 | tf_op jit(solution)/shard_map/ppermute | solution.py:423
  56.2 33.7 %collective-permute-start.4 = (bf16[256,1024]{1,0:T(8,128)(2,1)}, bf16[256,1024]{1,0:T(8,128)(2,1)}, u32[]{:S(2)}, u32[]{:S(2)}) collective-permute-start(bf16[256,1024]{1,0:T(8,128)(2,1)} %collective-permute-done.3.refs_1_), channel_id=1, source_target_pairs={{0,1},{1,2},{2,3},{4,5},{5,6},{6,7},{8,9},{9,10},{10,11},{12,13},{... | collective-permute-start | bytes 1572872 | tf_op jit(solution)/shard_map/ppermute | solution.py:423
  67.5 33.7 %collective-permute-start.8 = (bf16[256,1024]{1,0:T(8,128)(2,1)}, bf16[256,1024]{1,0:T(8,128)(2,1)}, u32[]{:S(2)}, u32[]{:S(2)}) collective-permute-start(bf16[256,1024]{1,0:T(8,128)(2,1)} %collective-permute-done.7.refs_2_), channel_id=1, source_target_pairs={{0,1},{1,2},{2,3},{4,5},{5,6},{6,7},{8,9},{9,10},{10,11},{12,13},{... | collective-permute-start | bytes 1572872 | tf_op jit(solution)/shard_map/ppermute | solution.py:423
  78.7 62.1 %collective-permute-start.2 = (bf16[256,1024]{1,0:T(8,128)(2,1)}, bf16[256,1024]{1,0:T(8,128)(2,1)S(1)}, u32[]{:S(2)}, u32[]{:S(2)}) collective-permute-start(bf16[256,1024]{1,0:T(8,128)(2,1)} %collective-permute-done.1.refs_2_), channel_id=1, source_target_pairs={{0,1},{1,2},{2,3},{4,5},{5,6},{6,7},{8,9},{9,10},{10,11},{12,13},{... | collective-permute-start | bytes 1572872 | tf_op jit(solution)/shard_map/ppermute | solution.py:423
  89.9 32.6 %collective-permute-start.5 = (bf16[256,1024]{1,0:T(8,128)(2,1)}, bf16[256,1024]{1,0:T(8,128)(2,1)S(1)}, u32[]{:S(2)}, u32[]{:S(2)}) collective-permute-start(bf16[256,1024]{1,0:T(8,128)(2,1)} %collective-permute-done.4.refs_2_), channel_id=1, source_target_pairs={{0,1},{1,2},{2,3},{4,5},{5,6},{6,7},{8,9},{9,10},{10,11},{12,13},{... | collective-permute-start | bytes 1572872 | tf_op jit(solution)/shard_map/ppermute | solution.py:423
  247.4 96.4 %collective-permute-start.15 = (bf16[256,1024]{1,0:T(8,128)(2,1)}, bf16[256,1024]{1,0:T(8,128)(2,1)S(1)}, u32[]{:S(2)}, u32[]{:S(2)}) collective-permute-start(bf16[256,1024]{1,0:T(8,128)(2,1)} %get-tuple-element.89), channel_id=1, source_target_pairs={{1,0},{2,1},{3,2},{5,4},{6,5},{7,6},{9,8},{10,9},{11,10},{13,12},{... | collective-permute-start | bytes 1572872 | tf_op jit(solution)/shard_map/ppermute | solution.py:443
  294.4 50.9 %collective-permute-start.12 = (bf16[256,1024]{1,0:T(8,128)(2,1)}, bf16[256,1024]{1,0:T(8,128)(2,1)S(1)}, u32[]{:S(2)}, u32[]{:S(2)}) collective-permute-start(bf16[256,1024]{1,0:T(8,128)(2,1)} %get-tuple-element.78), channel_id=1, source_target_pairs={{1,0},{2,1},{3,2},{5,4},{6,5},{7,6},{9,8},{10,9},{11,10},{13,12},{... | collective-permute-start | bytes 1572872 | tf_op jit(solution)/shard_map/ppermute | solution.py:443
  341.5 18.2 %collective-permute-start.9 = (bf16[256,1024]{1,0:T(8,128)(2,1)}, bf16[256,1024]{1,0:T(8,128)(2,1)S(1)}, u32[]{:S(2)}, u32[]{:S(2)}) collective-permute-start(bf16[256,1024]{1,0:T(8,128)(2,1)} %get-tuple-element.67), channel_id=1, source_target_pairs={{1,0},{2,1},{3,2},{5,4},{6,5},{7,6},{9,8},{10,9},{11,10},{13,12},{... | collective-permute-start | bytes 1572872 | tf_op jit(solution)/shard_map/ppermute | solution.py:443
  344.0 27.0 %collective-permute-start.16 = (bf16[256,1024]{1,0:T(8,128)(2,1)S(1)}, bf16[256,1024]{1,0:T(8,128)(2,1)S(1)}, u32[]{:S(2)}, u32[]{:S(2)}) collective-permute-start(bf16[256,1024]{1,0:T(8,128)(2,1)S(1)} %add_convert_fusion.1), channel_id=1, source_target_pairs={{1,0},{2,1},{3,2},{5,4},{6,5},{7,6},{9,8},{10,9},{11,10},{13,12},{... | collective-permute-start | bytes 1572872 | tf_op jit(solution)/shard_map/ppermute | solution.py:443
  345.5 36.7 %collective-permute-start.13 = (bf16[256,1024]{1,0:T(8,128)(2,1)S(1)}, bf16[256,1024]{1,0:T(8,128)(2,1)S(1)}, u32[]{:S(2)}, u32[]{:S(2)}) collective-permute-start(bf16[256,1024]{1,0:T(8,128)(2,1)S(1)} %add_convert_fusion.3), channel_id=1, source_target_pairs={{1,0},{2,1},{3,2},{5,4},{6,5},{7,6},{9,8},{10,9},{11,10},{13,12},{... | collective-permute-start | bytes 1572872 | tf_op jit(solution)/shard_map/ppermute | solution.py:443
  360.0 33.5 %collective-permute-start.10 = (bf16[256,1024]{1,0:T(8,128)(2,1)S(1)}, bf16[256,1024]{1,0:T(8,128)(2,1)S(1)}, u32[]{:S(2)}, u32[]{:S(2)}) collective-permute-start(bf16[256,1024]{1,0:T(8,128)(2,1)S(1)} %add_convert_fusion.5), channel_id=1, source_target_pairs={{1,0},{2,1},{3,2},{5,4},{6,5},{7,6},{9,8},{10,9},{11,10},{13,12},{... | collective-permute-start | bytes 1572872 | tf_op jit(solution)/shard_map/ppermute | solution.py:443
  372.0 147.4 %collective-permute-start.17 = (bf16[256,1024]{1,0:T(8,128)(2,1)}, bf16[256,1024]{1,0:T(8,128)(2,1)S(1)}, u32[]{:S(2)}, u32[]{:S(2)}) collective-permute-start(bf16[256,1024]{1,0:T(8,128)(2,1)} %add_convert_fusion), channel_id=1, source_target_pairs={{1,0},{2,1},{3,2},{5,4},{6,5},{7,6},{9,8},{10,9},{11,10},{13,12},{... | collective-permute-start | bytes 1572872 | tf_op jit(solution)/shard_map/ppermute | solution.py:443
  383.3 136.1 %collective-permute-start.14 = (bf16[256,1024]{1,0:T(8,128)(2,1)}, bf16[256,1024]{1,0:T(8,128)(2,1)}, u32[]{:S(2)}, u32[]{:S(2)}) collective-permute-start(bf16[256,1024]{1,0:T(8,128)(2,1)} %add_convert_fusion.2), channel_id=1, source_target_pairs={{1,0},{2,1},{3,2},{5,4},{6,5},{7,6},{9,8},{10,9},{11,10},{13,12},{... | collective-permute-start | bytes 1572872 | tf_op jit(solution)/shard_map/ppermute | solution.py:443
  394.5 124.9 %collective-permute-start.11 = (bf16[256,1024]{1,0:T(8,128)(2,1)}, bf16[256,1024]{1,0:T(8,128)(2,1)}, u32[]{:S(2)}, u32[]{:S(2)}) collective-permute-start(bf16[256,1024]{1,0:T(8,128)(2,1)} %add_convert_fusion.4), channel_id=1, source_target_pairs={{1,0},{2,1},{3,2},{5,4},{6,5},{7,6},{9,8},{10,9},{11,10},{13,12},{... | collective-permute-start | bytes 1572872 | tf_op jit(solution)/shard_map/ppermute | solution.py:443
  396.8 122.6 %copy-start.1 = (f32[256,1024]{1,0:T(8,128)S(1)}, f32[256,1024]{1,0:T(8,128)}, u32[]{:S(2)}) copy-start(f32[256,1024]{1,0:T(8,128)} %get-tuple-element.86) | copy-start | bytes 3145732
  (31 other events, 515.3 us)
Sparse Core Ops, SparseCore 0:
  10.9 48.2 all-gather.4
  61.0 27.8 all-gather.6
  90.9 54.3 all-gather.8
  147.0 54.3 all-gather.10
  396.9 120.9 all-reduce.1

commit v2 on v1

--- a/solution.py
+++ b/solution.py
@@ -353,7 +353,82 @@
     )(place, start, *hidden, q, k, v, mixed, g_mixed, lse, down, up_wide, weight)
 
 
+def sum_kernel(dp, seq, part_ref, out_ref, plane_ref, line_ref, send_sems, recv_sems):
+    me, place = lax.axis_index("dp"), lax.axis_index("seq")
+    barrier = pltpu.get_barrier_semaphore()
+    mesh_type = pl.DeviceIdType.MESH
+
+    def peer(delta):
+        return lax.rem(me + delta, dp), place
+
+    def line_peer(delta):
+        return me, lax.rem(place + delta, seq)
+
+    for delta in range(1, dp):
+        pl.semaphore_signal(barrier, inc=1, device_id=peer(delta), device_id_type=mesh_type)
+    for delta in range(1, seq):
+        pl.semaphore_signal(barrier, inc=1, device_id=line_peer(delta), device_id_type=mesh_type)
+    pl.semaphore_wait(barrier, dp + seq - 2)
+
+    def send(source, target, slot, device):
+        copy = pltpu.make_async_remote_copy(
+            src_ref=source, dst_ref=target, send_sem=send_sems.at[slot], recv_sem=recv_sems.at[slot],
+            device_id=device, device_id_type=mesh_type,
+        )
+        copy.start()
+        return copy
+
+    copies = [
+        send(part_ref.at[lax.rem(me + delta, dp)], plane_ref.at[delta], delta, peer(delta))
+        for delta in range(1, dp)
+    ]
+    total = part_ref[me]
+    for delta in range(1, dp):
+        copies[delta - 1].wait()
+        total = total + plane_ref[delta]
+    line_ref[place] = total
+    copies = [
+        send(line_ref.at[place], line_ref.at[place], dp + delta, line_peer(delta)) for delta in range(1, seq)
+    ]
+    for copy in copies:
+        copy.wait()
+    total = line_ref[0]
+    for index in range(1, seq):
+        total = total + line_ref[index]
+    out_ref[me] = total
+    copies = [
+        send(out_ref.at[me], out_ref.at[me], dp + seq + delta, peer(delta)) for delta in range(1, dp)
+    ]
+    for copy in copies:
+        copy.wait()
+
+
+def run_sum(dp, seq, part):
+    rows, width = part.shape
+    piece = max(8, rows * width // (PAIR * dp))
+    flat = part.reshape(-1, PAIR)
+    used = flat.shape[0]
+    flat = jnp.pad(flat, ((0, dp * piece - used), (0, 0)))
+    slots = 2 * dp + seq
+    total = pl.pallas_call(
+        partial(sum_kernel, dp, seq),
+        in_specs=[pl.BlockSpec(memory_space=pltpu.VMEM)],
+        out_specs=pl.BlockSpec(memory_space=pltpu.VMEM),
+        out_shape=jax.ShapeDtypeStruct((dp, piece, PAIR), F32),
+        scratch_shapes=[
+            pltpu.VMEM((dp, piece, PAIR), F32),
+            pltpu.VMEM((seq, piece, PAIR), F32),
+            pltpu.SemaphoreType.DMA((slots,)),
+            pltpu.SemaphoreType.DMA((slots,)),
+        ],
+        compiler_params=pltpu.CompilerParams(collective_id=1, has_side_effects=True),
+        name="sum_all",
+    )(flat.reshape(dp, piece, PAIR))
+    return total.reshape(-1, PAIR)[:used].reshape(rows, width)
+
+
 def on_device(
+    dp,
     seq,
     block_input,
     seg_start,
@@ -418,6 +493,8 @@
     for r in range(rows):
         normed, _ = norm_parts(block_input[r].astype(F32))
         first = (normed * ln1_gain + ln1_bias).astype(BF16)
+        if r > 0:
+            first = lax.optimization_barrier((first, hidden_rows[-1][-1]))[0]
         hidden = [first]
         for _ in range(seq - 1):
             hidden.append(lax.ppermute(hidden[-1], "seq", upward))
@@ -446,7 +523,7 @@
         normed, inverse = norm_parts(block_input[r].astype(F32))
         grads.append(g_middle + norm_backward(total, normed, inverse, ln1_gain))
 
-    summed = lax.psum(jnp.concatenate([reduce_sum * ADAPTER_SCALE, up_sum], axis=0), ("dp", "seq"))
+    summed = run_sum(dp, seq, jnp.concatenate([reduce_sum * ADAPTER_SCALE, up_sum], axis=0))
     return (
         jnp.stack(outs),
         jnp.stack(grads),
@@ -459,7 +536,7 @@
 
 def solution(mesh):
     return jax.shard_map(
-        partial(on_device, mesh.shape["seq"]),
+        partial(on_device, mesh.shape["dp"], mesh.shape["seq"]),
         mesh=mesh,
         in_specs=(
             P("dp", "seq", None),

time: 541 us -> 457 us (0.84)
  waiting for transfers between devices: 241 us -> 122 us
  Pallas kernels: 190 us -> 227 us
    psum x1 -> x0, waiting for transfers between devices: 118 us -> none  [on_device(): lax.psum(jnp.concatenate([reduce_sum * ADAPTER_SCALE, up_sum], axis=0), (...]
    pallas_call x0 -> x1, Pallas kernels: none -> 36.7 us  [run_sum(): pl.pallas_call(partial(sum_kernel, dp, seq), in_specs=[pl.BlockSpec(memor...]
    ppermute x9, waiting for transfers between devices: 37.2 us -> 61.2 us  [on_device(): hidden.append(lax.ppermute(hidden[-1], 'seq', upward))]
    all_gather x1, waiting for transfers between devices: 42.4 us -> 18.6 us  [on_device(): whole_proj = lax.all_gather(proj_weight, 'dp', axis=0, tiled=True)]
  transfers between devices with their start and end apart: 23 -> 22, of which waited for: 14 -> 13; matrix products, arithmetic and copies ran while one was open for 4% -> 5% of each run, Pallas kernels for 27% -> 40%
where the time goes in v2:
time: 457 us; the launch traced here: 452 us
  Pallas kernels  227 us (50%)
  waiting for transfers between devices  122 us (27%)
  starting transfers between devices  54.2 us (12%)
  other arithmetic  17.7 us (4%)
  between operations  14.9 us (3%)
  local copies, waits for them, and re-layouts  14 us (3%)
    pallas_call x3, Pallas kernels, run_backward(): pl.pallas_call(partial(backward_kernel, chunks), grid=(quads,), in_specs=...  83 us
    ppermute x9, waiting for transfers between devices, on_device(): hidden.append(lax.ppermute(hidden[-1], 'seq', upward))  61.2 us
    pallas_call x3, Pallas kernels, run_feed(): pl.pallas_call(feed_kernel, grid=(hidden_units // block,), in_specs=[whol...  54.5 us
    pallas_call x3, Pallas kernels, run_forward(): pl.pallas_call(partial(forward_kernel, chunks), grid=(quads,), in_specs=[...  52.4 us
    ppermute x9, starting transfers between devices, on_device(): hidden.append(lax.ppermute(hidden[-1], 'seq', upward))  42.1 us
    ppermute x9, waiting for transfers between devices, on_device(): arrived = lax.ppermute(moving, 'seq', downward)  40.6 us
    pallas_call x1, Pallas kernels, run_sum(): pl.pallas_call(partial(sum_kernel, dp, seq), in_specs=[pl.BlockSpec(memor...  36.7 us
    all_gather x1, waiting for transfers between devices, on_device(): whole_proj = lax.all_gather(proj_weight, 'dp', axis=0, tiled=True)  18.6 us
  transfers between devices with their start and end apart: 22, of which 13 were waited for; matrix products, arithmetic and copies ran while one was open for 5% of the time, Pallas kernels for 40%

profile of v2, /device:TPU:0, one launch (start us, length us, event | category | flops | bytes accessed | tf_op | source)
XLA Modules:
  0.0 452.4 jit_solution(5974329436553860176)
XLA Ops:
  16.2 5.1 %collective-permute-start = (bf16[256,1024]{1,0:T(8,128)(2,1)S(1)}, bf16[256,1024]{1,0:T(8,128)(2,1)S(1)}, u32[]{:S(2)}, u32[]{:S(2)}) collective-permute-start(bf16[256,1024]{1,0:T(8,128)(2,1)S(1)} %get-tuple-element.111.refs_0_), channel_id=1, source_target_pairs={{0,1},{1,2},{2,3},{4,5},{5,6},{6,7},{8,9},{9,10},{10,11},{12,13},{... | collective-permute-start | bytes 1572872 | tf_op jit(solution)/shard_map/ppermute | solution.py:500
  21.3 11.1 %collective-permute-done.refs_1_ = bf16[256,1024]{1,0:T(8,128)(2,1)S(1)} collective-permute-done((bf16[256,1024]{1,0:T(8,128)(2,1)S(1)}, bf16[256,1024]{1,0:T(8,128)(2,1)S(1)}, u32[]{:S(2)}, u32[]{:S(2)}) %collective-permute-start) | collective-permute-done | bytes 524320 | tf_op jit(solution)/shard_map/ppermute | solution.py:500
  36.8 10.4 %collective-permute-done.1.refs_2_ = bf16[256,1024]{1,0:T(8,128)(2,1)S(1)} collective-permute-done((bf16[256,1024]{1,0:T(8,128)(2,1)S(1)}, bf16[256,1024]{1,0:T(8,128)(2,1)S(1)}, u32[]{:S(2)}, u32[]{:S(2)}) %collective-permute-start.1) | collective-permute-done | bytes 524320 | tf_op jit(solution)/shard_map/ppermute | solution.py:500
  51.6 9.5 %collective-permute-done.2.refs_3_ = bf16[256,1024]{1,0:T(8,128)(2,1)S(1)} collective-permute-done((bf16[256,1024]{1,0:T(8,128)(2,1)S(1)}, bf16[256,1024]{1,0:T(8,128)(2,1)S(1)}, u32[]{:S(2)}, u32[]{:S(2)}) %collective-permute-start.2) | collective-permute-done | bytes 524320 | tf_op jit(solution)/shard_map/ppermute | solution.py:500
  65.6 8.6 %collective-permute-done.3.refs_1_ = bf16[256,1024]{1,0:T(8,128)(2,1)S(1)} collective-permute-done((bf16[256,1024]{1,0:T(8,128)(2,1)S(1)}, bf16[256,1024]{1,0:T(8,128)(2,1)S(1)}, u32[]{:S(2)}, u32[]{:S(2)}) %collective-permute-start.3) | collective-permute-done | bytes 524320 | tf_op jit(solution)/shard_map/ppermute | solution.py:500
  78.6 7.7 %collective-permute-done.4.refs_2_ = bf16[256,1024]{1,0:T(8,128)(2,1)S(1)} collective-permute-done((bf16[256,1024]{1,0:T(8,128)(2,1)S(1)}, bf16[256,1024]{1,0:T(8,128)(2,1)S(1)}, u32[]{:S(2)}, u32[]{:S(2)}) %collective-permute-start.4) | collective-permute-done | bytes 524320 | tf_op jit(solution)/shard_map/ppermute | solution.py:500
  90.8 6.9 %collective-permute-done.5.refs_3_ = bf16[256,1024]{1,0:T(8,128)(2,1)S(1)} collective-permute-done((bf16[256,1024]{1,0:T(8,128)(2,1)S(1)}, bf16[256,1024]{1,0:T(8,128)(2,1)S(1)}, u32[]{:S(2)}, u32[]{:S(2)}) %collective-permute-start.5) | collective-permute-done | bytes 524320 | tf_op jit(solution)/shard_map/ppermute | solution.py:500
  98.4 5.2 %collective-permute-start.6 = (bf16[256,1024]{1,0:T(8,128)(2,1)}, bf16[256,1024]{1,0:T(8,128)(2,1)}, u32[]{:S(2)}, u32[]{:S(2)}) collective-permute-start(bf16[256,1024]{1,0:T(8,128)(2,1)} %get-tuple-element.58.refs_0_), channel_id=1, source_target_pairs={{0,1},{1,2},{2,3},{4,5},{5,6},{6,7},{8,9},{9,10},{10,11},{12,13},{... | collective-permute-start | bytes 1572872 | tf_op jit(solution)/shard_map/ppermute | solution.py:500
  111.2 5.2 %collective-permute-start.7 = (bf16[256,1024]{1,0:T(8,128)(2,1)}, bf16[256,1024]{1,0:T(8,128)(2,1)}, u32[]{:S(2)}, u32[]{:S(2)}) collective-permute-start(bf16[256,1024]{1,0:T(8,128)(2,1)} %collective-permute-done.6.refs_1_), channel_id=1, source_target_pairs={{0,1},{1,2},{2,3},{4,5},{5,6},{6,7},{8,9},{9,10},{10,11},{12,13},{... | collective-permute-start | bytes 1572872 | tf_op jit(solution)/shard_map/ppermute | solution.py:500
  129.6 17.5 %attend_forward.4 = (bf16[256,1024]{1,0:T(8,128)(2,1)}, bf16[1024,1024]{1,0:T(8,128)(2,1)}, bf16[1024,1024]{1,0:T(8,128)(2,1)}, bf16[256,1024]{1,0:T(8,128)(2,1)...) custom-call(s32[1]{0:T(128)} %bitcast.place_ref, s32[256,1]{1,0:T(8,128)} %copy.31.start_ref, ...), custom_call_target="tpu_custom_call" | custom-call | flops 5905580032 | bytes 18874368 | tf_op jit(solution)/shard_map/attend_forward/pallas_call | solution.py:240
  147.1 17.5 %attend_forward.3 = (bf16[256,1024]{1,0:T(8,128)(2,1)}, bf16[1024,1024]{1,0:T(8,128)(2,1)}, bf16[1024,1024]{1,0:T(8,128)(2,1)}, bf16[256,1024]{1,0:T(8,128)(2,1)...) custom-call(s32[1]{0:T(128)} %bitcast.place_ref, s32[256,1]{1,0:T(8,128)} %copy.30.start_ref, ...), custom_call_target="tpu_custom_call" | custom-call | flops 5905580032 | bytes 18874368 | tf_op jit(solution)/shard_map/attend_forward/pallas_call | solution.py:240
  165.4 17.4 %attend_forward.5 = (bf16[256,1024]{1,0:T(8,128)(2,1)}, bf16[1024,1024]{1,0:T(8,128)(2,1)}, bf16[1024,1024]{1,0:T(8,128)(2,1)}, bf16[256,1024]{1,0:T(8,128)(2,1)...) custom-call(s32[1]{0:T(128)} %bitcast.place_ref, s32[256,1]{1,0:T(8,128)} %copy.32.start_ref, ...), custom_call_target="tpu_custom_call" | custom-call | flops 5905580032 | bytes 18874368 | tf_op jit(solution)/shard_map/attend_forward/pallas_call | solution.py:240
  182.9 18.6 %all-gather.11.cloned.1.call-done.proj_ref = bf16[4096,1024]{1,0:T(8,128)(2,1)} async-done(((bf16[512,1024]{1,0:T(8,128)(2,1)}), bf16[4096,1024]{1,0:T(8,128)(2,1)}) %all-gather.11.cloned.1.call-update) | async-done | bytes 8388624 | tf_op jit(solution)/shard_map/all_gather | solution.py:479
  201.5 18.4 %feed.5 = (bf16[256,1024]{1,0:T(8,128)(2,1)}, f32[256,1024]{1,0:T(8,128)}, bf16[256,1024]{1,0:T(8,128)(2,1)}) custom-call(bf16[256,1024]{1,0:T(8,128)(2,1)} %get-tuple-element.59.mix_ref.refs_7_, bf16[256,1024]{1,0:T(8,128)(2,1)} %get-tuple-element.132.x_ref, bf16[256,1024]{1,0:T(8,128)(2,1)} %get-tuple-element.117.gout_ref, ...), custom_call_target="tpu_custom_call" | custom-call | flops 9663676416 | bytes 23068672 | tf_op jit(solution)/shard_map/feed/pallas_call | solution.py:284
  219.9 27.6 %attend_backward.5 = (f32[256,1024]{1,0:T(8,128)}, bf16[256,1024]{1,0:T(8,128)(2,1)}, bf16[256,1024]{1,0:T(8,128)(2,1)}, bf16[256,1024]{1,0:T(8,128)(2,1)}, f32[8,1024]{1,0:T(8,128)}, /*index=5*/f32[8,1024]{1,0:T(8,128)}) custom-call(s32[1]{0:T(128)} %bitcast.place_ref, s32[1,256]{1,0:T(1,128)} %copy-done.29, bf16[256,1024]{1,0:T(8,128)(2,1)} %get-tuple-element.58.refs_0_, ...), custom_call_target="tpu_custom_call" | custom-call | flops 7516192768 | bytes 20971520 | tf_op jit(solution)/shard_map/attend_backward/pallas_call | solution.py:325
  248.8 18.0 %feed.4 = (bf16[256,1024]{1,0:T(8,128)(2,1)}, f32[256,1024]{1,0:T(8,128)}, bf16[256,1024]{1,0:T(8,128)(2,1)}) custom-call(bf16[256,1024]{1,0:T(8,128)(2,1)} %get-tuple-element.56.mix_ref.refs_7_, bf16[256,1024]{1,0:T(8,128)(2,1)} %get-tuple-element.131.x_ref, bf16[256,1024]{1,0:T(8,128)(2,1)} %get-tuple-element.118.gout_ref, ...), custom_call_target="tpu_custom_call" | custom-call | flops 9663676416 | bytes 23068672 | tf_op jit(solution)/shard_map/feed/pallas_call | solution.py:284
  266.9 27.6 %attend_backward.4 = (f32[256,1024]{1,0:T(8,128)}, bf16[256,1024]{1,0:T(8,128)(2,1)}, bf16[256,1024]{1,0:T(8,128)(2,1)}, bf16[256,1024]{1,0:T(8,128)(2,1)}, f32[8,1024]{1,0:T(8,128)}, /*index=5*/f32[8,1024]{1,0:T(8,128)}) custom-call(s32[1]{0:T(128)} %bitcast.place_ref, s32[1,256]{1,0:T(1,128)} %copy-done.28, bf16[256,1024]{1,0:T(8,128)(2,1)} %copy-done.15, ...), custom_call_target="tpu_custom_call" | custom-call | flops 7516192768 | bytes 20971520 | tf_op jit(solution)/shard_map/attend_backward/pallas_call | solution.py:325
  295.8 18.1 %feed.3 = (bf16[256,1024]{1,0:T(8,128)(2,1)}, f32[256,1024]{1,0:T(8,128)}, bf16[256,1024]{1,0:T(8,128)(2,1)}) custom-call(bf16[256,1024]{1,0:T(8,128)(2,1)} %get-tuple-element.53.mix_ref.refs_7_, bf16[256,1024]{1,0:T(8,128)(2,1)} %get-tuple-element.133.x_ref, bf16[256,1024]{1,0:T(8,128)(2,1)} %get-tuple-element.116.gout_ref, ...), custom_call_target="tpu_custom_call" | custom-call | flops 9663676416 | bytes 23068672 | tf_op jit(solution)/shard_map/feed/pallas_call | solution.py:284
  313.9 27.7 %attend_backward.3 = (f32[256,1024]{1,0:T(8,128)}, bf16[256,1024]{1,0:T(8,128)(2,1)}, bf16[256,1024]{1,0:T(8,128)(2,1)}, bf16[256,1024]{1,0:T(8,128)(2,1)}, f32[8,1024]{1,0:T(8,128)}, /*index=5*/f32[8,1024]{1,0:T(8,128)}) custom-call(s32[1]{0:T(128)} %bitcast.place_ref, s32[1,256]{1,0:T(1,128)} %copy-done.27, bf16[256,1024]{1,0:T(8,128)(2,1)} %copy-done.14, ...), custom_call_target="tpu_custom_call" | custom-call | flops 7516192768 | bytes 20971520 | tf_op jit(solution)/shard_map/attend_backward/pallas_call | solution.py:325
  346.9 13.0 %collective-permute-done.9 = bf16[256,1024]{1,0:T(8,128)(2,1)S(1)} collective-permute-done((bf16[256,1024]{1,0:T(8,128)(2,1)}, bf16[256,1024]{1,0:T(8,128)(2,1)S(1)}, u32[]{:S(2)}, u32[]{:S(2)}) %collective-permute-start.9) | collective-permute-done | bytes 524320 | tf_op jit(solution)/shard_map/ppermute | solution.py:520
  361.4 9.7 %collective-permute-done.16 = bf16[256,1024]{1,0:T(8,128)(2,1)S(1)} collective-permute-done((bf16[256,1024]{1,0:T(8,128)(2,1)S(1)}, bf16[256,1024]{1,0:T(8,128)(2,1)S(1)}, u32[]{:S(2)}, u32[]{:S(2)}) %collective-permute-start.16) | collective-permute-done | bytes 524320 | tf_op jit(solution)/shard_map/ppermute | solution.py:520
  373.4 8.9 %collective-permute-done.13 = bf16[256,1024]{1,0:T(8,128)(2,1)S(1)} collective-permute-done((bf16[256,1024]{1,0:T(8,128)(2,1)S(1)}, bf16[256,1024]{1,0:T(8,128)(2,1)S(1)}, u32[]{:S(2)}, u32[]{:S(2)}) %collective-permute-start.13) | collective-permute-done | bytes 524320 | tf_op jit(solution)/shard_map/ppermute | solution.py:520
  384.6 9.0 %collective-permute-done.10 = bf16[256,1024]{1,0:T(8,128)(2,1)S(1)} collective-permute-done((bf16[256,1024]{1,0:T(8,128)(2,1)S(1)}, bf16[256,1024]{1,0:T(8,128)(2,1)S(1)}, u32[]{:S(2)}, u32[]{:S(2)}) %collective-permute-start.10) | collective-permute-done | bytes 524320 | tf_op jit(solution)/shard_map/ppermute | solution.py:520
  396.8 36.7 %sum_all.1 = f32[8,16,128]{2,1,0:T(8,128)} custom-call(f32[8,16,128]{2,1,0:T(8,128)} %reshape.121.part_ref), custom_call_target="tpu_custom_call" | custom-call | tf_op jit(solution)/shard_map/sum_all/pallas_call | solution.py:413
  (159 shorter events, 82.0 us)
Async XLA Ops:
  7.2 122.4 %all-gather.5.cloned.1.call-start = ((), (), s32[]{:S(2)}) async-start(), calls=%async_computation | async-start | bytes 7077888 | tf_op jit(solution)/shard_map/all_gather | solution.py:476
  10.8 172.1 %all-gather.7.cloned.1.call-start = ((), (), s32[]{:S(2)}) async-start(), calls=%async_computation.1 | async-start | bytes 2359296 | tf_op jit(solution)/shard_map/all_gather | solution.py:477
  11.5 171.3 %all-gather.9.cloned.1.call-start = ((), (), s32[]{:S(2)}) async-start(), calls=%async_computation.2 | async-start | bytes 9437184 | tf_op jit(solution)/shard_map/all_gather | solution.py:478
  12.3 189.2 %all-gather.11.cloned.1.call-start = ((), (), s32[]{:S(2)}) async-start(), calls=%async_computation.3 | async-start | bytes 9437184 | tf_op jit(solution)/shard_map/all_gather | solution.py:479
  13.9 94.1 %copy-start.24 = (bf16[4,1024]{1,0:T(4,128)(2,1)S(1)}, bf16[4,1024]{1,0:T(4,128)(2,1)}, u32[]{:S(2)}) copy-start(bf16[4,1024]{1,0:T(4,128)(2,1)} %param.30) | copy-start | bytes 24580
  15.4 102.8 %copy-start.4 = (bf16[3,256,1024]{2,1,0:T(8,128)(2,1)S(1)}, bf16[3,256,1024]{2,1,0:T(8,128)(2,1)}, u32[]{:S(2)}) copy-start(bf16[3,256,1024]{2,1,0:T(8,128)(2,1)} %param.39) | copy-start | bytes 4718596
  16.2 16.2 %collective-permute-start = (bf16[256,1024]{1,0:T(8,128)(2,1)S(1)}, bf16[256,1024]{1,0:T(8,128)(2,1)S(1)}, u32[]{:S(2)}, u32[]{:S(2)}) collective-permute-start(bf16[256,1024]{1,0:T(8,128)(2,1)S(1)} %get-tuple-element.111.refs_0_), channel_id=1, source_target_pairs={{0,1},{1,2},{2,3},{4,5},{5,6},{6,7},{8,9},{9,10},{10,11},{12,13},{... | collective-permute-start | bytes 1572872 | tf_op jit(solution)/shard_map/ppermute | solution.py:500
  32.4 14.8 %collective-permute-start.1 = (bf16[256,1024]{1,0:T(8,128)(2,1)S(1)}, bf16[256,1024]{1,0:T(8,128)(2,1)S(1)}, u32[]{:S(2)}, u32[]{:S(2)}) collective-permute-start(bf16[256,1024]{1,0:T(8,128)(2,1)S(1)} %collective-permute-done.refs_1_), channel_id=1, source_target_pairs={{0,1},{1,2},{2,3},{4,5},{5,6},{6,7},{8,9},{9,10},{10,11},{12,13},{... | collective-permute-start | bytes 1572872 | tf_op jit(solution)/shard_map/ppermute | solution.py:500
  47.2 14.0 %collective-permute-start.2 = (bf16[256,1024]{1,0:T(8,128)(2,1)S(1)}, bf16[256,1024]{1,0:T(8,128)(2,1)S(1)}, u32[]{:S(2)}, u32[]{:S(2)}) collective-permute-start(bf16[256,1024]{1,0:T(8,128)(2,1)S(1)} %collective-permute-done.1.refs_2_), channel_id=1, source_target_pairs={{0,1},{1,2},{2,3},{4,5},{5,6},{6,7},{8,9},{9,10},{10,11},{12,13},{... | collective-permute-start | bytes 1572872 | tf_op jit(solution)/shard_map/ppermute | solution.py:500
  61.2 13.0 %collective-permute-start.3 = (bf16[256,1024]{1,0:T(8,128)(2,1)S(1)}, bf16[256,1024]{1,0:T(8,128)(2,1)S(1)}, u32[]{:S(2)}, u32[]{:S(2)}) collective-permute-start(bf16[256,1024]{1,0:T(8,128)(2,1)S(1)} %get-tuple-element.55.refs_0_), channel_id=1, source_target_pairs={{0,1},{1,2},{2,3},{4,5},{5,6},{6,7},{8,9},{9,10},{10,11},{12,13},{... | collective-permute-start | bytes 1572872 | tf_op jit(solution)/shard_map/ppermute | solution.py:500
  74.2 12.1 %collective-permute-start.4 = (bf16[256,1024]{1,0:T(8,128)(2,1)S(1)}, bf16[256,1024]{1,0:T(8,128)(2,1)S(1)}, u32[]{:S(2)}, u32[]{:S(2)}) collective-permute-start(bf16[256,1024]{1,0:T(8,128)(2,1)S(1)} %collective-permute-done.3.refs_1_), channel_id=1, source_target_pairs={{0,1},{1,2},{2,3},{4,5},{5,6},{6,7},{8,9},{9,10},{10,11},{12,13},{... | collective-permute-start | bytes 1572872 | tf_op jit(solution)/shard_map/ppermute | solution.py:500
  86.3 11.3 %collective-permute-start.5 = (bf16[256,1024]{1,0:T(8,128)(2,1)S(1)}, bf16[256,1024]{1,0:T(8,128)(2,1)S(1)}, u32[]{:S(2)}, u32[]{:S(2)}) collective-permute-start(bf16[256,1024]{1,0:T(8,128)(2,1)S(1)} %collective-permute-done.4.refs_2_), channel_id=1, source_target_pairs={{0,1},{1,2},{2,3},{4,5},{5,6},{6,7},{8,9},{9,10},{10,11},{12,13},{... | collective-permute-start | bytes 1572872 | tf_op jit(solution)/shard_map/ppermute | solution.py:500
  98.4 12.7 %collective-permute-start.6 = (bf16[256,1024]{1,0:T(8,128)(2,1)}, bf16[256,1024]{1,0:T(8,128)(2,1)}, u32[]{:S(2)}, u32[]{:S(2)}) collective-permute-start(bf16[256,1024]{1,0:T(8,128)(2,1)} %get-tuple-element.58.refs_0_), channel_id=1, source_target_pairs={{0,1},{1,2},{2,3},{4,5},{5,6},{6,7},{8,9},{9,10},{10,11},{12,13},{... | collective-permute-start | bytes 1572872 | tf_op jit(solution)/shard_map/ppermute | solution.py:500
  111.2 13.8 %collective-permute-start.7 = (bf16[256,1024]{1,0:T(8,128)(2,1)}, bf16[256,1024]{1,0:T(8,128)(2,1)}, u32[]{:S(2)}, u32[]{:S(2)}) collective-permute-start(bf16[256,1024]{1,0:T(8,128)(2,1)} %collective-permute-done.6.refs_1_), channel_id=1, source_target_pairs={{0,1},{1,2},{2,3},{4,5},{5,6},{6,7},{8,9},{9,10},{10,11},{12,13},{... | collective-permute-start | bytes 1572872 | tf_op jit(solution)/shard_map/ppermute | solution.py:500
  124.9 39.6 %collective-permute-start.8 = (bf16[256,1024]{1,0:T(8,128)(2,1)}, bf16[256,1024]{1,0:T(8,128)(2,1)S(1)}, u32[]{:S(2)}, u32[]{:S(2)}) collective-permute-start(bf16[256,1024]{1,0:T(8,128)(2,1)} %collective-permute-done.7.refs_2_), channel_id=1, source_target_pairs={{0,1},{1,2},{2,3},{4,5},{5,6},{6,7},{8,9},{9,10},{10,11},{12,13},{... | collective-permute-start | bytes 1572872 | tf_op jit(solution)/shard_map/ppermute | solution.py:500
  247.5 96.3 %collective-permute-start.15 = (bf16[256,1024]{1,0:T(8,128)(2,1)}, bf16[256,1024]{1,0:T(8,128)(2,1)S(1)}, u32[]{:S(2)}, u32[]{:S(2)}) collective-permute-start(bf16[256,1024]{1,0:T(8,128)(2,1)} %get-tuple-element.93), channel_id=1, source_target_pairs={{1,0},{2,1},{3,2},{5,4},{6,5},{7,6},{9,8},{10,9},{11,10},{13,12},{... | collective-permute-start | bytes 1572872 | tf_op jit(solution)/shard_map/ppermute | solution.py:520
  294.5 50.9 %collective-permute-start.12 = (bf16[256,1024]{1,0:T(8,128)(2,1)}, bf16[256,1024]{1,0:T(8,128)(2,1)S(1)}, u32[]{:S(2)}, u32[]{:S(2)}) collective-permute-start(bf16[256,1024]{1,0:T(8,128)(2,1)} %get-tuple-element.82), channel_id=1, source_target_pairs={{1,0},{2,1},{3,2},{5,4},{6,5},{7,6},{9,8},{10,9},{11,10},{13,12},{... | collective-permute-start | bytes 1572872 | tf_op jit(solution)/shard_map/ppermute | solution.py:520
  341.6 18.3 %collective-permute-start.9 = (bf16[256,1024]{1,0:T(8,128)(2,1)}, bf16[256,1024]{1,0:T(8,128)(2,1)S(1)}, u32[]{:S(2)}, u32[]{:S(2)}) collective-permute-start(bf16[256,1024]{1,0:T(8,128)(2,1)} %get-tuple-element.71), channel_id=1, source_target_pairs={{1,0},{2,1},{3,2},{5,4},{6,5},{7,6},{9,8},{10,9},{11,10},{13,12},{... | collective-permute-start | bytes 1572872 | tf_op jit(solution)/shard_map/ppermute | solution.py:520
  344.1 27.1 %collective-permute-start.16 = (bf16[256,1024]{1,0:T(8,128)(2,1)S(1)}, bf16[256,1024]{1,0:T(8,128)(2,1)S(1)}, u32[]{:S(2)}, u32[]{:S(2)}) collective-permute-start(bf16[256,1024]{1,0:T(8,128)(2,1)S(1)} %add_convert_fusion.1), channel_id=1, source_target_pairs={{1,0},{2,1},{3,2},{5,4},{6,5},{7,6},{9,8},{10,9},{11,10},{13,12},{... | collective-permute-start | bytes 1572872 | tf_op jit(solution)/shard_map/ppermute | solution.py:520
  345.6 36.8 %collective-permute-start.13 = (bf16[256,1024]{1,0:T(8,128)(2,1)S(1)}, bf16[256,1024]{1,0:T(8,128)(2,1)S(1)}, u32[]{:S(2)}, u32[]{:S(2)}) collective-permute-start(bf16[256,1024]{1,0:T(8,128)(2,1)S(1)} %add_convert_fusion.3), channel_id=1, source_target_pairs={{1,0},{2,1},{3,2},{5,4},{6,5},{7,6},{9,8},{10,9},{11,10},{13,12},{... | collective-permute-start | bytes 1572872 | tf_op jit(solution)/shard_map/ppermute | solution.py:520
  360.1 33.5 %collective-permute-start.10 = (bf16[256,1024]{1,0:T(8,128)(2,1)S(1)}, bf16[256,1024]{1,0:T(8,128)(2,1)S(1)}, u32[]{:S(2)}, u32[]{:S(2)}) collective-permute-start(bf16[256,1024]{1,0:T(8,128)(2,1)S(1)} %add_convert_fusion.5), channel_id=1, source_target_pairs={{1,0},{2,1},{3,2},{5,4},{6,5},{7,6},{9,8},{10,9},{11,10},{13,12},{... | collective-permute-start | bytes 1572872 | tf_op jit(solution)/shard_map/ppermute | solution.py:520
  372.1 67.5 %collective-permute-start.17 = (bf16[256,1024]{1,0:T(8,128)(2,1)}, bf16[256,1024]{1,0:T(8,128)(2,1)S(1)}, u32[]{:S(2)}, u32[]{:S(2)}) collective-permute-start(bf16[256,1024]{1,0:T(8,128)(2,1)} %add_convert_fusion), channel_id=1, source_target_pairs={{1,0},{2,1},{3,2},{5,4},{6,5},{7,6},{9,8},{10,9},{11,10},{13,12},{... | collective-permute-start | bytes 1572872 | tf_op jit(solution)/shard_map/ppermute | solution.py:520
  383.3 56.3 %collective-permute-start.14 = (bf16[256,1024]{1,0:T(8,128)(2,1)}, bf16[256,1024]{1,0:T(8,128)(2,1)S(1)}, u32[]{:S(2)}, u32[]{:S(2)}) collective-permute-start(bf16[256,1024]{1,0:T(8,128)(2,1)} %add_convert_fusion.2), channel_id=1, source_target_pairs={{1,0},{2,1},{3,2},{5,4},{6,5},{7,6},{9,8},{10,9},{11,10},{13,12},{... | collective-permute-start | bytes 1572872 | tf_op jit(solution)/shard_map/ppermute | solution.py:520
  394.6 45.1 %collective-permute-start.11 = (bf16[256,1024]{1,0:T(8,128)(2,1)}, bf16[256,1024]{1,0:T(8,128)(2,1)S(1)}, u32[]{:S(2)}, u32[]{:S(2)}) collective-permute-start(bf16[256,1024]{1,0:T(8,128)(2,1)} %add_convert_fusion.4), channel_id=1, source_target_pairs={{1,0},{2,1},{3,2},{5,4},{6,5},{7,6},{9,8},{10,9},{11,10},{13,12},{... | collective-permute-start | bytes 1572872 | tf_op jit(solution)/shard_map/ppermute | solution.py:520
  (36 other events, 731.8 us)
Sparse Core Ops, SparseCore 0:
  10.9 48.2 all-gather.4
  61.0 27.8 all-gather.6
  90.9 54.3 all-gather.8
  147.0 54.3 all-gather.10

commit v3 on v2

--- a/solution.py
+++ b/solution.py
@@ -1,3 +1,4 @@
+import math
 from functools import partial
 
 import jax
@@ -50,50 +51,290 @@
     return lane < HEAD
 
 
-def forward_kernel(chunks, place_ref, start_ref, *refs):
-    hidden = refs[:chunks]
-    wq, wk, wv, bias_q, bias_v, reduce_ref = refs[chunks : chunks + 6]
-    q_out, k_out, v_out, mix_out, lse_out, down_out, mask_ref = refs[chunks + 6 :]
-    tokens = hidden[0].shape[0]
-    quad = pl.program_id(0)
-
-    @pl.when(quad == 0)
+def start_kernel(
+    plane, seq, rows,
+    x_ref, start_ref, gain_ref, shift_ref, shard_ref, reduce_ref, up_ref, bias_q, bias_v, wo_in, fc_in, proj_in,
+    w_out, wo_out, fc_out, proj_out, hidden_out, q_out, k_out, v_out, mix_out, lse_out, down_out,
+    w_held, hidden, q_held, k_held, v_held, mix_held, mask_ref,
+    send_sems, recv_sems, hop_send, hop_recv, own_sems, store_sems,
+):
+    nx, ny = plane
+    tokens, width = x_ref.shape[1], x_ref.shape[2]
+    length = seq * tokens
+    mesh_type = pl.DeviceIdType.MESH
+    me, place = lax.axis_index("dp"), lax.axis_index("seq")
+    core = lax.rem(me, 2)
+    my_x = lax.rem(me // 2, nx)
+    my_y = me // (2 * nx)
+
+    def index(y, x, c):
+        return (y * nx + x) * 2 + c
+
+    def x_peer(delta):
+        return index(my_y, lax.rem(my_x + delta, nx), core), place
+
+    def y_peer(delta):
+        return index(lax.rem(my_y + delta, ny), my_x, core), place
+
+    twin = (index(my_y, my_x, 1 - core), place)
+
+    def owner(dy, dx, c):
+        return index(lax.rem(my_y + ny - dy, ny), lax.rem(my_x + nx - dx, nx), c)
+
+    barrier = pltpu.get_barrier_semaphore()
+    for delta in range(1, nx):
+        pl.semaphore_signal(barrier, inc=1, device_id=x_peer(delta), device_id_type=mesh_type)
+    for delta in range(1, ny):
+        pl.semaphore_signal(barrier, inc=1, device_id=y_peer(delta), device_id_type=mesh_type)
+    pl.semaphore_signal(barrier, inc=1, device_id=twin, device_id_type=mesh_type)
+
+    @pl.when(place > 0)
     def _():
-        place = place_ref[0]
+        pl.semaphore_signal(barrier, inc=1, device_id=(me, place - 1), device_id_type=mesh_type)
+
+    @pl.when(place < seq - 1)
+    def _():
+        pl.semaphore_signal(barrier, inc=1, device_id=(me, place + 1), device_id_type=mesh_type)
+
+    shards = [shard_ref.shape[0], wo_in.shape[0], fc_in.shape[0], proj_in.shape[0]]
+    sources = [None, wo_in, fc_in, proj_in]
+    targets = [w_held, wo_out, fc_out, proj_out]
+
+    def region(t, device, half=None):
+        size = shards[t]
+        if half is None:
+            return targets[t].at[pl.ds(pl.multiple_of(device * size, size), size), :]
+        part = size // 2
+        return targets[t].at[pl.ds(pl.multiple_of(device * size + half * part, part), part), :]
+
+    pending = []
+
+    def send(t, slot, source, target, device):
+        copy = pltpu.make_async_remote_copy(
+            src_ref=source, dst_ref=target, send_sem=send_sems.at[t, slot], recv_sem=recv_sems.at[t, slot],
+            device_id=device, device_id_type=mesh_type,
+        )
+        copy.start()
+        pending.append(copy)
+        return copy
+
+    first_x, first_y = nx - 1, nx - 1 + ny - 1
+    cross = (nx - 1) * (ny - 1)
+
+    def slot_a(dy, dx):
+        return first_y + (dy - 1) * (nx - 1) + dx - 1
+
+    def slot_b(dy, dx):
+        return first_y + cross + (dy - 1) * (nx - 1) + dx - 1
+
+    def slot_twin(dy, dx):
+        return first_y + 2 * cross + dy * nx + dx
+
+    flights = {}
+
+    def wave_one(t):
+        mine = region(t, me) if sources[t] is None else sources[t]
+        for delta in range(1, nx):
+            flights[t, "x", delta] = send(t, delta - 1, mine, region(t, me), x_peer(delta))
+        for delta in range(1, ny):
+            flights[t, "y", delta] = send(t, first_x + delta - 1, mine, region(t, me), y_peer(delta))
+        flights[t, "t", 0, 0] = send(t, slot_twin(0, 0), mine, region(t, me), twin)
+
+    def wave_two(t):
+        for dx in range(1, nx):
+            flights[t, "x", dx].wait_recv()
+            device = owner(0, dx, core)
+            for dy in range(1, ny):
+                part = region(t, device, 0)
+                flights[t, "a", dy, dx] = send(t, slot_a(dy, dx), part, part, y_peer(dy))
+        for dy in range(1, ny):
+            flights[t, "y", dy].wait_recv()
+            device = owner(dy, 0, core)
+            for dx in range(1, nx):
+                part = region(t, device, 1)
+                flights[t, "b", dy, dx] = send(t, slot_b(dy, dx), part, part, x_peer(dx))
+        for dx in range(1, nx):
+            part = region(t, owner(0, dx, core))
+            flights[t, "t", 0, dx] = send(t, slot_twin(0, dx), part, part, twin)
+        for dy in range(1, ny):
+            part = region(t, owner(dy, 0, core))
+            flights[t, "t", dy, 0] = send(t, slot_twin(dy, 0), part, part, twin)
+
+    def wave_three(t):
+        for dy in range(1, ny):
+            for dx in range(1, nx):
+                flights[t, "a", dy, dx].wait_recv()
+                flights[t, "b", dy, dx].wait_recv()
+                part = region(t, owner(dy, dx, core))
+                flights[t, "t", dy, dx] = send(t, slot_twin(dy, dx), part, part, twin)
+
+    def wave_end(t):
+        for dy in range(ny):
+            for dx in range(nx):
+                flights[t, "t", dy, dx].wait_recv()
+
+    def hop(row, s):
+        return pltpu.make_async_remote_copy(
+            src_ref=hidden.at[row, s - 1], dst_ref=hidden.at[row, s],
+            send_sem=hop_send.at[row, s - 1], recv_sem=hop_recv.at[row, s - 1],
+            device_id=(me, place + 1), device_id_type=mesh_type,
+        )
+
+    def hop_start(row, s):
+        @pl.when((place >= s - 1) & (place < seq - 1))
+        def _():
+            hop(row, s).start()
+
+    size = shards[0]
+    mine = pl.ds(pl.multiple_of(me * size, size), size)
+    reduce_own = reduce_ref[mine, :]
+    up = up_ref[...]
+    low_rank = lax.broadcasted_iota(jnp.int32, up.shape, 0) < 4
+    for column, rank_up in ((0, jnp.where(low_rank, up, jnp.zeros_like(up))), (2, jnp.where(low_rank, jnp.zeros_like(up), up))):
+        span = slice(column * width, (column + 1) * width)
+        change = dot_nn(reduce_own, rank_up) * ADAPTER_SCALE
+        w_held[mine, span] = (shard_ref[:, span].astype(F32) + change).astype(BF16)
+    w_held[mine, width : 2 * width] = shard_ref[:, width : 2 * width]
+
+    def first_norm(row):
+        normed, _ = norm_parts(x_ref[row].astype(F32))
+        hidden[row, 0] = (normed * gain_ref[...] + shift_ref[...]).astype(BF16)
+
+    first_norm(0)
+    heard = (nx - 1) + (ny - 1) + 1 + (place > 0).astype(jnp.int32) + (place < seq - 1).astype(jnp.int32)
+    pl.semaphore_wait(barrier, heard)
+    hop_start(0, 1)
+    wave_one(0)
+    own_copies = [
+        pltpu.make_async_copy(sources[t], region(t, me), own_sems.at[t]) for t in range(1, 4)
+    ]
+    for copy in own_copies:
+        copy.start()
+    for row in range(1, rows):
+        first_norm(row)
+    for s in range(1, seq):
+        @pl.when(place < s)
+        def _():
+            for row in range(rows):
+                hidden[row, s] = jnp.zeros((tokens, width), BF16)
+
+    low = head_lanes(tokens, BF16)
+    lane = lax.broadcasted_iota(jnp.int32, (tokens, PAIR), 1)
+
+    def row_hops(row):
+        for s in range(1, seq):
+            @pl.when(place >= s)
+            def _():
+                hop(row, s).wait_recv()
+
+            if s < seq - 1:
+                hop_start(row, s + 1)
+            elif row < rows - 1:
+                hop_start(row + 1, 1)
+
+    def stores(row):
+        slot = row % 2
+        return [
+            pltpu.make_async_copy(held.at[slot], out.at[row], store_sems.at[slot, i])
+            for i, (held, out) in enumerate(
+                ((q_held, q_out), (k_held, k_out), (v_held, v_out), (mix_held, mix_out))
+            )
+        ]
+
+    def attend(row):
+        slot = row % 2
         query = place * tokens + lax.broadcasted_iota(jnp.int32, (tokens, tokens), 0)
-        start = start_ref[...]
-        for s in range(chunks):
+        start = start_ref[row]
+        for s in range(seq):
             key = (place - s) * tokens + lax.broadcasted_iota(jnp.int32, (tokens, tokens), 1)
             allowed = key >= start
             if s == 0:
                 allowed = allowed & (key <= query)
-            mask_ref[:, s * tokens : (s + 1) * tokens] = jnp.where(allowed, 0.0, MASKED)
-            down = dot_nn(hidden[s][...], reduce_ref[...]) * ADAPTER_SCALE
-            down_out[:, s * tokens : (s + 1) * tokens] = down.T[:8].astype(BF16)
-
-    q_out[...] = ((dot_nn(hidden[0][...], wq[...]) + bias_q[...]).astype(BF16) * (HEAD**-0.5)).astype(BF16)
-    for s in range(chunks):
-        span = slice(s * tokens, (s + 1) * tokens)
-        k_out[span, :] = dot_nn(hidden[s][...], wk[...]).astype(BF16)
-        v_out[span, :] = (dot_nn(hidden[s][...], wv[...]) + bias_v[...]).astype(BF16)
-    low = head_lanes(tokens, BF16)
-    lane = lax.broadcasted_iota(jnp.int32, (tokens, PAIR), 1)
-    totals = jnp.zeros((tokens, PAIR), F32)
-    for pair in range(QUAD // PAIR):
-        span = slice(pair * PAIR, (pair + 1) * PAIR)
-        q_pair = q_out[:, span]
-        mixed = []
-        for half in range(2):
-            own = low if half == 0 else jnp.logical_not(low)
-            q_head = jnp.where(own, q_pair, jnp.zeros_like(q_pair))
-            score = dot_nt(q_head, k_out[:, span]) + mask_ref[...]
-            highest = jnp.max(score, axis=-1, keepdims=True)
-            weight = jnp.exp(score - highest)
-            total = jnp.sum(weight, axis=-1, keepdims=True)
-            mixed.append(dot_nn(weight.astype(BF16), v_out[:, span]) * (1.0 / total))
-            totals = jnp.where(lane == pair * 2 + half, highest + jnp.log(total), totals)
-        mix_out[:, span] = jnp.where(low, mixed[0], mixed[1]).astype(BF16)
-    lse_out[0] = totals.T[:8]
+            span = slice(s * tokens, (s + 1) * tokens)
+            mask_ref[:, span] = jnp.where(allowed, 0.0, MASKED)
+            down = dot_nn(hidden[row, s], reduce_ref[...]) * ADAPTER_SCALE
+            down_out[row, :, span] = down.T[:8].astype(BF16)
+
+        @pl.loop(0, width // QUAD)
+        def _(quad):
+            def part(block):
+                return pl.ds(pl.multiple_of(block * width + quad * QUAD, QUAD), QUAD)
+
+            q = dot_nn(hidden[row, 0], w_held[:, part(0)]) + bias_q[:, part(0)]
+            q_held[slot, :, part(0)] = (q.astype(BF16) * (HEAD**-0.5)).astype(BF16)
+            for s in range(seq):
+                span = slice(s * tokens, (s + 1) * tokens)
+                k_held[slot, span, part(0)] = dot_nn(hidden[row, s], w_held[:, part(1)]).astype(BF16)
+                v = dot_nn(hidden[row, s], w_held[:, part(2)]) + bias_v[:, part(0)]
+                v_held[slot, span, part(0)] = v.astype(BF16)
+            totals = jnp.zeros((tokens, PAIR), F32)
+            for pair in range(QUAD // PAIR):
+                span = pl.ds(pl.multiple_of(quad * QUAD, QUAD) + pair * PAIR, PAIR)
+                q_pair = q_held[slot, :, span]
+                mixed = []
+                for half in range(2):
+                    own = low if half == 0 else jnp.logical_not(low)
+                    q_head = jnp.where(own, q_pair, jnp.zeros_like(q_pair))
+                    score = dot_nt(q_head, k_held[slot, :, span]) + mask_ref[...]
+                    highest = jnp.max(score, axis=-1, keepdims=True)
+                    weight = jnp.exp(score - highest)
+                    total = jnp.sum(weight, axis=-1, keepdims=True)
+                    mixed.append(dot_nn(weight.astype(BF16), v_held[slot, :, span]) * (1.0 / total))
+                    totals = jnp.where(lane == pair * 2 + half, highest + jnp.log(total), totals)
+                mix_held[slot, :, span] = jnp.where(low, mixed[0], mixed[1]).astype(BF16)
+            lse_out[row, quad] = totals.T[:8]
+
+    hidden_copies = [pltpu.make_async_copy(hidden.at[row], hidden_out.at[row], own_sems.at[4 + row]) for row in range(rows)]
+    w_copy = pltpu.make_async_copy(w_held, w_out, own_sems.at[0])
+    for row in range(rows):
+        if row == 0:
+            wave_two(0)
+            wave_one(1)
+            wave_one(2)
+        elif row == 1:
+            wave_two(1)
+            wave_two(2)
+            wave_one(3)
+        elif row == 2:
+            wave_three(1)
+            wave_three(2)
+            wave_two(3)
+        row_hops(row)
+        if row == 0:
+            wave_three(0)
+            wave_end(0)
+            w_copy.start()
+        hidden_copies[row].start()
+        if row >= 2:
+            for copy in stores(row - 2):
+                copy.wait()
+        attend(row)
+        for copy in stores(row):
+            copy.start()
+    done = min(rows, 3)
+    if done < 2:
+        wave_two(1)
+        wave_two(2)
+        wave_one(3)
+    if done < 3:
+        wave_three(1)
+        wave_three(2)
+        wave_two(3)
+    wave_three(3)
+    for t in range(1, 4):
+        wave_end(t)
+    for row in range(max(0, rows - 2), rows):
+        for copy in stores(row):
+            copy.wait()
+    for copy in own_copies + hidden_copies + [w_copy]:
+        copy.wait()
+    for copy in pending:
+        copy.wait_send()
+    for row in range(rows):
+        for s in range(1, seq):
+            @pl.when((place >= s - 1) & (place < seq - 1))
+            def _():
+                hop(row, s).wait_send()
 
 
 def feed_kernel(
@@ -140,10 +381,10 @@
 
 
 def backward_kernel(chunks, place_ref, start_ref, *refs):
-    hidden = refs[:chunks]
-    q_ref, k_ref, v_ref, mix_ref, g_ref, lse_ref, down_ref, up_ref, w_ref = refs[chunks : chunks + 9]
-    grads = refs[chunks + 9 : 2 * chunks + 9]
-    reduce_out, up_out, mask_ref, dq_ref, dkv_ref, w_held, w_sem = refs[2 * chunks + 9 :]
+    hidden_ref, q_ref, k_ref, v_ref, mix_ref, g_ref, lse_ref, down_ref, up_ref, w_ref = refs[:10]
+    grads = refs[10 : chunks + 10]
+    reduce_out, up_out, mask_ref, dq_ref, dkv_ref, w_held, w_sem = refs[chunks + 10 :]
+    hidden = [hidden_ref.at[s] for s in range(chunks)]
     tokens = hidden[0].shape[0]
     width = hidden[0].shape[1]
     quad = pl.program_id(0)
@@ -231,60 +472,65 @@
     return pl.BlockSpec(shape, lambda i: (0,) * len(shape))
 
 
-def run_forward(place, start, hidden, weight, query_bias, value_bias, reduce_wide):
-    chunks = len(hidden)
-    tokens, width = hidden[0].shape
-    length = chunks * tokens
+def run_start(plane, seq, x, starts, gain, shift, shard, reduce_wide, up_wide, bias_q, bias_v, wo, fc, proj):
+    rows, tokens, width = x.shape
+    length = seq * tokens
     quads = width // QUAD
-    flops = 2 * width * width * (tokens + 2 * length) + 4 * tokens * length * width
+    dp = plane[0] * plane[1] * 2
+    anywhere = pl.BlockSpec(memory_space=pl.ANY)
+    vmem = pl.BlockSpec(memory_space=pltpu.VMEM)
+    nx, ny = plane
+    slots = nx - 1 + ny - 1 + 2 * (nx - 1) * (ny - 1) + nx * ny
+
+    def shape(*dims, dtype=BF16):
+        return jax.ShapeDtypeStruct(dims, dtype)
+
+    def whole_of(part):
+        return shape(part.shape[0] * dp, part.shape[1])
+
     return pl.pallas_call(
-        partial(forward_kernel, chunks),
-        grid=(quads,),
-        in_specs=[pl.BlockSpec(memory_space=pltpu.SMEM), whole((tokens, 1))]
-        + [whole((tokens, width))] * chunks
-        + [
-            pl.BlockSpec((width, QUAD), lambda i: (0, i)),
-            pl.BlockSpec((width, QUAD), lambda i: (0, i + quads)),
-            pl.BlockSpec((width, QUAD), lambda i: (0, i + 2 * quads)),
-            pl.BlockSpec((1, QUAD), lambda i: (0, i)),
-            pl.BlockSpec((1, QUAD), lambda i: (0, i)),
-            whole((width, PAIR)),
+        partial(start_kernel, plane, seq, rows),
+        in_specs=[vmem] * 9 + [anywhere] * 3,
+        out_specs=[anywhere] * 9 + [vmem] * 2,
+        out_shape=[
+            whole_of(shard), whole_of(wo), whole_of(fc), whole_of(proj),
+            shape(rows, seq, tokens, width),
+            shape(rows, tokens, width), shape(rows, length, width), shape(rows, length, width),
+            shape(rows, tokens, width),
+            shape(rows, quads, 8, tokens, dtype=F32),
+            shape(rows, 8, length),
         ],
-        out_specs=[
-            pl.BlockSpec((tokens, QUAD), lambda i: (0, i)),
-            pl.BlockSpec((length, QUAD), lambda i: (0, i)),
-            pl.BlockSpec((length, QUAD), lambda i: (0, i)),
-            pl.BlockSpec((tokens, QUAD), lambda i: (0, i)),
-            pl.BlockSpec((1, 8, tokens), lambda i: (i, 0, 0)),
-            whole((8, length)),
+        scratch_shapes=[
+            pltpu.VMEM((width, 3 * width), BF16),
+            pltpu.VMEM((rows, seq, tokens, width), BF16),
+            pltpu.VMEM((2, tokens, width), BF16),
+            pltpu.VMEM((2, length, width), BF16),
+            pltpu.VMEM((2, length, width), BF16),
+            pltpu.VMEM((2, tokens, width), BF16),
+            pltpu.VMEM((tokens, length), F32),
+            pltpu.SemaphoreType.DMA((4, slots)),
+            pltpu.SemaphoreType.DMA((4, slots)),
+            pltpu.SemaphoreType.DMA((rows, seq - 1)),
+            pltpu.SemaphoreType.DMA((rows, seq - 1)),
+            pltpu.SemaphoreType.DMA((4 + rows,)),
+            pltpu.SemaphoreType.DMA((2, 4)),
         ],
-        out_shape=[
-            jax.ShapeDtypeStruct((tokens, width), BF16),
-            jax.ShapeDtypeStruct((length, width), BF16),
-            jax.ShapeDtypeStruct((length, width), BF16),
-            jax.ShapeDtypeStruct((tokens, width), BF16),
-            jax.ShapeDtypeStruct((quads, 8, tokens), F32),
-            jax.ShapeDtypeStruct((8, length), BF16),
-        ],
-        scratch_shapes=[pltpu.VMEM((tokens, length), F32)],
-        compiler_params=pltpu.CompilerParams(vmem_limit_bytes=VMEM_BYTES),
-        cost_estimate=pl.CostEstimate(
-            flops=flops, bytes_accessed=8 * width * width + 10 * length * width,
-            transcendentals=tokens * length * width // HEAD,
+        compiler_params=pltpu.CompilerParams(
+            vmem_limit_bytes=VMEM_BYTES, collective_id=0, has_side_effects=True
         ),
-        name="attend_forward",
-    )(place, start, *hidden, weight, weight, weight, query_bias, value_bias, reduce_wide)
-
-
-def run_feed(mixed, x, grad_out, out_weight, vectors, fc_weight, fc_bias, proj_weight):
-    tokens, width = x.shape
+        name="start",
+    )(x, starts, gain, shift, shard, reduce_wide, up_wide, bias_q, bias_v, wo, fc, proj)
+
+
+def run_feed(row, mixed, x, grad_out, out_weight, vectors, fc_weight, fc_bias, proj_weight):
+    _, tokens, width = x.shape
     hidden_units = fc_weight.shape[1]
     block = 1024
     out_bias, gain, shift, proj_bias = vectors
     return pl.pallas_call(
         feed_kernel,
         grid=(hidden_units // block,),
-        in_specs=[whole((tokens, width))] * 3
+        in_specs=[pl.BlockSpec((None, tokens, width), lambda i: (row, 0, 0))] * 3
         + [whole((width, width))]
         + [whole((1, width))] * 4
         + [
@@ -314,23 +560,22 @@
     )(mixed, x, grad_out, out_weight, out_bias, gain, shift, proj_bias, fc_weight, fc_bias, proj_weight)
 
 
-def run_backward(place, start, hidden, q, k, v, mixed, g_mixed, lse, down, up_wide, weight):
-    chunks = len(hidden)
-    tokens, width = hidden[0].shape
+def run_backward(row, place, start, hidden, q, k, v, mixed, g_mixed, lse, down, up_wide, weight):
+    _, chunks, tokens, width = hidden.shape
     length = chunks * tokens
     quads = width // QUAD
     flops = 2 * width * width * (tokens + 2 * length) + 10 * tokens * length * width
-    own = pl.BlockSpec((tokens, QUAD), lambda i: (0, i))
-    every = pl.BlockSpec((length, QUAD), lambda i: (0, i))
+    own = pl.BlockSpec((None, tokens, QUAD), lambda i: (row, 0, i))
+    every = pl.BlockSpec((None, length, QUAD), lambda i: (row, 0, i))
     return pl.pallas_call(
         partial(backward_kernel, chunks),
         grid=(quads,),
         in_specs=[pl.BlockSpec(memory_space=pltpu.SMEM), whole((1, tokens))]
-        + [whole((tokens, width))] * chunks
         + [
-            own, every, every, own, own,
-            pl.BlockSpec((1, 8, tokens), lambda i: (i, 0, 0)),
-            whole((8, length)),
+            pl.BlockSpec((None, chunks, tokens, width), lambda i: (row, 0, 0, 0)),
+            own, every, every, own, pl.BlockSpec((tokens, QUAD), lambda i: (0, i)),
+            pl.BlockSpec((None, 1, 8, tokens), lambda i: (row, i, 0, 0)),
+            pl.BlockSpec((None, 8, length), lambda i: (row, 0, 0)),
             whole((PAIR, width)),
             pl.BlockSpec(memory_space=pl.ANY),
         ],
@@ -350,7 +595,7 @@
             transcendentals=tokens * length * width // HEAD,
         ),
         name="attend_backward",
-    )(place, start, *hidden, q, k, v, mixed, g_mixed, lse, down, up_wide, weight)
+    )(place, start, hidden, q, k, v, mixed, g_mixed, lse, down, up_wide, weight)
 
 
 def sum_kernel(dp, seq, part_ref, out_ref, plane_ref, line_ref, send_sems, recv_sems):
@@ -453,30 +698,9 @@
 ):
     rows, tokens, width = block_input.shape
     rank = query_up.shape[0]
-    shard = qkv_weight.shape[0]
     place = lax.axis_index("seq")
-    upward = [(i, i + 1) for i in range(seq - 1)]
     downward = [(i + 1, i) for i in range(seq - 1)]
-
-    def own_rows(reduce):
-        return lax.dynamic_slice(reduce, (lax.axis_index("dp") * shard, 0), (shard, rank))
-
-    def folded(part, reduce, up):
-        change = jnp.dot(own_rows(reduce), up, preferred_element_type=F32) * ADAPTER_SCALE
-        return (part.astype(F32) + change).astype(BF16)
-
-    weight_shard = jnp.concatenate(
-        [
-            folded(qkv_weight[:, :width], query_adapter_reduce, query_up),
-            qkv_weight[:, width : 2 * width],
-            folded(qkv_weight[:, 2 * width :], value_adapter_reduce, value_up),
-        ],
-        axis=1,
-    )
-    weight = lax.all_gather(weight_shard, "dp", axis=0, tiled=True)
-    whole_out = lax.all_gather(out_weight, "dp", axis=0, tiled=True)
-    whole_fc = lax.all_gather(fc_weight, "dp", axis=0, tiled=True)
-    whole_proj = lax.all_gather(proj_weight, "dp", axis=0, tiled=True)
+    side = math.isqrt(dp // 2)
 
     pad = jnp.zeros((width, PAIR - 2 * rank), BF16)
     reduce_wide = jnp.concatenate([query_adapter_reduce, value_adapter_reduce, pad], axis=1)
@@ -488,30 +712,19 @@
         return vector.reshape(1, -1)
 
     vectors = tuple(as_row(a) for a in (out_bias, ln2_gain, ln2_bias, proj_bias))
-
-    hidden_rows = []
-    for r in range(rows):
-        normed, _ = norm_parts(block_input[r].astype(F32))
-        first = (normed * ln1_gain + ln1_bias).astype(BF16)
-        if r > 0:
-            first = lax.optimization_barrier((first, hidden_rows[-1][-1]))[0]
-        hidden = [first]
-        for _ in range(seq - 1):
-            hidden.append(lax.ppermute(hidden[-1], "seq", upward))
-        hidden_rows.append(hidden)
+    weight, whole_out, whole_fc, whole_proj, hidden, q, k, v, mixed, lse, down = run_start(
+        (side, dp // (2 * side)), seq, block_input, starts[:, :, None], as_row(ln1_gain), as_row(ln1_bias), qkv_weight,
+        reduce_wide, up_wide, as_row(query_bias), as_row(value_bias), out_weight, fc_weight, proj_weight,
+    )
 
     outs, grads, reduce_sum, up_sum = [], [], 0.0, 0.0
     for r in range(rows):
-        hidden = hidden_rows[r]
-        q, k, v, mixed, lse, down = run_forward(
-            place_ref, starts[r].reshape(tokens, 1), hidden, weight, as_row(query_bias), as_row(value_bias), reduce_wide
-        )
         out, g_middle, g_mixed = run_feed(
-            mixed, block_input[r], grad_out[r], whole_out, vectors, whole_fc, as_row(fc_bias), whole_proj
+            r, mixed, block_input, grad_out, whole_out, vectors, whole_fc, as_row(fc_bias), whole_proj
         )
         outs.append(out)
         result = run_backward(
-            place_ref, starts[r].reshape(1, tokens), hidden, q, k, v, mixed, g_mixed, lse, down, up_wide, weight
+            r, place_ref, starts[r].reshape(1, tokens), hidden, q, k, v, mixed, g_mixed, lse, down, up_wide, weight
         )
         reduce_sum = reduce_sum + result[seq]
         up_sum = up_sum + result[seq + 1]

time: 457 us -> 395 us (0.86)
  Pallas kernels: 227 us -> 296 us
  waiting for transfers between devices: 122 us -> 54.6 us
  starting transfers between devices: 54.2 us -> 12 us
  between operations: 14.9 us -> 1.64 us
  local copies, waits for them, and re-layouts: 14 us -> 9.26 us
    pallas_call x6 -> x4, Pallas kernels: 107 us -> 172 us  [the longest x1 117 us: run_start(): pl.pallas_call(partial(start_kernel, plane, seq, rows), in_specs=[vmem] *...]
    ppermute x9 -> x0, waiting for transfers between devices: 61.2 us -> none  [on_device(): hidden.append(lax.ppermute(hidden[-1], 'seq', upward))]
    ppermute x9 -> x0, starting transfers between devices: 42.1 us -> none  [on_device(): hidden.append(lax.ppermute(hidden[-1], 'seq', upward))]
    all_gather x4 -> x0, waiting for transfers between devices: 18.7 us -> none  [the longest x1 18.6 us: on_device(): whole_proj = lax.all_gather(proj_weight, 'dp', axis=0, tiled=True)]
    ppermute x9, waiting for transfers between devices: 40.6 us -> 54.6 us  [on_device(): arrived = lax.ppermute(moving, 'seq', downward)]
    pallas_call x1, Pallas kernels: 36.7 us -> 41.5 us  [run_sum(): pl.pallas_call(partial(sum_kernel, dp, seq), in_specs=[pl.BlockSpec(memor...]
  transfers between devices with their start and end apart: 22 -> 9, of which waited for: 13 -> 6; matrix products, arithmetic and copies ran while one was open for 5% -> 3% of each run, Pallas kernels for 40% -> 34%
where the time goes in v3:
time: 395 us; the launch traced here: 392 us
  Pallas kernels  296 us (75%)
  waiting for transfers between devices  54.6 us (14%)
  other arithmetic  18.4 us (5%)
  starting transfers between devices  12 us (3%)
  local copies, waits for them, and re-layouts  9.26 us (2%)
    pallas_call x1, Pallas kernels, run_start(): pl.pallas_call(partial(start_kernel, plane, seq, rows), in_specs=[vmem] *...  117 us
    pallas_call x3, Pallas kernels, run_backward(): pl.pallas_call(partial(backward_kernel, chunks), grid=(quads,), in_specs=...  82.6 us
    ppermute x9, waiting for transfers between devices, on_device(): arrived = lax.ppermute(moving, 'seq', downward)  54.6 us
    pallas_call x3, Pallas kernels, run_feed(): pl.pallas_call(feed_kernel, grid=(hidden_units // block,), in_specs=[pl.B...  54.4 us
    pallas_call x1, Pallas kernels, run_sum(): pl.pallas_call(partial(sum_kernel, dp, seq), in_specs=[pl.BlockSpec(memor...  41.5 us
    ppermute x9, starting transfers between devices, on_device(): arrived = lax.ppermute(moving, 'seq', downward)  12 us
  transfers between devices with their start and end apart: 9, of which 6 were waited for; matrix products, arithmetic and copies ran while one was open for 3% of the time, Pallas kernels for 34%

profile of v3, /device:TPU:0, one launch (start us, length us, event | category | flops | bytes accessed | tf_op | source)
XLA Modules:
  0.0 391.8 jit_solution(8594963432963259203)
XLA Ops:
  5.9 1.4 fusion.37
  7.3 117.4 %start.1 = (bf16[1024,3072]{1,0:T(8,128)(2,1)}, bf16[1024,1024]{1,0:T(8,128)(2,1)}, bf16[1024,4096]{1,0:T(8,128)(2,1)}, bf16[4096,1024]{1,0:T(8,128)(2,1)}, bf16...) custom-call(bf16[3,256,1024]{2,1,0:T(8,128)(2,1)} %x_ref.7, ...), custom_call_target="tpu_custom_call" | custom-call | tf_op jit(solution)/shard_map/start/pallas_call | solution.py:491
  124.7 18.3 %feed.3 = (bf16[256,1024]{1,0:T(8,128)(2,1)}, f32[256,1024]{1,0:T(8,128)}, bf16[256,1024]{1,0:T(8,128)(2,1)}) custom-call(bf16[3,256,1024]{2,1,0:T(8,128)(2,1)} %get-tuple-element.44.mix_ref.refs_4_, bf16[3,256,1024]{2,1,0:T(8,128)(2,1)} %x_ref.7, bf16[3,256,1024]{2,1,0:T(8,128)(2,1)} %gout_ref.5, bf16[1024,1024]{1,0:T(8,128)(2,1)} %get-tuple-element.45.wo_ref, ...), custom_call_target="tpu_custom_call" | custom-call | flops 9663676416 | bytes 23068672 | tf_op jit(solution)/shard_map/feed/pallas_call | solution.py:530
  143.1 27.6 %attend_backward.3 = (f32[256,1024]{1,0:T(8,128)}, bf16[256,1024]{1,0:T(8,128)(2,1)}, bf16[256,1024]{1,0:T(8,128)(2,1)}, bf16[256,1024]{1,0:T(8,128)(2,1)}, f32[8,1024]{1,0:T(8,128)}, /*index=5*/f32[8,1024]{1,0:T(8,128)}) custom-call(s32[1]{0:T(128)} %bitcast.14.place_ref, s32[1,256]{1,0:T(1,128)} %get-tuple-element.102.start_ref, ...), custom_call_target="tpu_custom_call" | custom-call | flops 7516192768 | bytes 20971520 | tf_op jit(solution)/shard_map/attend_backward/pallas_call | solution.py:570
  171.9 18.1 %feed.5 = (bf16[256,1024]{1,0:T(8,128)(2,1)}, f32[256,1024]{1,0:T(8,128)}, bf16[256,1024]{1,0:T(8,128)(2,1)}) custom-call(bf16[3,256,1024]{2,1,0:T(8,128)(2,1)} %get-tuple-element.44.mix_ref.refs_4_, bf16[3,256,1024]{2,1,0:T(8,128)(2,1)} %x_ref.7, bf16[3,256,1024]{2,1,0:T(8,128)(2,1)} %gout_ref.5, bf16[1024,1024]{1,0:T(8,128)(2,1)} %get-tuple-element.45.wo_ref, ...), custom_call_target="tpu_custom_call" | custom-call | flops 9663676416 | bytes 23068672 | tf_op jit(solution)/shard_map/feed/pallas_call | solution.py:530
  190.0 27.5 %attend_backward.5 = (f32[256,1024]{1,0:T(8,128)}, bf16[256,1024]{1,0:T(8,128)(2,1)}, bf16[256,1024]{1,0:T(8,128)(2,1)}, bf16[256,1024]{1,0:T(8,128)(2,1)}, f32[8,1024]{1,0:T(8,128)}, /*index=5*/f32[8,1024]{1,0:T(8,128)}) custom-call(s32[1]{0:T(128)} %bitcast.14.place_ref, s32[1,256]{1,0:T(1,128)} %get-tuple-element.101.start_ref, ...), custom_call_target="tpu_custom_call" | custom-call | flops 7516192768 | bytes 20971520 | tf_op jit(solution)/shard_map/attend_backward/pallas_call | solution.py:570
  218.8 18.0 %feed.4 = (bf16[256,1024]{1,0:T(8,128)(2,1)}, f32[256,1024]{1,0:T(8,128)}, bf16[256,1024]{1,0:T(8,128)(2,1)}) custom-call(bf16[3,256,1024]{2,1,0:T(8,128)(2,1)} %get-tuple-element.44.mix_ref.refs_4_, bf16[3,256,1024]{2,1,0:T(8,128)(2,1)} %x_ref.7, bf16[3,256,1024]{2,1,0:T(8,128)(2,1)} %gout_ref.5, bf16[1024,1024]{1,0:T(8,128)(2,1)} %get-tuple-element.45.wo_ref, ...), custom_call_target="tpu_custom_call" | custom-call | flops 9663676416 | bytes 23068672 | tf_op jit(solution)/shard_map/feed/pallas_call | solution.py:530
  236.8 27.6 %attend_backward.4 = (f32[256,1024]{1,0:T(8,128)}, bf16[256,1024]{1,0:T(8,128)(2,1)}, bf16[256,1024]{1,0:T(8,128)(2,1)}, bf16[256,1024]{1,0:T(8,128)(2,1)}, f32[8,1024]{1,0:T(8,128)}, /*index=5*/f32[8,1024]{1,0:T(8,128)}) custom-call(s32[1]{0:T(128)} %bitcast.14.place_ref, s32[1,256]{1,0:T(1,128)} %get-tuple-element.100.start_ref, ...), custom_call_target="tpu_custom_call" | custom-call | flops 7516192768 | bytes 20971520 | tf_op jit(solution)/shard_map/attend_backward/pallas_call | solution.py:570
  264.5 1.4 collective-permute-start.3
  267.5 41.5 %sum_all.1 = f32[8,16,128]{2,1,0:T(8,128)} custom-call(f32[8,16,128]{2,1,0:T(8,128)} %reshape.127.part_ref), custom_call_target="tpu_custom_call" | custom-call | tf_op jit(solution)/shard_map/sum_all/pallas_call | solution.py:658
  310.1 1.3 collective-permute-start.1
  312.7 1.3 collective-permute-start.7
  316.6 10.1 %collective-permute-done.1 = bf16[256,1024]{1,0:T(8,128)(2,1)S(1)} collective-permute-done((bf16[256,1024]{1,0:T(8,128)(2,1)S(1)}, bf16[256,1024]{1,0:T(8,128)(2,1)S(1)}, u32[]{:S(2)}, u32[]{:S(2)}) %collective-permute-start.1) | collective-permute-done | bytes 524320 | tf_op jit(solution)/shard_map/ppermute | solution.py:733
  327.7 1.5 collective-permute-start.2
  329.3 8.7 %collective-permute-done.7 = bf16[256,1024]{1,0:T(8,128)(2,1)S(1)} collective-permute-done((bf16[256,1024]{1,0:T(8,128)(2,1)S(1)}, bf16[256,1024]{1,0:T(8,128)(2,1)S(1)}, u32[]{:S(2)}, u32[]{:S(2)}) %collective-permute-start.7) | collective-permute-done | bytes 524320 | tf_op jit(solution)/shard_map/ppermute | solution.py:733
  340.2 9.0 %collective-permute-done.4 = bf16[256,1024]{1,0:T(8,128)(2,1)S(1)} collective-permute-done((bf16[256,1024]{1,0:T(8,128)(2,1)S(1)}, bf16[256,1024]{1,0:T(8,128)(2,1)S(1)}, u32[]{:S(2)}, u32[]{:S(2)}) %collective-permute-start.4) | collective-permute-done | bytes 524320 | tf_op jit(solution)/shard_map/ppermute | solution.py:733
  351.6 1.3 pad_maximum_fusion.1
  355.4 5.1 %collective-permute-done.2 = bf16[256,1024]{1,0:T(8,128)(2,1)S(1)} collective-permute-done((bf16[256,1024]{1,0:T(8,128)(2,1)}, bf16[256,1024]{1,0:T(8,128)(2,1)S(1)}, u32[]{:S(2)}, u32[]{:S(2)}) %collective-permute-start.2) | collective-permute-done | bytes 524320 | tf_op jit(solution)/shard_map/ppermute | solution.py:733
  360.4 11.3 %collective-permute-done.8 = bf16[256,1024]{1,0:T(8,128)(2,1)} collective-permute-done((bf16[256,1024]{1,0:T(8,128)(2,1)}, bf16[256,1024]{1,0:T(8,128)(2,1)}, u32[]{:S(2)}, u32[]{:S(2)}) %collective-permute-start.8) | collective-permute-done | bytes 524320 | tf_op jit(solution)/shard_map/ppermute | solution.py:733
  371.8 10.4 %collective-permute-done.5 = bf16[256,1024]{1,0:T(8,128)(2,1)} collective-permute-done((bf16[256,1024]{1,0:T(8,128)(2,1)}, bf16[256,1024]{1,0:T(8,128)(2,1)}, u32[]{:S(2)}, u32[]{:S(2)}) %collective-permute-start.5) | collective-permute-done | bytes 524320 | tf_op jit(solution)/shard_map/ppermute | solution.py:733
  382.2 3.1 fusion.33
  385.4 1.6 fusion.31
  387.4 1.8 fusion.9
  389.3 2.1 pad_maximum_fusion
  (93 shorter events, 22.6 us)
Async XLA Ops:
  0.6 4.4 %copy-start.23 = (bf16[4,1024]{1,0:T(4,128)(2,1)S(1)}, bf16[4,1024]{1,0:T(4,128)(2,1)}, u32[]{:S(2)}) copy-start(bf16[4,1024]{1,0:T(4,128)(2,1)} %param.30) | copy-start | bytes 24580
  0.6 4.4 %copy-start.24 = (bf16[4,1024]{1,0:T(4,128)(2,1)S(1)}, bf16[4,1024]{1,0:T(4,128)(2,1)}, u32[]{:S(2)}) copy-start(bf16[4,1024]{1,0:T(4,128)(2,1)} %param.28) | copy-start | bytes 24580
  170.6 139.2 %collective-permute-start = (bf16[256,1024]{1,0:T(8,128)(2,1)}, bf16[256,1024]{1,0:T(8,128)(2,1)S(1)}, u32[]{:S(2)}, u32[]{:S(2)}) collective-permute-start(bf16[256,1024]{1,0:T(8,128)(2,1)} %get-tuple-element.63), channel_id=1, source_target_pairs={{1,0},{2,1},{3,2},{5,4},{6,5},{7,6},{9,8},{10,9},{11,10},{13,12},{... | collective-permute-start | bytes 1572872 | tf_op jit(solution)/shard_map/ppermute | solution.py:733
  217.5 93.9 %collective-permute-start.6 = (bf16[256,1024]{1,0:T(8,128)(2,1)}, bf16[256,1024]{1,0:T(8,128)(2,1)}, u32[]{:S(2)}, u32[]{:S(2)}) collective-permute-start(bf16[256,1024]{1,0:T(8,128)(2,1)} %get-tuple-element.75), channel_id=1, source_target_pairs={{1,0},{2,1},{3,2},{5,4},{6,5},{7,6},{9,8},{10,9},{11,10},{13,12},{... | collective-permute-start | bytes 1572872 | tf_op jit(solution)/shard_map/ppermute | solution.py:733
  236.8 29.1 %copy-start = (bf16[3,256,1024]{2,1,0:T(8,128)(2,1)S(1)}, bf16[3,256,1024]{2,1,0:T(8,128)(2,1)}, u32[]{:S(2)}) copy-start(bf16[3,256,1024]{2,1,0:T(8,128)(2,1)} %x_ref.7) | copy-start | bytes 4718596
  264.5 49.5 %collective-permute-start.3 = (bf16[256,1024]{1,0:T(8,128)(2,1)}, bf16[256,1024]{1,0:T(8,128)(2,1)}, u32[]{:S(2)}, u32[]{:S(2)}) collective-permute-start(bf16[256,1024]{1,0:T(8,128)(2,1)} %get-tuple-element.69), channel_id=1, source_target_pairs={{1,0},{2,1},{3,2},{5,4},{6,5},{7,6},{9,8},{10,9},{11,10},{13,12},{... | collective-permute-start | bytes 1572872 | tf_op jit(solution)/shard_map/ppermute | solution.py:733
  266.2 43.7 %copy-start.10 = (bf16[256,1024]{1,0:T(8,128)(2,1)S(1)}, bf16[256,1024]{1,0:T(8,128)(2,1)}, u32[]{:S(2)}) copy-start(bf16[256,1024]{1,0:T(8,128)(2,1)} %get-tuple-element.62) | copy-start | bytes 1572868
  266.8 44.6 %copy-start.11 = (bf16[256,1024]{1,0:T(8,128)(2,1)S(1)}, bf16[256,1024]{1,0:T(8,128)(2,1)}, u32[]{:S(2)}) copy-start(bf16[256,1024]{1,0:T(8,128)(2,1)} %get-tuple-element.74) | copy-start | bytes 1572868
  309.9 4.1 %copy-start.12 = (bf16[256,1024]{1,0:T(8,128)(2,1)S(1)}, bf16[256,1024]{1,0:T(8,128)(2,1)}, u32[]{:S(2)}) copy-start(bf16[256,1024]{1,0:T(8,128)(2,1)} %get-tuple-element.68) | copy-start | bytes 1572868
  310.1 16.7 %collective-permute-start.1 = (bf16[256,1024]{1,0:T(8,128)(2,1)S(1)}, bf16[256,1024]{1,0:T(8,128)(2,1)S(1)}, u32[]{:S(2)}, u32[]{:S(2)}) collective-permute-start(bf16[256,1024]{1,0:T(8,128)(2,1)S(1)} %add_convert_fusion.5), channel_id=1, source_target_pairs={{1,0},{2,1},{3,2},{5,4},{6,5},{7,6},{9,8},{10,9},{11,10},{13,12},{... | collective-permute-start | bytes 1572872 | tf_op jit(solution)/shard_map/ppermute | solution.py:733
  311.4 15.4 %copy-start.7 = (bf16[256,1024]{1,0:T(8,128)(2,1)S(1)}, bf16[256,1024]{1,0:T(8,128)(2,1)}, u32[]{:S(2)}) copy-start(bf16[256,1024]{1,0:T(8,128)(2,1)} %get-tuple-element.61) | copy-start | bytes 1572868
  312.7 25.3 %collective-permute-start.7 = (bf16[256,1024]{1,0:T(8,128)(2,1)S(1)}, bf16[256,1024]{1,0:T(8,128)(2,1)S(1)}, u32[]{:S(2)}, u32[]{:S(2)}) collective-permute-start(bf16[256,1024]{1,0:T(8,128)(2,1)S(1)} %add_convert_fusion.1), channel_id=1, source_target_pairs={{1,0},{2,1},{3,2},{5,4},{6,5},{7,6},{9,8},{10,9},{11,10},{13,12},{... | collective-permute-start | bytes 1572872 | tf_op jit(solution)/shard_map/ppermute | solution.py:733
  314.0 24.0 %copy-start.8 = (bf16[256,1024]{1,0:T(8,128)(2,1)S(1)}, bf16[256,1024]{1,0:T(8,128)(2,1)}, u32[]{:S(2)}) copy-start(bf16[256,1024]{1,0:T(8,128)(2,1)} %get-tuple-element.73) | copy-start | bytes 1572868
  315.3 33.9 %collective-permute-start.4 = (bf16[256,1024]{1,0:T(8,128)(2,1)S(1)}, bf16[256,1024]{1,0:T(8,128)(2,1)S(1)}, u32[]{:S(2)}, u32[]{:S(2)}) collective-permute-start(bf16[256,1024]{1,0:T(8,128)(2,1)S(1)} %add_convert_fusion.3), channel_id=1, source_target_pairs={{1,0},{2,1},{3,2},{5,4},{6,5},{7,6},{9,8},{10,9},{11,10},{13,12},{... | collective-permute-start | bytes 1572872 | tf_op jit(solution)/shard_map/ppermute | solution.py:733
  326.7 22.5 %copy-start.9 = (bf16[256,1024]{1,0:T(8,128)(2,1)S(1)}, bf16[256,1024]{1,0:T(8,128)(2,1)}, u32[]{:S(2)}) copy-start(bf16[256,1024]{1,0:T(8,128)(2,1)} %get-tuple-element.67) | copy-start | bytes 1572868
  327.7 32.7 %collective-permute-start.2 = (bf16[256,1024]{1,0:T(8,128)(2,1)}, bf16[256,1024]{1,0:T(8,128)(2,1)S(1)}, u32[]{:S(2)}, u32[]{:S(2)}) collective-permute-start(bf16[256,1024]{1,0:T(8,128)(2,1)} %add_convert_fusion.4), channel_id=1, source_target_pairs={{1,0},{2,1},{3,2},{5,4},{6,5},{7,6},{9,8},{10,9},{11,10},{13,12},{... | collective-permute-start | bytes 1572872 | tf_op jit(solution)/shard_map/ppermute | solution.py:733
  338.0 13.6 %copy-start.13 = (bf16[256,1024]{1,0:T(8,128)(2,1)S(1)}, bf16[256,1024]{1,0:T(8,128)(2,1)}, u32[]{:S(2)}) copy-start(bf16[256,1024]{1,0:T(8,128)(2,1)} %get-tuple-element.48) | copy-start | bytes 1572868
  338.0 13.6 %copy-start.14 = (bf16[256,1024]{1,0:T(8,128)(2,1)S(1)}, bf16[256,1024]{1,0:T(8,128)(2,1)}, u32[]{:S(2)}) copy-start(bf16[256,1024]{1,0:T(8,128)(2,1)} %get-tuple-element.50) | copy-start | bytes 1572868
  338.0 13.6 %copy-start.15 = (bf16[256,1024]{1,0:T(8,128)(2,1)S(1)}, bf16[256,1024]{1,0:T(8,128)(2,1)}, u32[]{:S(2)}) copy-start(bf16[256,1024]{1,0:T(8,128)(2,1)} %get-tuple-element.49) | copy-start | bytes 1572868
  339.0 32.8 %collective-permute-start.8 = (bf16[256,1024]{1,0:T(8,128)(2,1)}, bf16[256,1024]{1,0:T(8,128)(2,1)}, u32[]{:S(2)}, u32[]{:S(2)}) collective-permute-start(bf16[256,1024]{1,0:T(8,128)(2,1)} %add_convert_fusion), channel_id=1, source_target_pairs={{1,0},{2,1},{3,2},{5,4},{6,5},{7,6},{9,8},{10,9},{11,10},{13,12},{... | collective-permute-start | bytes 1572872 | tf_op jit(solution)/shard_map/ppermute | solution.py:733
  350.2 31.9 %collective-permute-start.5 = (bf16[256,1024]{1,0:T(8,128)(2,1)}, bf16[256,1024]{1,0:T(8,128)(2,1)}, u32[]{:S(2)}, u32[]{:S(2)}) collective-permute-start(bf16[256,1024]{1,0:T(8,128)(2,1)} %add_convert_fusion.2), channel_id=1, source_target_pairs={{1,0},{2,1},{3,2},{5,4},{6,5},{7,6},{9,8},{10,9},{11,10},{13,12},{... | collective-permute-start | bytes 1572872 | tf_op jit(solution)/shard_map/ppermute | solution.py:733
  351.6 30.6 %copy-start.1 = (f32[256,1024]{1,0:T(8,128)S(1)}, f32[256,1024]{1,0:T(8,128)}, u32[]{:S(2)}) copy-start(f32[256,1024]{1,0:T(8,128)} %get-tuple-element.60) | copy-start | bytes 3145732
  351.6 30.6 %copy-start.16 = (f32[1024]{0:T(1024)S(1)}, f32[1024]{0:T(1024)}, u32[]{:S(2)}) copy-start(f32[1024]{0:T(1024)} %param.22) | copy-start | bytes 12292
  382.2 3.2 copy-start.6
  (10 other events, 22.9 us)

commit v4 on v3

--- a/solution.py
+++ b/solution.py
@@ -20,6 +20,7 @@
 F32 = jnp.float32
 BF16 = jnp.bfloat16
 VMEM_BYTES = 56 * 1024 * 1024
+FINISH_BYTES = 63 * 1024 * 1024
 
 
 def dot_nn(left, right):
@@ -337,139 +338,356 @@
                 hop(row, s).wait_send()
 
 
-def feed_kernel(
-    mix_ref, x_ref, gout_ref, wo_ref, out_bias, gain, shift, proj_bias, fc_ref, fc_bias, proj_ref,
-    out_ref, gmid_ref, gmix_ref, middle_ref, hidden_ref, acc_ref, grad_ref,
+def finish_kernel(
+    dp, seq, rows, block,
+    x_ref, start_ref, lse_ref, down_ref, up_ref, gain1, out_bias, gain2, shift2, proj_bias, fc_bias,
+    gout_in, w_in, wo_in, fc_in, proj_in, hidden_in, q_in, k_in, v_in, mix_in,
+    out_out, grad_out, sum_out,
+    w_held, wo_held, fc_held, proj_held, hidden, q_held, k_held, v_held, mix_held, gout_held,
+    gmix_ref, middle_ref, h2_ref, acc_ref, back_ref, gmid_ref, own_ref, mask_ref, delta_ref, dq_ref, dkv_ref,
+    leaving, arriving, stage_ref, up_sum, reduce_sum, part_ref, plane_ref, line_ref,
+    weight_sems, row_sems, store_sems, leave_sems, arrive_sems, sum_send, sum_recv,
 ):
-    step = pl.program_id(0)
-
-    @pl.when(step == 0)
-    def _():
-        middle = x_ref[...].astype(F32) + dot_nn(mix_ref[...], wo_ref[...]) + out_bias[...]
+    tokens, width = x_ref.shape[1], x_ref.shape[2]
+    quads = width // QUAD
+    steps = fc_held.shape[1] // block
+    mesh_type = pl.DeviceIdType.MESH
+    me, place = lax.axis_index("dp"), lax.axis_index("seq")
+    top = seq - 1
+
+    def peer(delta):
+        return lax.rem(me + delta, dp), place
+
+    def line_peer(delta):
+        return me, lax.rem(place + delta, seq)
+
+    barrier = pltpu.get_barrier_semaphore()
+    for delta in range(1, dp):
+        pl.semaphore_signal(barrier, inc=1, device_id=peer(delta), device_id_type=mesh_type)
+    for delta in range(1, seq):
+        pl.semaphore_signal(barrier, inc=1, device_id=line_peer(delta), device_id_type=mesh_type)
+
+    def feed_loads(row):
+        return [
+            pltpu.make_async_copy(mix_in.at[row], mix_held, row_sems.at[0]),
+            pltpu.make_async_copy(gout_in.at[row], gout_held, row_sems.at[1]),
+        ]
+
+    def attend_loads(row):
+        return [
+            pltpu.make_async_copy(q_in.at[row], q_held, row_sems.at[2]),
+            pltpu.make_async_copy(k_in.at[row], k_held, row_sems.at[3]),
+            pltpu.make_async_copy(v_in.at[row], v_held, row_sems.at[4]),
+            pltpu.make_async_copy(hidden_in.at[row], hidden, row_sems.at[5]),
+        ]
+
+    def chunk_loads(step):
+        part = pl.ds(pl.multiple_of(step * block, block), block)
+        return [
+            pltpu.make_async_copy(fc_in.at[:, part], fc_held.at[:, part], weight_sems.at[0, step]),
+            pltpu.make_async_copy(proj_in.at[part, :], proj_held.at[part, :], weight_sems.at[1, step]),
+        ]
+
+    wo_load = pltpu.make_async_copy(wo_in, wo_held, weight_sems.at[2, 0])
+    w_load = pltpu.make_async_copy(w_in, w_held, weight_sems.at[2, 1])
+    for copy in feed_loads(0):
+        copy.start()
+    wo_load.start()
+    for step in range(steps):
+        for copy in chunk_loads(step):
+            copy.start()
+    for copy in attend_loads(0):
+        copy.start()
+    w_load.start()
+    up_sum[...] = jnp.zeros_like(up_sum)
+    reduce_sum[...] = jnp.zeros_like(reduce_sum)
+    pl.semaphore_wait(barrier, dp + seq - 2)
+    wo_load.wait()
+
+    def out_store(row):
+        return pltpu.make_async_copy(stage_ref, out_out.at[row], store_sems.at[0])
+
+    def grad_store(row):
+        slot = lax.rem(row, 2)
+        return pltpu.make_async_copy(gmid_ref.at[slot], grad_out.at[row], store_sems.at[1 + slot])
+
+    def leave(row, s):
+        return pltpu.make_async_remote_copy(
+            src_ref=leaving.at[s - 1], dst_ref=arriving.at[row, s - 1],
+            send_sem=leave_sems.at[s - 1], recv_sem=arrive_sems.at[row, s - 1],
+            device_id=(me, place - 1), device_id_type=mesh_type,
+        )
+
+    def chain(row, k):
+        s = seq - 1 - k
+
+        @pl.when((place < top) & (place >= s))
+        def _():
+            leave(row, s + 1).wait_recv()
+            arrived = arriving[row, s].astype(F32)
+            if s > 0:
+                leaving[s - 1] = (leaving[s - 1].astype(F32) + arrived).astype(BF16)
+                leave(row, s).start()
+            else:
+                own_ref[...] = own_ref[...] + arrived
+
+        if s == 0:
+            slot = lax.rem(row, 2)
+            normed, inverse = norm_parts(x_ref[row].astype(F32))
+            gmid_ref[slot] = gmid_ref[slot] + norm_backward(own_ref[...], normed, inverse, gain1[...])
+            grad_store(row).start()
+
+    def feed(row):
+        for copy in feed_loads(row):
+            copy.wait()
+        middle = x_ref[row].astype(F32) + dot_nn(mix_held[...], wo_held[...]) + out_bias[...]
         middle_ref[...] = middle
         normed, _ = norm_parts(middle)
-        hidden_ref[...] = (normed * gain[...] + shift[...]).astype(BF16)
-
-    before = dot_nn(hidden_ref[...], fc_ref[...]) + fc_bias[...]
-    square = before * before
-    bend = jnp.tanh(GELU_A * before * (1.0 + GELU_B * square))
-    half = 0.5 * (1.0 + bend)
-    slope = half + 0.5 * before * (1.0 - bend * bend) * (GELU_A * (1.0 + 3.0 * GELU_B * square))
-    act = (before * half).astype(BF16)
-    g_before = (dot_nt(gout_ref[...], proj_ref[...]) * slope).astype(BF16)
-    fed = dot_nn(act, proj_ref[...])
-    back = dot_nt(g_before, fc_ref[...])
-
-    @pl.when(step == 0)
-    def _():
-        acc_ref[...] = fed
-        grad_ref[...] = back
-
-    @pl.when(step > 0)
-    def _():
-        acc_ref[...] += fed
-        grad_ref[...] += back
-
-    @pl.when(step == pl.num_programs(0) - 1)
-    def _():
+        h2_ref[...] = (normed * gain2[...] + shift2[...]).astype(BF16)
+        acc_ref[...] = jnp.zeros_like(acc_ref)
+        back_ref[...] = jnp.zeros_like(back_ref)
+
+        @pl.loop(0, steps)
+        def _(step):
+            @pl.when(row == 0)
+            def _():
+                for copy in chunk_loads(step):
+                    copy.wait()
+
+            part = pl.ds(pl.multiple_of(step * block, block), block)
+            before = dot_nn(h2_ref[...], fc_held[:, part]) + fc_bias[:, part]
+            square = before * before
+            bend = jnp.tanh(GELU_A * before * (1.0 + GELU_B * square))
+            half = 0.5 * (1.0 + bend)
+            slope = half + 0.5 * before * (1.0 - bend * bend) * (GELU_A * (1.0 + 3.0 * GELU_B * square))
+            act = (before * half).astype(BF16)
+            g_before = (dot_nt(gout_held[...], proj_held[part, :]) * slope).astype(BF16)
+            acc_ref[...] += dot_nn(act, proj_held[part, :])
+            back_ref[...] += dot_nt(g_before, fc_held[:, part])
+
+        slot = lax.rem(row, 2)
+
+        @pl.when(row >= 1)
+        def _():
+            out_store(row - 1).wait()
+
+        @pl.when(row >= 2)
+        def _():
+            grad_store(row - 2).wait()
+
         middle = middle_ref[...]
-        out_ref[...] = (middle + acc_ref[...] + proj_bias[...]).astype(BF16)
+        stage_ref[...] = (middle + acc_ref[...] + proj_bias[...]).astype(BF16)
+        out_store(row).start()
         normed, inverse = norm_parts(middle)
-        g_middle = gout_ref[...].astype(F32) + norm_backward(grad_ref[...], normed, inverse, gain[...])
-        gmid_ref[...] = g_middle
-        gmix_ref[...] = dot_nt(g_middle.astype(BF16), wo_ref[...]).astype(BF16)
-
-
-def backward_kernel(chunks, place_ref, start_ref, *refs):
-    hidden_ref, q_ref, k_ref, v_ref, mix_ref, g_ref, lse_ref, down_ref, up_ref, w_ref = refs[:10]
-    grads = refs[10 : chunks + 10]
-    reduce_out, up_out, mask_ref, dq_ref, dkv_ref, w_held, w_sem = refs[chunks + 10 :]
-    hidden = [hidden_ref.at[s] for s in range(chunks)]
-    tokens = hidden[0].shape[0]
-    width = hidden[0].shape[1]
-    quad = pl.program_id(0)
-
-    @pl.when(quad == 0)
-    def _():
-        pltpu.make_async_copy(w_ref, w_held, w_sem).start()
-        place = place_ref[0]
+        g_middle = gout_held[...].astype(F32) + norm_backward(back_ref[...], normed, inverse, gain2[...])
+        gmid_ref[slot] = g_middle
+        gmix_ref[...] = dot_nt(g_middle.astype(BF16), wo_held[...]).astype(BF16)
+        for pair in range(width // PAIR):
+            span = slice(pair * PAIR, (pair + 1) * PAIR)
+            product = (gmix_ref[:, span].astype(F32) * mix_held[:, span].astype(F32)).T
+            for half in range(2):
+                head = pair * 2 + half
+                delta_ref[head // 4, head % 4 : head % 4 + 1, :] = jnp.sum(
+                    product[half * HEAD : (half + 1) * HEAD], axis=0, keepdims=True
+                )
+
+        @pl.when(row < rows - 1)
+        def _():
+            for copy in feed_loads(row + 1):
+                copy.start()
+
+    low = head_lanes(tokens, BF16)
+    rank_row = lax.broadcasted_iota(jnp.int32, (8, width), 0) < 4
+
+    def attend_chunk(row, s):
         query = place * tokens + lax.broadcasted_iota(jnp.int32, (tokens, tokens), 1)
-        start = start_ref[...]
-        for s in range(chunks):
-            key = (place - s) * tokens + lax.broadcasted_iota(jnp.int32, (tokens, tokens), 0)
-            allowed = key >= start
-            if s == 0:
-                allowed = allowed & (key <= query)
-            mask_ref[s * tokens : (s + 1) * tokens, :] = jnp.where(allowed, 0.0, MASKED)
-
-    low = head_lanes(tokens, BF16)
-    for pair in range(QUAD // PAIR):
-        span = slice(pair * PAIR, (pair + 1) * PAIR)
-        q_pair = q_ref[:, span]
-        g_pair = g_ref[:, span]
-        product = (g_pair.astype(F32) * mix_ref[:, span].astype(F32)).T
-        heads = []
-        for half in range(2):
-            own = low if half == 0 else jnp.logical_not(low)
-            inner = jnp.sum(product[half * HEAD : (half + 1) * HEAD], axis=0, keepdims=True)
-            row = pair * 2 + half
-            heads.append(
-                (
-                    jnp.where(own, q_pair, jnp.zeros_like(q_pair)),
-                    jnp.where(own, g_pair, jnp.zeros_like(g_pair)),
-                    inner,
-                    lse_ref[0, row : row + 1, :],
-                )
-            )
-        dq_parts = [jnp.zeros((HEAD, tokens), F32)] * 2
-        for s in range(chunks):
-            rows = slice(s * tokens, (s + 1) * tokens)
-            k_pair = k_ref[rows, span]
-            v_pair = v_ref[rows, span]
-            k_turned = k_pair.astype(F32).T.astype(BF16)
-            dk = None
-            for half, (q_head, g_head, inner, lse) in enumerate(heads):
-                score = dot_nt(k_pair, q_head) + mask_ref[rows, :]
-                prob = jnp.exp(score - lse)
-                g_score = (prob * (dot_nt(v_pair, g_head) - inner)).astype(BF16)
-                part_v = dot_nn(prob.astype(BF16), g_head)
-                part_k = dot_nn(g_score, q_head)
-                dk = part_k if dk is None else dk + part_k
-                dv = part_v if half == 0 else dv + part_v
-                dq_parts[half] = dq_parts[half] + dot_nn(k_turned[half * HEAD : (half + 1) * HEAD], g_score)
-            columns = pl.ds(pl.multiple_of(quad * QUAD, QUAD) + pair * PAIR, PAIR)
-            dkv_ref[rows, columns] = dk.astype(BF16)
-            columns = pl.ds(pl.multiple_of(quad * QUAD, QUAD) + (width + pair * PAIR), PAIR)
-            dkv_ref[rows, columns] = dv.astype(BF16)
-        dq = jnp.concatenate(dq_parts, axis=0).T * (HEAD**-0.5)
-        dq_ref[:, pl.ds(pl.multiple_of(quad * QUAD, QUAD) + pair * PAIR, PAIR)] = dq.astype(BF16)
-
-    @pl.when(quad == pl.num_programs(0) - 1)
-    def _():
-        pltpu.make_async_copy(w_ref, w_held, w_sem).wait()
-        rank_row = lax.broadcasted_iota(jnp.int32, (8, width), 0) < 4
-        up_grad = jnp.zeros((8, width), F32)
-        reduce_grad = jnp.zeros((8, width), F32)
-        for s in range(chunks - 1, -1, -1):
-            rows = slice(s * tokens, (s + 1) * tokens)
-            dkv = dkv_ref[rows, :]
-            grad = dot_nt(dkv, w_held[:, width:])
-            if s == 0:
-                grad = grad + dot_nt(dq_ref[...], w_held[:, :width])
-            grads[s][...] = grad.astype(grads[s].dtype)
-            dv = dkv_ref[rows, width:]
-            down = down_ref[:, rows]
-            up_grad = up_grad + dot_nn(down, dv)
-            g_down = dot_nt(dv, up_ref[...]).T[:8].astype(BF16)
-            reduce_grad = reduce_grad + dot_nn(g_down, hidden[s][...])
-        dq = dq_ref[...]
-        g_down = dot_nt(dq, up_ref[...]).T[:8].astype(BF16)
-        up_out[...] = jnp.where(rank_row, dot_nn(down_ref[:, :tokens], dq), up_grad)
-        reduce_out[...] = jnp.where(rank_row, dot_nn(g_down, hidden[0][...]), reduce_grad)
-
-
-def whole(shape):
-    return pl.BlockSpec(shape, lambda i: (0,) * len(shape))
+        key = (place - s) * tokens + lax.broadcasted_iota(jnp.int32, (tokens, tokens), 0)
+        allowed = key >= start_ref[row]
+        if s == 0:
+            allowed = allowed & (key <= query)
+        mask_ref[...] = jnp.where(allowed, 0.0, MASKED)
+        rows_s = slice(s * tokens, (s + 1) * tokens)
+
+        @pl.loop(0, quads)
+        def _(quad):
+            base = pl.multiple_of(quad * QUAD, QUAD)
+            for pair in range(QUAD // PAIR):
+                span = pl.ds(base + pair * PAIR, PAIR)
+                q_pair, g_pair = q_held[:, span], gmix_ref[:, span]
+                k_pair, v_pair = k_held[rows_s, span], v_held[rows_s, span]
+                k_turned = k_pair.astype(F32).T.astype(BF16)
+                dk, dv = None, None
+                for half in range(2):
+                    own = low if half == 0 else jnp.logical_not(low)
+                    q_head = jnp.where(own, q_pair, jnp.zeros_like(q_pair))
+                    g_head = jnp.where(own, g_pair, jnp.zeros_like(g_pair))
+                    head = pair * 2 + half
+                    lse = lse_ref[row, quad, head : head + 1, :]
+                    inner = delta_ref[quad, head : head + 1, :]
+                    prob = jnp.exp(dot_nt(k_pair, q_head) + mask_ref[...] - lse)
+                    g_score = (prob * (dot_nt(v_pair, g_head) - inner)).astype(BF16)
+                    part_v = dot_nn(prob.astype(BF16), g_head)
+                    part_k = dot_nn(g_score, q_head)
+                    dv = part_v if dv is None else dv + part_v
+                    dk = part_k if dk is None else dk + part_k
+                    lines = pl.ds(base + (pair * PAIR + half * HEAD), HEAD)
+                    dq_ref[lines, :] += dot_nn(k_turned[half * HEAD : (half + 1) * HEAD], g_score)
+                dkv_ref[:, span] = dk.astype(BF16)
+                dkv_ref[:, pl.ds(base + (width + pair * PAIR), PAIR)] = dv.astype(BF16)
+
+        grad = dot_nt(dkv_ref[...], w_held[:, width:])
+        dv = dkv_ref[:, width:]
+        up_grad = dot_nn(down_ref[row, :, rows_s], dv)
+        g_down = dot_nt(dv, up_ref[...]).T[:8].astype(BF16)
+        reduce_grad = dot_nn(g_down, hidden[s])
+        up_sum[...] += jnp.where(rank_row, 0.0, up_grad)
+        reduce_sum[...] += jnp.where(rank_row, 0.0, reduce_grad)
+        if s > 0:
+            @pl.when(row > 0)
+            def _():
+                leave(row - 1, s).wait_send()
+
+            leaving[s - 1] = grad.astype(BF16)
+
+            @pl.when(place == top)
+            def _():
+                leave(row, s).start()
+        else:
+            dq = (dq_ref[...].T * (HEAD**-0.5)).astype(BF16)
+            own_ref[...] = grad + dot_nt(dq, w_held[:, :width])
+            up_grad = dot_nn(down_ref[row, :, rows_s], dq)
+            g_down = dot_nt(dq, up_ref[...]).T[:8].astype(BF16)
+            reduce_grad = dot_nn(g_down, hidden[s])
+            up_sum[...] += jnp.where(rank_row, up_grad, 0.0)
+            reduce_sum[...] += jnp.where(rank_row, reduce_grad, 0.0)
+
+    @pl.loop(0, rows)
+    def _(row):
+        feed(row)
+
+        @pl.when(row > 0)
+        def _():
+            chain(row - 1, 2)
+
+        for copy in attend_loads(row):
+            copy.wait()
+
+        @pl.when(row == 0)
+        def _():
+            w_load.wait()
+
+        dq_ref[...] = jnp.zeros_like(dq_ref)
+        for s in range(seq - 1, -1, -1):
+            if s < seq - 3:
+                @pl.when(row > 0)
+                def _():
+                    chain(row - 1, seq - 1 - s)
+
+            @pl.when(place >= s)
+            def _():
+                attend_chunk(row, s)
+
+            if s == 1:
+                chain(row, 1)
+
+        @pl.when(row < rows - 1)
+        def _():
+            for copy in attend_loads(row + 1):
+                copy.start()
+
+    def send(source, target, slot, device):
+        copy = pltpu.make_async_remote_copy(
+            src_ref=source, dst_ref=target, send_sem=sum_send.at[slot], recv_sem=sum_recv.at[slot],
+            device_id=device, device_id_type=mesh_type,
+        )
+        copy.start()
+        return copy
+
+    pieces, piece = part_ref.shape[0], part_ref.shape[1]
+    lanes = width // PAIR
+    part_ref[...] = jnp.zeros_like(part_ref)
+    for half, total in enumerate((reduce_sum[...] * ADAPTER_SCALE, up_sum[...])):
+        for lane in range(lanes):
+            line = (half * lanes + lane) * 8
+            part_ref[line // piece, line % piece : line % piece + 8, :] = total[:, lane * PAIR : (lane + 1) * PAIR]
+    copies = [send(part_ref.at[lax.rem(me + delta, dp)], plane_ref.at[delta], delta, peer(delta)) for delta in range(1, dp)]
+    last = rows - 1
+    chain(last, 2)
+    total = part_ref[me]
+    for delta in range(1, dp):
+        copies[delta - 1].wait()
+        total = total + plane_ref[delta]
+    line_ref[place] = total
+    copies = [send(line_ref.at[place], line_ref.at[place], dp + delta, line_peer(delta)) for delta in range(1, seq)]
+    for copy in copies:
+        copy.wait()
+    total = line_ref[0]
+    for index in range(1, seq):
+        total = total + line_ref[index]
+    sum_out[me] = total
+    copies = [send(sum_out.at[me], sum_out.at[me], dp + seq + delta, peer(delta)) for delta in range(1, dp)]
+    for k in range(3, seq):
+        chain(last, k)
+    for copy in copies:
+        copy.wait()
+    for s in range(1, seq):
+        @pl.when(place >= s)
+        def _():
+            leave(last, s).wait_send()
+    out_store(last).wait()
+    for row in range(max(0, rows - 2), rows):
+        grad_store(row).wait()
+
+
+def run_finish(dp, seq, x, starts, lse, down, up_wide, vectors, gout, w, wo, fc, proj, hidden, q, k, v, mixed):
+    rows, tokens, width = x.shape
+    length = seq * tokens
+    hidden_units = fc.shape[1]
+    block = 1024
+    quads = width // QUAD
+    piece = max(8, 16 * width // (PAIR * dp))
+    anywhere = pl.BlockSpec(memory_space=pl.ANY)
+    vmem = pl.BlockSpec(memory_space=pltpu.VMEM)
+    slots = 2 * dp + seq
+
+    def held(*dims, dtype=BF16):
+        return pltpu.VMEM(dims, dtype)
+
+    out, grad, total = pl.pallas_call(
+        partial(finish_kernel, dp, seq, rows, block),
+        in_specs=[vmem] * 11 + [anywhere] * 10,
+        out_specs=[anywhere, anywhere, vmem],
+        out_shape=[
+            jax.ShapeDtypeStruct((rows, tokens, width), BF16),
+            jax.ShapeDtypeStruct((rows, tokens, width), F32),
+            jax.ShapeDtypeStruct((dp, piece, PAIR), F32),
+        ],
+        scratch_shapes=[
+            held(width, 3 * width), held(width, width), held(width, hidden_units), held(hidden_units, width),
+            held(seq, tokens, width), held(tokens, width), held(length, width), held(length, width),
+            held(tokens, width), held(tokens, width),
+            held(tokens, width), held(tokens, width, dtype=F32), held(tokens, width),
+            held(tokens, width, dtype=F32), held(tokens, width, dtype=F32), held(2, tokens, width, dtype=F32),
+            held(tokens, width, dtype=F32), held(tokens, tokens, dtype=F32), held(quads, 8, tokens, dtype=F32),
+            held(width, tokens, dtype=F32), held(tokens, 2 * width),
+            held(seq - 1, tokens, width), held(rows, seq - 1, tokens, width), held(tokens, width),
+            held(8, width, dtype=F32), held(8, width, dtype=F32),
+            held(dp, piece, PAIR, dtype=F32), held(dp, piece, PAIR, dtype=F32), held(seq, piece, PAIR, dtype=F32),
+            pltpu.SemaphoreType.DMA((3, max(2, hidden_units // block))),
+            pltpu.SemaphoreType.DMA((6,)),
+            pltpu.SemaphoreType.DMA((3,)),
+            pltpu.SemaphoreType.DMA((seq - 1,)),
+            pltpu.SemaphoreType.DMA((rows, seq - 1)),
+            pltpu.SemaphoreType.DMA((slots,)),
+            pltpu.SemaphoreType.DMA((slots,)),
+        ],
+        compiler_params=pltpu.CompilerParams(
+            vmem_limit_bytes=FINISH_BYTES, collective_id=1, has_side_effects=True
+        ),
+        name="finish",
+    )(x, starts, lse, down, up_wide, *vectors, gout, w, wo, fc, proj, hidden, q, k, v, mixed)
+    flat = total.reshape(-1, PAIR)[: 16 * width // PAIR]
+    return out, grad, flat.reshape(2, width // PAIR, 8, PAIR).transpose(0, 2, 1, 3).reshape(2, 8, width)
 
 
 def run_start(plane, seq, x, starts, gain, shift, shard, reduce_wide, up_wide, bias_q, bias_v, wo, fc, proj):
@@ -522,156 +740,6 @@
     )(x, starts, gain, shift, shard, reduce_wide, up_wide, bias_q, bias_v, wo, fc, proj)
 
 
-def run_feed(row, mixed, x, grad_out, out_weight, vectors, fc_weight, fc_bias, proj_weight):
-    _, tokens, width = x.shape
-    hidden_units = fc_weight.shape[1]
-    block = 1024
-    out_bias, gain, shift, proj_bias = vectors
-    return pl.pallas_call(
-        feed_kernel,
-        grid=(hidden_units // block,),
-        in_specs=[pl.BlockSpec((None, tokens, width), lambda i: (row, 0, 0))] * 3
-        + [whole((width, width))]
-        + [whole((1, width))] * 4
-        + [
-            pl.BlockSpec((width, block), lambda i: (0, i)),
-            pl.BlockSpec((1, block), lambda i: (0, i)),
-            pl.BlockSpec((block, width), lambda i: (i, 0)),
-        ],
-        out_specs=[whole((tokens, width))] * 3,
-        out_shape=[
-            jax.ShapeDtypeStruct((tokens, width), BF16),
-            jax.ShapeDtypeStruct((tokens, width), F32),
-            jax.ShapeDtypeStruct((tokens, width), BF16),
-        ],
-        scratch_shapes=[
-            pltpu.VMEM((tokens, width), F32),
-            pltpu.VMEM((tokens, width), BF16),
-            pltpu.VMEM((tokens, width), F32),
-            pltpu.VMEM((tokens, width), F32),
-        ],
-        compiler_params=pltpu.CompilerParams(vmem_limit_bytes=VMEM_BYTES),
-        cost_estimate=pl.CostEstimate(
-            flops=2 * tokens * width * (4 * hidden_units + 2 * width),
-            bytes_accessed=2 * width * (2 * hidden_units + width) + 16 * tokens * width,
-            transcendentals=tokens * hidden_units,
-        ),
-        name="feed",
-    )(mixed, x, grad_out, out_weight, out_bias, gain, shift, proj_bias, fc_weight, fc_bias, proj_weight)
-
-
-def run_backward(row, place, start, hidden, q, k, v, mixed, g_mixed, lse, down, up_wide, weight):
-    _, chunks, tokens, width = hidden.shape
-    length = chunks * tokens
-    quads = width // QUAD
-    flops = 2 * width * width * (tokens + 2 * length) + 10 * tokens * length * width
-    own = pl.BlockSpec((None, tokens, QUAD), lambda i: (row, 0, i))
-    every = pl.BlockSpec((None, length, QUAD), lambda i: (row, 0, i))
-    return pl.pallas_call(
-        partial(backward_kernel, chunks),
-        grid=(quads,),
-        in_specs=[pl.BlockSpec(memory_space=pltpu.SMEM), whole((1, tokens))]
-        + [
-            pl.BlockSpec((None, chunks, tokens, width), lambda i: (row, 0, 0, 0)),
-            own, every, every, own, pl.BlockSpec((tokens, QUAD), lambda i: (0, i)),
-            pl.BlockSpec((None, 1, 8, tokens), lambda i: (row, i, 0, 0)),
-            pl.BlockSpec((None, 8, length), lambda i: (row, 0, 0)),
-            whole((PAIR, width)),
-            pl.BlockSpec(memory_space=pl.ANY),
-        ],
-        out_specs=[whole((tokens, width))] * chunks + [whole((8, width))] * 2,
-        out_shape=[jax.ShapeDtypeStruct((tokens, width), F32 if s == 0 else BF16) for s in range(chunks)]
-        + [jax.ShapeDtypeStruct((8, width), F32)] * 2,
-        scratch_shapes=[
-            pltpu.VMEM((length, tokens), F32),
-            pltpu.VMEM((tokens, width), BF16),
-            pltpu.VMEM((length, 2 * width), BF16),
-            pltpu.VMEM((width, 3 * width), BF16),
-            pltpu.SemaphoreType.DMA,
-        ],
-        compiler_params=pltpu.CompilerParams(vmem_limit_bytes=VMEM_BYTES),
-        cost_estimate=pl.CostEstimate(
-            flops=flops, bytes_accessed=6 * width * width + 14 * length * width,
-            transcendentals=tokens * length * width // HEAD,
-        ),
-        name="attend_backward",
-    )(place, start, hidden, q, k, v, mixed, g_mixed, lse, down, up_wide, weight)
-
-
-def sum_kernel(dp, seq, part_ref, out_ref, plane_ref, line_ref, send_sems, recv_sems):
-    me, place = lax.axis_index("dp"), lax.axis_index("seq")
-    barrier = pltpu.get_barrier_semaphore()
-    mesh_type = pl.DeviceIdType.MESH
-
-    def peer(delta):
-        return lax.rem(me + delta, dp), place
-
-    def line_peer(delta):
-        return me, lax.rem(place + delta, seq)
-
-    for delta in range(1, dp):
-        pl.semaphore_signal(barrier, inc=1, device_id=peer(delta), device_id_type=mesh_type)
-    for delta in range(1, seq):
-        pl.semaphore_signal(barrier, inc=1, device_id=line_peer(delta), device_id_type=mesh_type)
-    pl.semaphore_wait(barrier, dp + seq - 2)
-
-    def send(source, target, slot, device):
-        copy = pltpu.make_async_remote_copy(
-            src_ref=source, dst_ref=target, send_sem=send_sems.at[slot], recv_sem=recv_sems.at[slot],
-            device_id=device, device_id_type=mesh_type,
-        )
-        copy.start()
-        return copy
-
-    copies = [
-        send(part_ref.at[lax.rem(me + delta, dp)], plane_ref.at[delta], delta, peer(delta))
-        for delta in range(1, dp)
-    ]
-    total = part_ref[me]
-    for delta in range(1, dp):
-        copies[delta - 1].wait()
-        total = total + plane_ref[delta]
-    line_ref[place] = total
-    copies = [
-        send(line_ref.at[place], line_ref.at[place], dp + delta, line_peer(delta)) for delta in range(1, seq)
-    ]
-    for copy in copies:
-        copy.wait()
-    total = line_ref[0]
-    for index in range(1, seq):
-        total = total + line_ref[index]
-    out_ref[me] = total
-    copies = [
-        send(out_ref.at[me], out_ref.at[me], dp + seq + delta, peer(delta)) for delta in range(1, dp)
-    ]
-    for copy in copies:
-        copy.wait()
-
-
-def run_sum(dp, seq, part):
-    rows, width = part.shape
-    piece = max(8, rows * width // (PAIR * dp))
-    flat = part.reshape(-1, PAIR)
-    used = flat.shape[0]
-    flat = jnp.pad(flat, ((0, dp * piece - used), (0, 0)))
-    slots = 2 * dp + seq
-    total = pl.pallas_call(
-        partial(sum_kernel, dp, seq),
-        in_specs=[pl.BlockSpec(memory_space=pltpu.VMEM)],
-        out_specs=pl.BlockSpec(memory_space=pltpu.VMEM),
-        out_shape=jax.ShapeDtypeStruct((dp, piece, PAIR), F32),
-        scratch_shapes=[
-            pltpu.VMEM((dp, piece, PAIR), F32),
-            pltpu.VMEM((seq, piece, PAIR), F32),
-            pltpu.SemaphoreType.DMA((slots,)),
-            pltpu.SemaphoreType.DMA((slots,)),
-        ],
-        compiler_params=pltpu.CompilerParams(collective_id=1, has_side_effects=True),
-        name="sum_all",
-    )(flat.reshape(dp, piece, PAIR))
-    return total.reshape(-1, PAIR)[:used].reshape(rows, width)
-
-
 def on_device(
     dp,
     seq,
@@ -699,52 +767,27 @@
     rows, tokens, width = block_input.shape
     rank = query_up.shape[0]
     place = lax.axis_index("seq")
-    downward = [(i + 1, i) for i in range(seq - 1)]
     side = math.isqrt(dp // 2)
 
     pad = jnp.zeros((width, PAIR - 2 * rank), BF16)
     reduce_wide = jnp.concatenate([query_adapter_reduce, value_adapter_reduce, pad], axis=1)
     up_wide = jnp.concatenate([query_up, value_up, pad.T], axis=0)
     starts = lax.dynamic_slice(seg_start, (0, place * tokens), (rows, tokens))
-    place_ref = place.astype(jnp.int32).reshape(1)
-
     def as_row(vector):
         return vector.reshape(1, -1)
 
-    vectors = tuple(as_row(a) for a in (out_bias, ln2_gain, ln2_bias, proj_bias))
     weight, whole_out, whole_fc, whole_proj, hidden, q, k, v, mixed, lse, down = run_start(
         (side, dp // (2 * side)), seq, block_input, starts[:, :, None], as_row(ln1_gain), as_row(ln1_bias), qkv_weight,
         reduce_wide, up_wide, as_row(query_bias), as_row(value_bias), out_weight, fc_weight, proj_weight,
     )
 
-    outs, grads, reduce_sum, up_sum = [], [], 0.0, 0.0
-    for r in range(rows):
-        out, g_middle, g_mixed = run_feed(
-            r, mixed, block_input, grad_out, whole_out, vectors, whole_fc, as_row(fc_bias), whole_proj
-        )
-        outs.append(out)
-        result = run_backward(
-            r, place_ref, starts[r].reshape(1, tokens), hidden, q, k, v, mixed, g_mixed, lse, down, up_wide, weight
-        )
-        reduce_sum = reduce_sum + result[seq]
-        up_sum = up_sum + result[seq + 1]
-        moving = result[seq - 1]
-        for s in range(seq - 2, -1, -1):
-            arrived = lax.ppermute(moving, "seq", downward)
-            total = result[s].astype(F32) + arrived.astype(F32)
-            moving = total.astype(BF16)
-        normed, inverse = norm_parts(block_input[r].astype(F32))
-        grads.append(g_middle + norm_backward(total, normed, inverse, ln1_gain))
-
-    summed = run_sum(dp, seq, jnp.concatenate([reduce_sum * ADAPTER_SCALE, up_sum], axis=0))
-    return (
-        jnp.stack(outs),
-        jnp.stack(grads),
-        summed[:rank].T,
-        summed[8 : 8 + rank],
-        summed[rank : 2 * rank].T,
-        summed[8 + rank : 8 + 2 * rank],
+    vectors = tuple(as_row(a) for a in (ln1_gain, out_bias, ln2_gain, ln2_bias, proj_bias, fc_bias))
+    out, grad, small = run_finish(
+        dp, seq, block_input, starts[:, None, :], lse, down, up_wide, vectors, grad_out,
+        weight, whole_out, whole_fc, whole_proj, hidden, q, k, v, mixed,
     )
+    reduce, up = small[0], small[1]
+    return out, grad, reduce[:rank].T, up[:rank], reduce[rank : 2 * rank].T, up[rank : 2 * rank]
 
 
 def solution(mesh):

time: 395 us -> 307 us (0.78)
  waiting for transfers between devices: 54.6 us -> 0 us
  other arithmetic: 18.4 us -> 2.37 us
  starting transfers between devices: 12 us -> 0 us
    ppermute x9 -> x0, waiting for transfers between devices: 54.6 us -> none  [on_device(): arrived = lax.ppermute(moving, 'seq', downward)]
    ppermute x9 -> x0, starting transfers between devices: 12 us -> none  [on_device(): arrived = lax.ppermute(moving, 'seq', downward)]
    another operation x4 -> x0, other arithmetic: 6.88 us -> none  [the longest x3 5.57 us: on_device(): jnp.stack(grads)]
    convert_element_type x6 -> x0, other arithmetic: 5.76 us -> none  [on_device(): moving = total.astype(BF16)]
    unnamed x52 -> x8, local copies, waits for them, and re-layouts: 2.23 us -> 6.76 us
    reduce_sum x3 -> x0, other arithmetic: 3.97 us -> none  [the longest x1 3.12 us: norm_backward(): jnp.mean(scaled, axis=-1, keepdims=True)]
    pallas_call x7 -> x1, Pallas kernels: 179 us -> 176 us  [run_finish(): pl.pallas_call(partial(finish_kernel, dp, seq, rows, block), in_specs=[vm...]
  transfers between devices with their start and end apart: 9 -> 0, of which waited for: 6 -> 0; matrix products, arithmetic and copies ran while one was open for 3% -> 0% of each run, Pallas kernels for 34% -> 0%
where the time goes in v4:
time: 307 us; the launch traced here: 306 us
  Pallas kernels  293 us (95%)
  local copies, waits for them, and re-layouts  9.96 us (3%)
    pallas_call x1, Pallas kernels, run_finish(): pl.pallas_call(partial(finish_kernel, dp, seq, rows, block), in_specs=[vm...  176 us
    pallas_call x1, Pallas kernels, run_start(): pl.pallas_call(partial(start_kernel, plane, seq, rows), in_specs=[vmem] *...  117 us
    unnamed x8, local copies, waits for them, and re-layouts  6.76 us

profile of v4, /device:TPU:0, one launch (start us, length us, event | category | flops | bytes accessed | tf_op | source)
XLA Modules:
  0.0 306.2 jit_solution(3666014724910987091)
XLA Ops:
  0.6 0.0 copy-start
  0.7 0.1 pad.5.clone
  0.7 0.6 copy-done
  1.4 0.6 broadcast_in_dim.9.start_ref
  1.9 1.5 maximum_maximum_fusion.1.up_ref
  3.4 0.9 copy.30
  4.3 0.9 copy.31
  5.2 0.9 maximum_maximum_fusion.reduce_ref
  6.1 0.9 copy.32.start_ref
  7.1 117.4 %start.1 = (bf16[1024,3072]{1,0:T(8,128)(2,1)}, bf16[1024,1024]{1,0:T(8,128)(2,1)}, bf16[1024,4096]{1,0:T(8,128)(2,1)}, bf16[4096,1024]{1,0:T(8,128)(2,1)}, bf16...) custom-call(bf16[3,256,1024]{2,1,0:T(8,128)(2,1)} %x_ref.3, ...), custom_call_target="tpu_custom_call" | custom-call | tf_op jit(solution)/shard_map/start/pallas_call | solution.py:709
  124.5 175.8 %finish.1 = (bf16[3,256,1024]{2,1,0:T(8,128)(2,1)}, f32[3,256,1024]{2,1,0:T(8,128)}, f32[8,16,128]{2,1,0:T(8,128)}) custom-call(bf16[3,256,1024]{2,1,0:T(8,128)(2,1)} %x_ref.3, s32[3,1,256]{2,1,0:T(1,128)} %broadcast_in_dim.9.start_ref, f32[3,4,8,256]{3,2,1,0:T(8,128)} %get-tuple-element.20.lse_ref, bf16[3,8,1024]{2,1,0:T(8,128)(2,1)} %get-tuple-element.21.down_ref, ...), custom_call_target="tpu_custom_call" | custom-call | tf_op jit(solution)/shard_map/finish/pallas_call | solution.py:656
  300.2 0.0 copy-start.1
  300.3 1.6 slice_bitcast_fusion
  301.8 2.7 copy.37
  304.5 0.0 copy-done.1
  304.5 1.7 copy.38
  (3 shorter events, 0.0 us)
Async XLA Ops:
  0.6 0.7 copy-start
  300.2 4.3 %copy-start.1 = (f32[3,256,1024]{2,1,0:T(8,128)S(1)}, f32[3,256,1024]{2,1,0:T(8,128)}, u32[]{:S(2)}) copy-start(f32[3,256,1024]{2,1,0:T(8,128)} %get-tuple-element.45) | copy-start | bytes 9437188

commit v5 on v4

v5 whole, which is shorter than its diff:
```python
import math
from functools import partial

import jax
import jax.numpy as jnp
from jax import lax
from jax.experimental import pallas as pl
from jax.experimental.pallas import tpu as pltpu
from jax.sharding import PartitionSpec as P

HEAD = 64
QUAD = 256
PAIR = 128
NORM_EPSILON = 1e-05
ADAPTER_SCALE = 8.0
MASKED = -1e30
GELU_A = 0.7978845608028654
GELU_B = 0.044715

F32 = jnp.float32
BF16 = jnp.bfloat16
VMEM_BYTES = 65400 * 1024


def dot_nn(left, right):
    return lax.dot_general(left, right, (((1,), (0,)), ((), ())), preferred_element_type=F32)


def dot_nt(left, right):
    return lax.dot_general(left, right, (((1,), (1,)), ((), ())), preferred_element_type=F32)


def norm_parts(values):
    average = jnp.mean(values, axis=-1, keepdims=True)
    centered = values - average
    inverse = lax.rsqrt(jnp.mean(centered * centered, axis=-1, keepdims=True) + NORM_EPSILON)
    return centered * inverse, inverse


def norm_backward(gradient, normed, inverse, gain):
    scaled = gradient * gain
    return inverse * (
        scaled
        - jnp.mean(scaled, axis=-1, keepdims=True)
        - normed * jnp.mean(scaled * normed, axis=-1, keepdims=True)
    )


def head_lanes(rows, dtype):
    lane = lax.broadcasted_iota(jnp.int32, (rows, PAIR), 1)
    return lane < HEAD


def own_starts(seg_ref, begin_ref, place, seq):
    rows, _, tokens = begin_ref.shape
    own = jnp.zeros((rows, tokens), jnp.int32)
    for index in range(seq):
        own = jnp.where(place == index, seg_ref[:, index * tokens : (index + 1) * tokens], own)
    own = own.astype(F32)
    for row in range(rows):
        begin_ref[row] = jnp.broadcast_to(own[row : row + 1], (8, tokens))


def block_kernel(
    plane, seq, rows, block,
    x_ref, seg_ref, small_ref, gain1, shift1, bias_q, bias_v, out_bias, gain2, shift2, proj_bias, fc_bias,
    shard_in, wo_in, fc_in, proj_in, gout_in,
    out_out, grad_out, sum_out, q_spill, k_spill, v_spill,
    w_held, wo_held, fc_held, proj_held, hidden, q_held, k_held, v_held, mix_held, gout_held,
    gmix_ref, h2_ref, acc_ref, back_ref, gmid_ref, own_ref, mask_ref, delta_ref, dq_ref, dkv_ref,
    leaving, arriving, begin_ref, turned_ref, lse_ref, down_ref, up_sum, reduce_sum,
    part_ref, plane_ref, line_ref,
    send_sems, recv_sems, hop_send, hop_recv, own_sems, spill_sems, gout_sem, store_sems,
    leave_sems, arrive_sems, sum_send, sum_recv,
):
    nx, ny = plane
    dp = nx * ny * 2
    tokens, width = x_ref.shape[1], x_ref.shape[2]
    quads = width // QUAD
    steps = fc_held.shape[1] // block
    top = seq - 1
    mesh_type = pl.DeviceIdType.MESH
    me, place = lax.axis_index("dp"), lax.axis_index("seq")
    core = lax.rem(me, 2)
    my_x = lax.rem(me // 2, nx)
    my_y = me // (2 * nx)

    def index(y, x, c):
        return (y * nx + x) * 2 + c

    def x_peer(delta):
        return index(my_y, lax.rem(my_x + delta, nx), core), place

    def y_peer(delta):
        return index(lax.rem(my_y + delta, ny), my_x, core), place

    twin = (index(my_y, my_x, 1 - core), place)

    def owner(dy, dx, c):
        return index(lax.rem(my_y + ny - dy, ny), lax.rem(my_x + nx - dx, nx), c)

    def peer(delta):
        return lax.rem(me + delta, dp), place

    def line_peer(delta):
        return me, lax.rem(place + delta, seq)

    barrier = pltpu.get_barrier_semaphore()
    for delta in range(1, dp):
        pl.semaphore_signal(barrier, inc=1, device_id=peer(delta), device_id_type=mesh_type)
    for delta in range(1, seq):
        pl.semaphore_signal(barrier, inc=1, device_id=line_peer(delta), device_id_type=mesh_type)

    sources = [shard_in, wo_in, fc_in, proj_in]
    targets = [w_held, wo_held, fc_held, proj_held]

    def region(t, device, half=None):
        size = sources[t].shape[0]
        if half is None:
            return targets[t].at[pl.ds(pl.multiple_of(device * size, size), size), :]
        part = size // 2
        return targets[t].at[pl.ds(pl.multiple_of(device * size + half * part, part), part), :]

    def flight(t, slot, part, device):
        return pltpu.make_async_remote_copy(
            src_ref=part, dst_ref=part, send_sem=send_sems.at[t, slot], recv_sem=recv_sems.at[t, slot],
            device_id=device, device_id_type=mesh_type,
        )

    flights = {}
    for t in range(4):
        names = [("x", 0, dx) for dx in range(1, nx)] + [("y", dy, 0) for dy in range(1, ny)]
        names += [(kind, dy, dx) for kind in "ab" for dy in range(1, ny) for dx in range(1, nx)]
        names += [("t", dy, dx) for dy in range(ny) for dx in range(nx)]
        for slot, (kind, dy, dx) in enumerate(names):
            if kind == "x":
                part, device = region(t, me), x_peer(dx)
            elif kind == "y":
                part, device = region(t, me), y_peer(dy)
            elif kind == "a":
                part, device = region(t, owner(0, dx, core), 0), y_peer(dy)
            elif kind == "b":
                part, device = region(t, owner(dy, 0, core), 1), x_peer(dx)
            else:
                part, device = region(t, owner(dy, dx, core)), twin
            flights[t, kind, dy, dx] = flight(t, slot, part, device)

    def wave_one(t):
        for dx in range(1, nx):
            flights[t, "x", 0, dx].start()
        for dy in range(1, ny):
            flights[t, "y", dy, 0].start()
        flights[t, "t", 0, 0].start()

    def wave_two(t):
        for dx in range(1, nx):
            flights[t, "x", 0, dx].wait_recv()
            for dy in range(1, ny):
                flights[t, "a", dy, dx].start()
        for dy in range(1, ny):
            flights[t, "y", dy, 0].wait_recv()
            for dx in range(1, nx):
                flights[t, "b", dy, dx].start()
        for dx in range(1, nx):
            flights[t, "t", 0, dx].start()
        for dy in range(1, ny):
            flights[t, "t", dy, 0].start()

    def wave_three(t):
        for dy in range(1, ny):
            for dx in range(1, nx):
                flights[t, "a", dy, dx].wait_recv()
                flights[t, "b", dy, dx].wait_recv()
                flights[t, "t", dy, dx].start()

    def wave_end(t):
        for dy in range(ny):
            for dx in range(nx):
                flights[t, "t", dy, dx].wait_recv()

    def hop(row, s):
        return pltpu.make_async_remote_copy(
            src_ref=hidden.at[row, s - 1], dst_ref=hidden.at[row, s],
            send_sem=hop_send.at[row, s - 1], recv_sem=hop_recv.at[row, s - 1],
            device_id=(me, place + 1), device_id_type=mesh_type,
        )

    def hop_start(row, s):
        @pl.when((place >= s - 1) & (place < top))
        def _():
            hop(row, s).start()

    def arrive(row, s):
        @pl.when(place >= s)
        def _():
            hop(row, s).wait_recv()

        if s < seq - 1:
            hop_start(row, s + 1)
        if s == seq - 1 and row < rows - 1:
            hop_start(row + 1, 1)

    def first_norm(row):
        normed, _ = norm_parts(x_ref[row].astype(F32))
        hidden[row, 0] = (normed * gain1[...] + shift1[...]).astype(BF16)

    def gout_load(row):
        return pltpu.make_async_copy(gout_in.at[row], gout_held, gout_sem)

    own_copies = [pltpu.make_async_copy(sources[t], region(t, me), own_sems.at[t]) for t in range(4)]
    for copy in own_copies:
        copy.start()
    gout_load(0).start()
    first_norm(0)
    turned_ref[...] = small_ref[:8, :].astype(F32).T
    pl.semaphore_wait(barrier, dp + seq - 2)
    hop_start(0, 1)
    own_copies[0].wait()
    size = shard_in.shape[0]
    mine = pl.ds(pl.multiple_of(me * size, size), size)
    reduce_own = turned_ref[mine, :].astype(BF16)
    up = small_ref[8:, :]
    low_rank = lax.broadcasted_iota(jnp.int32, up.shape, 0) < 4
    for column, rank_up in ((0, jnp.where(low_rank, up, jnp.zeros_like(up))), (2, jnp.where(low_rank, jnp.zeros_like(up), up))):
        span = slice(column * width, (column + 1) * width)
        change = dot_nn(reduce_own, rank_up) * ADAPTER_SCALE
        w_held[mine, span] = (w_held[mine, span].astype(F32) + change).astype(BF16)
    wave_one(0)
    for copy in own_copies[1:]:
        copy.wait()
    wave_one(1)
    own_starts(seg_ref, begin_ref, place, seq)
    for row in range(1, rows):
        first_norm(row)
    for s in range(1, seq):
        @pl.when(place < s)
        def _():
            for row in range(rows):
                hidden[row, s] = jnp.zeros((tokens, width), BF16)
    up_sum[...] = jnp.zeros_like(up_sum)
    reduce_sum[...] = jnp.zeros_like(reduce_sum)

    low = head_lanes(tokens, BF16)
    lane = lax.broadcasted_iota(jnp.int32, (tokens, PAIR), 1)
    rank_row = lax.broadcasted_iota(jnp.int32, (8, width), 0) < 4

    def both_heads(pair):
        none = jnp.zeros_like(pair)
        return jnp.concatenate([jnp.where(low, pair, none), jnp.where(low, none, pair)], axis=0)

    def spills(row):
        return [
            pltpu.make_async_copy(held, spill.at[row], spill_sems.at[i])
            for i, (held, spill) in enumerate(((q_held, q_spill), (k_held, k_spill), (v_held, v_spill)))
        ]

    def reloads(row):
        return [
            pltpu.make_async_copy(spill.at[row], held, spill_sems.at[3 + i])
            for i, (held, spill) in enumerate(((q_held, q_spill), (k_held, k_spill), (v_held, v_spill)))
        ]

    def attend(row, middle):
        slot = lax.rem(row, 2)
        query = place * tokens + lax.broadcasted_iota(jnp.int32, (tokens, tokens), 0)
        start = begin_ref[row].T[:, :1].astype(jnp.int32)
        for s in range(seq):
            key = (place - s) * tokens + lax.broadcasted_iota(jnp.int32, (tokens, tokens), 1)
            span = slice(s * tokens, (s + 1) * tokens)
            mask_ref[:, span] = jnp.where((key >= start) & (key <= query), 0.0, MASKED)
            down_ref[row, :, span] = (dot_nt(small_ref[:8, :], hidden[row, s]) * ADAPTER_SCALE).astype(BF16)

        for quad in range(quads):
            own = slice(quad * QUAD, (quad + 1) * QUAD)
            key_span = slice(width + quad * QUAD, width + (quad + 1) * QUAD)
            value_span = slice(2 * width + quad * QUAD, 2 * width + (quad + 1) * QUAD)
            q = dot_nn(hidden[row, 0], w_held[:, own]) + bias_q[:, own]
            q_held[:, own] = (q.astype(BF16) * (HEAD**-0.5)).astype(BF16)
            for s in range(seq):
                span = slice(s * tokens, (s + 1) * tokens)
                k_held[span, own] = dot_nn(hidden[row, s], w_held[:, key_span]).astype(BF16)
                v_held[span, own] = (dot_nn(hidden[row, s], w_held[:, value_span]) + bias_v[:, own]).astype(BF16)
            totals = jnp.zeros((tokens, PAIR), F32)
            for pair in range(QUAD // PAIR):
                span = slice(quad * QUAD + pair * PAIR, quad * QUAD + (pair + 1) * PAIR)
                score = dot_nt(both_heads(q_held[:, span]), k_held[:, span])
                score = jnp.concatenate([score[:tokens] + mask_ref[...], score[tokens:] + mask_ref[...]], axis=0)
                highest = jnp.max(score, axis=-1, keepdims=True)
                weight = jnp.exp(score - highest)
                total = jnp.sum(weight, axis=-1, keepdims=True)
                mixed = dot_nn(weight.astype(BF16), v_held[:, span]) * (1.0 / total)
                mix_held[slot, :, span] = jnp.where(low, mixed[:tokens], mixed[tokens:]).astype(BF16)
                lse = highest + jnp.log(total)
                totals = jnp.where(lane == 2 * pair, lse[:tokens], totals)
                totals = jnp.where(lane == 2 * pair + 1, lse[tokens:], totals)
            lse_ref[row, quad] = totals.T[:8]
            if 2 * (quad + 1) == quads:
                middle()

    def out_store(row):
        return pltpu.make_async_copy(h2_ref, out_out.at[row], store_sems.at[0])

    def grad_store(row):
        slot = lax.rem(row, 2)
        return pltpu.make_async_copy(gmid_ref.at[slot], grad_out.at[row], store_sems.at[1 + slot])

    def leave(row, s):
        return pltpu.make_async_remote_copy(
            src_ref=leaving.at[s - 1], dst_ref=arriving.at[row, s - 1],
            send_sem=leave_sems.at[s - 1], recv_sem=arrive_sems.at[row, s - 1],
            device_id=(me, place - 1), device_id_type=mesh_type,
        )

    def chain(row, s):
        @pl.when((place < top) & (place >= s))
        def _():
            leave(row, s + 1).wait_recv()
            leaving[s - 1] = (leaving[s - 1].astype(F32) + arriving[row, s].astype(F32)).astype(BF16)
            leave(row, s).start()

    def chain_end(row):
        @pl.when(place < top)
        def _():
            leave(row, 1).wait_recv()
            own_ref[...] += arriving[row, 0].astype(F32)

        slot = lax.rem(row, 2)
        normed, inverse = norm_parts(x_ref[row].astype(F32))
        gmid_ref[slot] = gmid_ref[slot] + norm_backward(own_ref[...], normed, inverse, gain1[...])
        grad_store(row).start()

    def feed(row):
        slot = lax.rem(row, 2)
        gout_load(row).wait()

        @pl.when(row >= 1)
        def _():
            out_store(row - 1).wait()

        @pl.when(row >= 2)
        def _():
            grad_store(row - 2).wait()

        middle = x_ref[row].astype(F32) + dot_nn(mix_held[slot], wo_held[...]) + out_bias[...]
        gmid_ref[slot] = middle
        normed, _ = norm_parts(middle)
        h2_ref[...] = (normed * gain2[...] + shift2[...]).astype(BF16)
        acc_ref[...] = jnp.zeros_like(acc_ref)
        back_ref[...] = jnp.zeros_like(back_ref)

        @pl.when(row < rows - 1)
        def _():
            for copy in spills(row + 1):
                copy.wait()

        for copy in reloads(row):
            copy.start()

        @pl.loop(0, steps)
        def _(step):
            part = pl.ds(pl.multiple_of(step * block, block), block)
            before = dot_nn(h2_ref[...], fc_held[:, part]) + fc_bias[:, part]
            square = before * before
            bend = jnp.tanh(GELU_A * before * (1.0 + GELU_B * square))
            half = 0.5 * (1.0 + bend)
            slope = half + 0.5 * before * (1.0 - bend * bend) * (GELU_A * (1.0 + 3.0 * GELU_B * square))
            act = (before * half).astype(BF16)
            g_before = (dot_nt(gout_held[...], proj_held[part, :]) * slope).astype(BF16)
            acc_ref[...] += dot_nn(act, proj_held[part, :])
            back_ref[...] += dot_nt(g_before, fc_held[:, part])

        middle = gmid_ref[slot]
        h2_ref[...] = (middle + acc_ref[...] + proj_bias[...]).astype(BF16)
        out_store(row).start()
        normed, inverse = norm_parts(middle)
        g_middle = gout_held[...].astype(F32) + norm_backward(back_ref[...], normed, inverse, gain2[...])
        gmid_ref[slot] = g_middle
        gmix_ref[...] = dot_nt(g_middle.astype(BF16), wo_held[...]).astype(BF16)
        for pair in range(width // PAIR):
            span = slice(pair * PAIR, (pair + 1) * PAIR)
            product = (gmix_ref[:, span].astype(F32) * mix_held[slot, :, span].astype(F32)).T
            for half in range(2):
                head = pair * 2 + half
                delta_ref[head // 4, head % 4 : head % 4 + 1, :] = jnp.sum(
                    product[half * HEAD : (half + 1) * HEAD], axis=0, keepdims=True
                )

        @pl.when(row < rows - 1)
        def _():
            gout_load(row + 1).start()

    def attend_chunk(row, s):
        query = place * tokens + lax.broadcasted_iota(jnp.int32, (tokens, tokens), 1)
        key = (place - s) * tokens + lax.broadcasted_iota(jnp.int32, (tokens, tokens), 0)
        start = begin_ref[row, :1, :].astype(jnp.int32)
        mask = jnp.where((key >= start) & (key <= query), 0.0, MASKED)
        mask_ref[:, :tokens] = mask
        mask_ref[:, tokens : 2 * tokens] = mask
        rows_s = pl.ds(pl.multiple_of(s * tokens, tokens), tokens)
        for pair in range(width // PAIR):
            span = slice(pair * PAIR, (pair + 1) * PAIR)
            k_pair, v_pair = k_held[rows_s, span], v_held[rows_s, span]
            q_both, g_both = both_heads(q_held[:, span]), both_heads(gmix_ref[:, span])
            head = 2 * (pair % 2)
            lse, inner = [
                jnp.concatenate([ref[head : head + 1, :], ref[head + 1 : head + 2, :]], axis=1)
                for ref in (lse_ref.at[row, pair // 2], delta_ref.at[pair // 2])
            ]
            prob = jnp.exp(dot_nt(k_pair, q_both) + mask_ref[:, : 2 * tokens] - lse)
            g_score = (prob * (dot_nt(v_pair, g_both) - inner)).astype(BF16)
            dkv_ref[:, span] = dot_nn(g_score, q_both).astype(BF16)
            dkv_ref[:, width + pair * PAIR : width + (pair + 1) * PAIR] = dot_nn(prob.astype(BF16), g_both).astype(BF16)
            k_turned = k_pair.astype(F32).T.astype(BF16)
            for half in range(2):
                lines = slice(pair * PAIR + half * HEAD, pair * PAIR + (half + 1) * HEAD)
                part = g_score[:, half * tokens : (half + 1) * tokens]
                dq_ref[lines, :] += dot_nn(k_turned[half * HEAD : (half + 1) * HEAD], part)

        grad = dot_nt(dkv_ref[...], w_held[:, width:])
        dv = dkv_ref[:, width:]
        up_grad = dot_nn(down_ref[row, :, rows_s], dv)
        g_down = dot_nt(small_ref[8:, :], dv).astype(BF16)
        reduce_grad = dot_nn(g_down, hidden[row, s])
        up_sum[...] += jnp.where(rank_row, 0.0, up_grad)
        reduce_sum[...] += jnp.where(rank_row, 0.0, reduce_grad)
        if not isinstance(s, int):
            @pl.when(row > 0)
            def _():
                leave(row - 1, s).wait_send()

            leaving[s - 1] = grad.astype(BF16)

            @pl.when(place == top)
            def _():
                leave(row, s).start()
        else:
            dq = (dq_ref[...].T * (HEAD**-0.5)).astype(BF16)
            own_ref[...] = grad + dot_nt(dq, w_held[:, :width])
            up_grad = dot_nn(down_ref[row, :, rows_s], dq)
            g_down = dot_nt(small_ref[8:, :], dq).astype(BF16)
            reduce_grad = dot_nn(g_down, hidden[row, s])
            up_sum[...] += jnp.where(rank_row, up_grad, 0.0)
            reduce_sum[...] += jnp.where(rank_row, reduce_grad, 0.0)

    def before_first():
        arrive(0, 1)
        wave_two(0)
        wave_one(2)
        wave_two(1)
        for s in range(2, seq):
            if s == seq - 1:
                wave_three(0)
                wave_three(1)
            arrive(0, s)
        wave_end(0)
        wave_one(3)

    def before_second():
        for s in range(1, seq):
            arrive(1, s)

    def amid_second():
        wave_two(2)
        wave_two(3)
        arrive(2, 1)

    def after_second():
        for s in range(2, seq):
            arrive(2, s)
        wave_three(2)
        wave_three(3)
        for t in range(1, 4):
            wave_end(t)

    def before_later(row):
        for s in range(1, seq):
            arrive(row, s)

    @pl.loop(0, rows + 1)
    def _(turn):
        for index in range(rows):
            if index != 2:
                action = before_first if index == 0 else before_second if index == 1 else partial(before_later, index)
                pl.when(turn == index)(action)

        @pl.when(turn == 1)
        def _():
            for copy in spills(0):
                copy.wait()

        @pl.when(turn < rows)
        def _():
            attend(turn, lambda: pl.when(turn == 1)(amid_second))
            for copy in spills(turn):
                copy.start()

        pl.when(turn == 1)(after_second)

        @pl.when(turn > 0)
        def _():
            row = turn - 1
            feed(row)

            @pl.when(row > 0)
            def _():
                chain(row - 1, seq - 3)

            for copy in reloads(row):
                copy.wait()
            dq_ref[...] = jnp.zeros_like(dq_ref)

            @pl.loop(0, seq - 1)
            def _(step):
                s = seq - 1 - step

                @pl.when((row > 0) & (s < seq - 3))
                def _():
                    chain(row - 1, s)

                @pl.when(place >= s)
                def _():
                    attend_chunk(row, s)

            chain(row, seq - 2)

            @pl.when(row > 0)
            def _():
                chain_end(row - 1)

            attend_chunk(row, 0)

    def send(source, target, slot, device):
        copy = pltpu.make_async_remote_copy(
            src_ref=source, dst_ref=target, send_sem=sum_send.at[slot], recv_sem=sum_recv.at[slot],
            device_id=device, device_id_type=mesh_type,
        )
        copy.start()
        return copy

    piece = part_ref.shape[1]
    lanes = width // PAIR
    part_ref[...] = jnp.zeros_like(part_ref)
    for half, total in enumerate((reduce_sum[...] * ADAPTER_SCALE, up_sum[...])):
        for block_lane in range(lanes):
            line = (half * lanes + block_lane) * 8
            part_ref[line // piece, line % piece : line % piece + 8, :] = total[:, block_lane * PAIR : (block_lane + 1) * PAIR]
    copies = [send(part_ref.at[lax.rem(me + delta, dp)], plane_ref.at[delta], delta, peer(delta)) for delta in range(1, dp)]
    last = rows - 1
    chain(last, seq - 3)
    total = part_ref[me]
    for delta in range(1, dp):
        copies[delta - 1].wait()
        total = total + plane_ref[delta]
    line_ref[place] = total
    copies = [send(line_ref.at[place], line_ref.at[place], dp + delta, line_peer(delta)) for delta in range(1, seq)]
    for copy in copies:
        copy.wait()
    total = line_ref[0]
    for other in range(1, seq):
        total = total + line_ref[other]
    sum_out[me] = total
    copies = [send(sum_out.at[me], sum_out.at[me], dp + seq + delta, peer(delta)) for delta in range(1, dp)]
    for s in range(seq - 4, 0, -1):
        chain(last, s)
    chain_end(last)
    for copy in copies:
        copy.wait()
    for copy in flights.values():
        copy.wait_send()
    for row in range(rows):
        for s in range(1, seq):
            @pl.when((place >= s - 1) & (place < top))
            def _():
                hop(row, s).wait_send()
    for s in range(1, seq):
        @pl.when(place >= s)
        def _():
            leave(last, s).wait_send()
    out_store(last).wait()
    for row in range(max(0, rows - 2), rows):
        grad_store(row).wait()


def run_block(plane, seq, x, seg, small, vectors, shards, gout):
    rows, tokens, width = x.shape
    length = seq * tokens
    dp = plane[0] * plane[1] * 2
    hidden_units = shards[2].shape[1]
    block = 1024
    quads = width // QUAD
    piece = max(8, 16 * width // (PAIR * dp))
    nx, ny = plane
    flights = nx - 1 + ny - 1 + 2 * (nx - 1) * (ny - 1) + nx * ny
    sums = 2 * dp + seq
    anywhere = pl.BlockSpec(memory_space=pl.ANY)
    vmem = pl.BlockSpec(memory_space=pltpu.VMEM)
    dma = pltpu.SemaphoreType.DMA

    def held(*dims, dtype=BF16):
        return pltpu.VMEM(dims, dtype)

    def shape(*dims, dtype=BF16):
        return jax.ShapeDtypeStruct(dims, dtype)

    result = pl.pallas_call(
        partial(block_kernel, plane, seq, rows, block),
        in_specs=[vmem] * 12 + [anywhere] * 5,
        out_specs=[anywhere, anywhere, vmem] + [anywhere] * 3,
        out_shape=[
            shape(rows, tokens, width), shape(rows, tokens, width, dtype=F32), shape(dp, piece, PAIR, dtype=F32),
            shape(rows, tokens, width), shape(rows, length, width), shape(rows, length, width),
        ],
        scratch_shapes=[
            held(width, 3 * width), held(width, width), held(width, hidden_units), held(hidden_units, width),
            held(rows, seq, tokens, width), held(tokens, width), held(length, width), held(length, width),
            held(2, tokens, width), held(tokens, width),
            held(tokens, width), held(tokens, width),
            held(tokens, width, dtype=F32), held(tokens, width, dtype=F32), held(2, tokens, width, dtype=F32),
            held(tokens, width, dtype=F32), held(tokens, length, dtype=F32), held(quads, 8, tokens, dtype=F32),
            held(width, tokens, dtype=F32), held(tokens, 2 * width),
            held(seq - 1, tokens, width), held(rows, seq - 1, tokens, width),
            held(rows, 8, tokens, dtype=F32), held(width, 8, dtype=F32),
            held(rows, quads, 8, tokens, dtype=F32), held(rows, 8, length),
            held(8, width, dtype=F32), held(8, width, dtype=F32),
            held(dp, piece, PAIR, dtype=F32), held(dp, piece, PAIR, dtype=F32), held(seq, piece, PAIR, dtype=F32),
            dma((4, flights)), dma((4, flights)), dma((rows, seq - 1)), dma((rows, seq - 1)),
            dma((4,)), dma((6,)), dma, dma((3,)),
            dma((seq - 1,)), dma((rows, seq - 1)), dma((sums,)), dma((sums,)),
        ],
        compiler_params=pltpu.CompilerParams(
            vmem_limit_bytes=VMEM_BYTES, collective_id=0, has_side_effects=True
        ),
        name="block",
    )(x, seg, small, *vectors, *shards, gout)
    out, grad, total = result[:3]
    flat = total.reshape(-1, PAIR)[: 16 * width // PAIR]
    return out, grad, flat.reshape(2, width // PAIR, 8, PAIR).transpose(0, 2, 1, 3).reshape(2, 8, width)


def on_device(
    dp,
    seq,
    block_input,
    seg_start,
    ln1_gain,
    ln1_bias,
    qkv_weight,
    query_bias,
    value_bias,
    query_adapter_reduce,
    query_up,
    value_adapter_reduce,
    value_up,
    out_weight,
    out_bias,
    ln2_gain,
    ln2_bias,
    fc_weight,
    fc_bias,
    proj_weight,
    proj_bias,
    grad_out,
):
    rows, tokens, width = block_input.shape
    rank = query_up.shape[0]
    side = math.isqrt(dp // 2)
    small = jnp.concatenate([query_adapter_reduce.T, value_adapter_reduce.T, query_up, value_up], axis=0)

    def as_row(vector):
        return vector.reshape(1, -1)

    vectors = tuple(
        as_row(a)
        for a in (ln1_gain, ln1_bias, query_bias, value_bias, out_bias, ln2_gain, ln2_bias, proj_bias, fc_bias)
    )
    out, grad, sums = run_block(
        (side, dp // (2 * side)), seq, block_input, seg_start, small, vectors,
        (qkv_weight, out_weight, fc_weight, proj_weight), grad_out,
    )
    reduce, up = sums[0], sums[1]
    return out, grad, reduce[:rank].T, up[:rank], reduce[rank : 2 * rank].T, up[rank : 2 * rank]


def solution(mesh):
    return jax.shard_map(
        partial(on_device, mesh.shape["dp"], mesh.shape["seq"]),
        mesh=mesh,
        in_specs=(
            P("dp", "seq", None),
            P("dp", None),
            P(),
            P(),
            P("dp", None),
            P(),
            P(),
            P(),
            P(),
            P(),
            P(),
            P("dp", None),
            P(),
            P(),
            P(),
            P("dp", None),
            P(),
            P("dp", None),
            P(),
            P("dp", "seq", None),
        ),
        out_specs=(P("dp", "seq", None), P("dp", "seq", None), P(), P(), P(), P()),
        check_vma=False,
    )
```

time: 307 us -> 283 us (0.922)
  Pallas kernels: 293 us -> 274 us
  local copies, waits for them, and re-layouts: 9.96 us -> 5.96 us
    pallas_call x2 -> x1, Pallas kernels: 293 us -> 274 us  [run_block(): pl.pallas_call(partial(block_kernel, plane, seq, rows, block), in_specs=[...]
    unnamed x8 -> x4, local copies, waits for them, and re-layouts: 6.76 us -> 4.49 us
where the time goes in v5:
time: 283 us; the launch traced here: 282 us
  Pallas kernels  274 us (97%)
  local copies, waits for them, and re-layouts  5.96 us (2%)
    pallas_call x1, Pallas kernels, run_block(): pl.pallas_call(partial(block_kernel, plane, seq, rows, block), in_specs=[...  274 us

profile of v5, /device:TPU:0, one launch (start us, length us, event | category | flops | bytes accessed | tf_op | source)
XLA Modules:
  0.0 282.3 jit_solution(16385765372195072533)
XLA Ops:
  0.6 1.4 pad_maximum_fusion.small_ref
  2.0 274.4 %block.1 = (bf16[3,256,1024]{2,1,0:T(8,128)(2,1)}, f32[3,256,1024]{2,1,0:T(8,128)}, f32[8,16,128]{2,1,0:T(8,128)}, bf16[3,256,1024]{2,1,0:T(8,128)(2,1)}, bf16[3...) custom-call(bf16[3,256,1024]{2,1,0:T(8,128)(2,1)} %x_ref.1, s32[3,1024]{1,0:T(4,128)} %seg_ref.1, ...), custom_call_target="tpu_custom_call" | custom-call | tf_op jit(solution)/shard_map/block/pallas_call | solution.py:605
  276.4 1.5 slice_bitcast_fusion
  277.9 0.0 copy-start
  277.9 2.8 copy.30
  280.7 0.0 copy-done
  280.7 1.7 copy.31
Async XLA Ops:
  277.9 2.8 %copy-start = (f32[3,256,1024]{2,1,0:T(8,128)S(1)}, f32[3,256,1024]{2,1,0:T(8,128)}, u32[]{:S(2)}) copy-start(f32[3,256,1024]{2,1,0:T(8,128)} %get-tuple-element.23) | copy-start | bytes 9437188

commit v6 on v5

--- a/solution.py
+++ b/solution.py
@@ -63,21 +63,35 @@
 
 def block_kernel(
     plane, seq, rows, block,
-    x_ref, seg_ref, small_ref, gain1, shift1, bias_q, bias_v, out_bias, gain2, shift2, proj_bias, fc_bias,
-    shard_in, wo_in, fc_in, proj_in, gout_in,
-    out_out, grad_out, sum_out, q_spill, k_spill, v_spill,
-    w_held, wo_held, fc_held, proj_held, hidden, q_held, k_held, v_held, mix_held, gout_held,
+    x_in, seg_in, small_in, gain1_in, shift1_in, bias_q_in, bias_v_in, out_bias_in, gain2_in, shift2_in, proj_bias_in,
+    fc_bias_in, shard_in, wo_in, fc_in, proj_in, gout_in,
+    out_out, grad_out, sum_out, q_spill, k_spill, v_spill, mix_spill,
+    x_ref, seg_ref, small_ref, gain1, shift1, bias_q, bias_v, out_bias, gain2, shift2, proj_bias, fc_bias, input_sems,
+    w_held, wo_held, fc_held, proj_held, hidden, q_held, k_held, v_held, mix_row, mix_held, gout_held,
     gmix_ref, h2_ref, acc_ref, back_ref, gmid_ref, own_ref, mask_ref, delta_ref, dq_ref, dkv_ref,
-    leaving, arriving, begin_ref, turned_ref, lse_ref, down_ref, up_sum, reduce_sum,
+    leaving, arriving, begin_ref, bias_held, lse_ref, down_ref, up_sum, reduce_sum,
     part_ref, plane_ref, line_ref,
-    send_sems, recv_sems, hop_send, hop_recv, own_sems, spill_sems, gout_sem, store_sems,
+    send_sems, recv_sems, hop_send, hop_recv, own_sems, spill_sems, load_sems, store_sems,
     leave_sems, arrive_sems, sum_send, sum_recv,
 ):
     nx, ny = plane
     dp = nx * ny * 2
+    inputs = [
+        pltpu.make_async_copy(source, target, input_sems.at[i])
+        for i, (source, target) in enumerate(
+            (
+                (x_in, x_ref), (gain1_in, gain1), (shift1_in, shift1), (seg_in, seg_ref), (small_in, small_ref),
+                (bias_q_in, bias_q), (bias_v_in, bias_v), (out_bias_in, out_bias), (gain2_in, gain2),
+                (shift2_in, shift2), (proj_bias_in, proj_bias), (fc_bias_in, fc_bias),
+            )
+        )
+    ]
     tokens, width = x_ref.shape[1], x_ref.shape[2]
     quads = width // QUAD
-    steps = fc_held.shape[1] // block
+    columns, chunk_units = fc_held.shape[0], fc_held.shape[2]
+    per_chunk = chunk_units // block
+    steps = columns * per_chunk
+    early = (columns - 1) * per_chunk
     top = seq - 1
     mesh_type = pl.DeviceIdType.MESH
     me, place = lax.axis_index("dp"), lax.axis_index("seq")
@@ -111,15 +125,18 @@
     for delta in range(1, seq):
         pl.semaphore_signal(barrier, inc=1, device_id=line_peer(delta), device_id_type=mesh_type)
 
-    sources = [shard_in, wo_in, fc_in, proj_in]
-    targets = [w_held, wo_held, fc_held, proj_held]
+    share = fc_in.shape[1] // dp
+    cut = share // columns
+    tensors = [(w_held, shard_in.shape[0]), (wo_held, wo_in.shape[0])]
+    for j in range(columns):
+        tensors += [(fc_held.at[j], fc_in.shape[0]), (proj_held.at[j], cut)]
 
     def region(t, device, half=None):
-        size = sources[t].shape[0]
+        target, size = tensors[t]
         if half is None:
-            return targets[t].at[pl.ds(pl.multiple_of(device * size, size), size), :]
+            return target.at[pl.ds(pl.multiple_of(device * size, size), size), :]
         part = size // 2
-        return targets[t].at[pl.ds(pl.multiple_of(device * size + half * part, part), part), :]
+        return target.at[pl.ds(pl.multiple_of(device * size + half * part, part), part), :]
 
     def flight(t, slot, part, device):
         return pltpu.make_async_remote_copy(
@@ -128,7 +145,7 @@
         )
 
     flights = {}
-    for t in range(4):
+    for t in range(len(tensors)):
         names = [("x", 0, dx) for dx in range(1, nx)] + [("y", dy, 0) for dy in range(1, ny)]
         names += [(kind, dy, dx) for kind in "ab" for dy in range(1, ny) for dx in range(1, nx)]
         names += [("t", dy, dx) for dy in range(ny) for dx in range(nx)]
@@ -205,20 +222,37 @@
         hidden[row, 0] = (normed * gain1[...] + shift1[...]).astype(BF16)
 
     def gout_load(row):
-        return pltpu.make_async_copy(gout_in.at[row], gout_held, gout_sem)
-
-    own_copies = [pltpu.make_async_copy(sources[t], region(t, me), own_sems.at[t]) for t in range(4)]
-    for copy in own_copies:
+        return pltpu.make_async_copy(gout_in.at[row], gout_held, load_sems.at[0])
+
+    def mix_load(row):
+        return pltpu.make_async_copy(mix_spill.at[row], mix_held, load_sems.at[1])
+
+    own_copies = [
+        pltpu.make_async_copy(source, region(t, me), own_sems.at[t, 0]) for t, source in enumerate((shard_in, wo_in))
+    ]
+    for j in range(columns):
+        for d in range(dp):
+            part = region(2 + 2 * j, me).at[:, d * cut : (d + 1) * cut]
+            source = fc_in.at[:, d * share + j * cut : d * share + (j + 1) * cut]
+            own_copies.append(pltpu.make_async_copy(source, part, own_sems.at[2 + 2 * j, d]))
+        source = proj_in.at[j * cut : (j + 1) * cut, :]
+        own_copies.append(pltpu.make_async_copy(source, region(3 + 2 * j, me), own_sems.at[3 + 2 * j, 0]))
+    for copy in inputs[:5]:
         copy.start()
-    gout_load(0).start()
+    own_copies[0].start()
+    for copy in inputs[5:]:
+        copy.start()
+    for copy in inputs[:3]:
+        copy.wait()
     first_norm(0)
-    turned_ref[...] = small_ref[:8, :].astype(F32).T
+    inputs[4].wait()
+    dq_ref[:, :8] = small_ref[:8, :].astype(F32).T
     pl.semaphore_wait(barrier, dp + seq - 2)
     hop_start(0, 1)
     own_copies[0].wait()
     size = shard_in.shape[0]
     mine = pl.ds(pl.multiple_of(me * size, size), size)
-    reduce_own = turned_ref[mine, :].astype(BF16)
+    reduce_own = dq_ref[mine, :8].astype(BF16)
     up = small_ref[8:, :]
     low_rank = lax.broadcasted_iota(jnp.int32, up.shape, 0) < 4
     for column, rank_up in ((0, jnp.where(low_rank, up, jnp.zeros_like(up))), (2, jnp.where(low_rank, jnp.zeros_like(up), up))):
@@ -227,8 +261,10 @@
         w_held[mine, span] = (w_held[mine, span].astype(F32) + change).astype(BF16)
     wave_one(0)
     for copy in own_copies[1:]:
+        copy.start()
+    gout_load(0).start()
+    for copy in inputs[5:] + inputs[3:4] + own_copies[1:]:
         copy.wait()
-    wave_one(1)
     own_starts(seg_ref, begin_ref, place, seq)
     for row in range(1, rows):
         first_norm(row)
@@ -237,6 +273,9 @@
         def _():
             for row in range(rows):
                 hidden[row, s] = jnp.zeros((tokens, width), BF16)
+    for j in range(columns):
+        for d in range(dp):
+            bias_held[j, :1, d * cut : (d + 1) * cut] = fc_bias[:, d * share + j * cut : d * share + (j + 1) * cut]
     up_sum[...] = jnp.zeros_like(up_sum)
     reduce_sum[...] = jnp.zeros_like(reduce_sum)
 
@@ -251,17 +290,18 @@
     def spills(row):
         return [
             pltpu.make_async_copy(held, spill.at[row], spill_sems.at[i])
+            for i, (held, spill) in enumerate(
+                ((q_held, q_spill), (k_held, k_spill), (v_held, v_spill), (mix_row, mix_spill))
+            )
+        ]
+
+    def reloads(row):
+        return [
+            pltpu.make_async_copy(spill.at[row], held, spill_sems.at[4 + i])
             for i, (held, spill) in enumerate(((q_held, q_spill), (k_held, k_spill), (v_held, v_spill)))
         ]
 
-    def reloads(row):
-        return [
-            pltpu.make_async_copy(spill.at[row], held, spill_sems.at[3 + i])
-            for i, (held, spill) in enumerate(((q_held, q_spill), (k_held, k_spill), (v_held, v_spill)))
-        ]
-
     def attend(row, middle):
-        slot = lax.rem(row, 2)
         query = place * tokens + lax.broadcasted_iota(jnp.int32, (tokens, tokens), 0)
         start = begin_ref[row].T[:, :1].astype(jnp.int32)
         for s in range(seq):
@@ -289,7 +329,7 @@
                 weight = jnp.exp(score - highest)
                 total = jnp.sum(weight, axis=-1, keepdims=True)
                 mixed = dot_nn(weight.astype(BF16), v_held[:, span]) * (1.0 / total)
-                mix_held[slot, :, span] = jnp.where(low, mixed[:tokens], mixed[tokens:]).astype(BF16)
+                mix_row[:, span] = jnp.where(low, mixed[:tokens], mixed[tokens:]).astype(BF16)
                 lse = highest + jnp.log(total)
                 totals = jnp.where(lane == 2 * pair, lse[:tokens], totals)
                 totals = jnp.where(lane == 2 * pair + 1, lse[tokens:], totals)
@@ -329,46 +369,42 @@
         gmid_ref[slot] = gmid_ref[slot] + norm_backward(own_ref[...], normed, inverse, gain1[...])
         grad_store(row).start()
 
-    def feed(row):
-        slot = lax.rem(row, 2)
+    def feed_begin(row):
         gout_load(row).wait()
+        mix_load(row).wait()
 
         @pl.when(row >= 1)
         def _():
             out_store(row - 1).wait()
+            for copy in reloads(row):
+                copy.start()
 
         @pl.when(row >= 2)
         def _():
             grad_store(row - 2).wait()
 
-        middle = x_ref[row].astype(F32) + dot_nn(mix_held[slot], wo_held[...]) + out_bias[...]
-        gmid_ref[slot] = middle
+        middle = x_ref[row].astype(F32) + dot_nn(mix_held[...], wo_held[...]) + out_bias[...]
+        gmid_ref[lax.rem(row, 2)] = middle
         normed, _ = norm_parts(middle)
         h2_ref[...] = (normed * gain2[...] + shift2[...]).astype(BF16)
         acc_ref[...] = jnp.zeros_like(acc_ref)
         back_ref[...] = jnp.zeros_like(back_ref)
 
-        @pl.when(row < rows - 1)
-        def _():
-            for copy in spills(row + 1):
-                copy.wait()
-
-        for copy in reloads(row):
-            copy.start()
-
-        @pl.loop(0, steps)
-        def _(step):
-            part = pl.ds(pl.multiple_of(step * block, block), block)
-            before = dot_nn(h2_ref[...], fc_held[:, part]) + fc_bias[:, part]
-            square = before * before
-            bend = jnp.tanh(GELU_A * before * (1.0 + GELU_B * square))
-            half = 0.5 * (1.0 + bend)
-            slope = half + 0.5 * before * (1.0 - bend * bend) * (GELU_A * (1.0 + 3.0 * GELU_B * square))
-            act = (before * half).astype(BF16)
-            g_before = (dot_nt(gout_held[...], proj_held[part, :]) * slope).astype(BF16)
-            acc_ref[...] += dot_nn(act, proj_held[part, :])
-            back_ref[...] += dot_nt(g_before, fc_held[:, part])
-
+    def feed_step(step):
+        j = step // per_chunk
+        part = pl.ds(pl.multiple_of(lax.rem(step, per_chunk) * block, block), block)
+        before = dot_nn(h2_ref[...], fc_held[j, :, part]) + bias_held[j, :1, part]
+        square = before * before
+        bend = jnp.tanh(GELU_A * before * (1.0 + GELU_B * square))
+        half = 0.5 * (1.0 + bend)
+        slope = half + 0.5 * before * (1.0 - bend * bend) * (GELU_A * (1.0 + 3.0 * GELU_B * square))
+        act = (before * half).astype(BF16)
+        g_before = (dot_nt(gout_held[...], proj_held[j, part, :]) * slope).astype(BF16)
+        acc_ref[...] += dot_nn(act, proj_held[j, part, :])
+        back_ref[...] += dot_nt(g_before, fc_held[j, :, part])
+
+    def feed_end(row):
+        slot = lax.rem(row, 2)
         middle = gmid_ref[slot]
         h2_ref[...] = (middle + acc_ref[...] + proj_bias[...]).astype(BF16)
         out_store(row).start()
@@ -378,7 +414,7 @@
         gmix_ref[...] = dot_nt(g_middle.astype(BF16), wo_held[...]).astype(BF16)
         for pair in range(width // PAIR):
             span = slice(pair * PAIR, (pair + 1) * PAIR)
-            product = (gmix_ref[:, span].astype(F32) * mix_held[slot, :, span].astype(F32)).T
+            product = (gmix_ref[:, span].astype(F32) * mix_held[:, span].astype(F32)).T
             for half in range(2):
                 head = pair * 2 + half
                 delta_ref[head // 4, head % 4 : head % 4 + 1, :] = jnp.sum(
@@ -388,6 +424,7 @@
         @pl.when(row < rows - 1)
         def _():
             gout_load(row + 1).start()
+            mix_load(row + 1).start()
 
     def attend_chunk(row, s):
         query = place * tokens + lax.broadcasted_iota(jnp.int32, (tokens, tokens), 1)
@@ -442,92 +479,145 @@
             up_sum[...] += jnp.where(rank_row, up_grad, 0.0)
             reduce_sum[...] += jnp.where(rank_row, reduce_grad, 0.0)
 
+    def backward(row):
+        feed_end(row)
+
+        @pl.when(row > 0)
+        def _():
+            chain(row - 1, seq - 3)
+
+        for copy in reloads(row):
+            copy.wait()
+        dq_ref[...] = jnp.zeros_like(dq_ref)
+
+        @pl.loop(0, seq - 1)
+        def _(step):
+            s = seq - 1 - step
+
+            @pl.when((row > 0) & (s < seq - 3))
+            def _():
+                chain(row - 1, s)
+
+            @pl.when(place >= s)
+            def _():
+                attend_chunk(row, s)
+
+        chain(row, seq - 2)
+
+        @pl.when(row > 0)
+        def _():
+            chain_end(row - 1)
+
+        attend_chunk(row, 0)
+
+    def both(action, j):
+        if j < columns:
+            action(2 + 2 * j)
+            action(3 + 2 * j)
+
     def before_first():
         arrive(0, 1)
         wave_two(0)
-        wave_one(2)
-        wave_two(1)
+        wave_one(1)
         for s in range(2, seq):
             if s == seq - 1:
                 wave_three(0)
-                wave_three(1)
+                both(wave_one, 0)
+                wave_two(1)
             arrive(0, s)
         wave_end(0)
-        wave_one(3)
+        both(wave_one, 1)
 
     def before_second():
+        both(wave_two, 0)
+        both(wave_one, 2)
         for s in range(1, seq):
+            if s == seq - 1:
+                both(wave_two, 1)
+                wave_three(1)
+                both(wave_three, 0)
             arrive(1, s)
+        both(wave_one, 3)
 
     def amid_second():
-        wave_two(2)
-        wave_two(3)
+        both(wave_two, 2)
+        both(wave_three, 1)
+
+    def before_third():
         arrive(2, 1)
-
-    def after_second():
+        wave_end(1)
+        both(wave_two, 3)
+
+    def amid_early(step):
+        for j in range(columns - 1):
+            @pl.when(step == j * per_chunk)
+            def _():
+                if j == 1:
+                    for s in range(2, seq - 1):
+                        arrive(2, s)
+                if j >= 2:
+                    both(wave_three, j)
+                both(wave_end, j)
+
+    def after_early():
         for s in range(2, seq):
-            arrive(2, s)
-        wave_three(2)
-        wave_three(3)
-        for t in range(1, 4):
-            wave_end(t)
+            if columns < 3 or s == seq - 1:
+                arrive(2, s)
+
+    def amid_third():
+        if columns > 2:
+            both(wave_three, columns - 1)
 
     def before_later(row):
         for s in range(1, seq):
             arrive(row, s)
 
-    @pl.loop(0, rows + 1)
+    last = rows - 1
+
+    @pl.loop(0, 2 * rows)
     def _(turn):
+        row = jnp.maximum(turn - rows, 0)
         for index in range(rows):
-            if index != 2:
-                action = before_first if index == 0 else before_second if index == 1 else partial(before_later, index)
-                pl.when(turn == index)(action)
+            befores = (before_first, before_second, before_third)
+            pl.when(turn == index)(befores[index] if index < 3 else partial(before_later, index))
+
+        @pl.when((turn > 0) & (turn <= rows))
+        def _():
+            for copy in spills(turn - 1):
+                copy.wait()
 
         @pl.when(turn == 1)
         def _():
-            for copy in spills(0):
-                copy.wait()
+            mix_load(0).start()
+
+        @pl.when(turn == rows)
+        def _():
+            for copy in reloads(0):
+                copy.start()
+            both(wave_end, columns - 1)
+
+        pl.when((turn == last) | (turn > rows))(partial(feed_begin, row))
+
+        @pl.when(turn >= last)
+        def _():
+            @pl.loop(jnp.where(turn == rows, early, 0), jnp.where(turn == last, early, steps))
+            def _(step):
+                pl.when(turn == last)(partial(amid_early, step))
+                feed_step(step)
+
+        pl.when(turn == 2)(after_early)
+
+        def middle():
+            pl.when(turn == 1)(amid_second)
+            pl.when(turn == 2)(amid_third)
 
         @pl.when(turn < rows)
         def _():
-            attend(turn, lambda: pl.when(turn == 1)(amid_second))
+            attend(turn, middle)
             for copy in spills(turn):
                 copy.start()
 
-        pl.when(turn == 1)(after_second)
-
-        @pl.when(turn > 0)
-        def _():
-            row = turn - 1
-            feed(row)
-
-            @pl.when(row > 0)
-            def _():
-                chain(row - 1, seq - 3)
-
-            for copy in reloads(row):
-                copy.wait()
-            dq_ref[...] = jnp.zeros_like(dq_ref)
-
-            @pl.loop(0, seq - 1)
-            def _(step):
-                s = seq - 1 - step
-
-                @pl.when((row > 0) & (s < seq - 3))
-                def _():
-                    chain(row - 1, s)
-
-                @pl.when(place >= s)
-                def _():
-                    attend_chunk(row, s)
-
-            chain(row, seq - 2)
-
-            @pl.when(row > 0)
-            def _():
-                chain_end(row - 1)
-
-            attend_chunk(row, 0)
+        pl.when(turn >= rows)(partial(backward, row))
 
     def send(source, target, slot, device):
         copy = pltpu.make_async_remote_copy(
@@ -545,7 +635,6 @@
             line = (half * lanes + block_lane) * 8
             part_ref[line // piece, line % piece : line % piece + 8, :] = total[:, block_lane * PAIR : (block_lane + 1) * PAIR]
     copies = [send(part_ref.at[lax.rem(me + delta, dp)], plane_ref.at[delta], delta, peer(delta)) for delta in range(1, dp)]
-    last = rows - 1
     chain(last, seq - 3)
     total = part_ref[me]
     for delta in range(1, dp):
@@ -590,6 +679,7 @@
     quads = width // QUAD
     piece = max(8, 16 * width // (PAIR * dp))
     nx, ny = plane
+    columns = max(1, min(4, hidden_units // (dp * PAIR)))
     flights = nx - 1 + ny - 1 + 2 * (nx - 1) * (ny - 1) + nx * ny
     sums = 2 * dp + seq
     anywhere = pl.BlockSpec(memory_space=pl.ANY)
@@ -604,27 +694,29 @@
 
     result = pl.pallas_call(
         partial(block_kernel, plane, seq, rows, block),
-        in_specs=[vmem] * 12 + [anywhere] * 5,
-        out_specs=[anywhere, anywhere, vmem] + [anywhere] * 3,
+        in_specs=[anywhere] * 17,
+        out_specs=[anywhere, anywhere, vmem] + [anywhere] * 4,
         out_shape=[
             shape(rows, tokens, width), shape(rows, tokens, width, dtype=F32), shape(dp, piece, PAIR, dtype=F32),
             shape(rows, tokens, width), shape(rows, length, width), shape(rows, length, width),
+            shape(rows, tokens, width),
         ],
         scratch_shapes=[
-            held(width, 3 * width), held(width, width), held(width, hidden_units), held(hidden_units, width),
+            *(held(*a.shape, dtype=a.dtype) for a in (x, seg, small, *vectors)), dma((12,)),
+            held(width, 3 * width), held(width, width), held(columns, width, hidden_units // columns), held(columns, hidden_units // columns, width),
             held(rows, seq, tokens, width), held(tokens, width), held(length, width), held(length, width),
-            held(2, tokens, width), held(tokens, width),
+            held(tokens, width), held(tokens, width), held(tokens, width),
             held(tokens, width), held(tokens, width),
             held(tokens, width, dtype=F32), held(tokens, width, dtype=F32), held(2, tokens, width, dtype=F32),
             held(tokens, width, dtype=F32), held(tokens, length, dtype=F32), held(quads, 8, tokens, dtype=F32),
             held(width, tokens, dtype=F32), held(tokens, 2 * width),
             held(seq - 1, tokens, width), held(rows, seq - 1, tokens, width),
-            held(rows, 8, tokens, dtype=F32), held(width, 8, dtype=F32),
+            held(rows, 8, tokens, dtype=F32), held(columns, 8, hidden_units // columns, dtype=F32),
             held(rows, quads, 8, tokens, dtype=F32), held(rows, 8, length),
             held(8, width, dtype=F32), held(8, width, dtype=F32),
             held(dp, piece, PAIR, dtype=F32), held(dp, piece, PAIR, dtype=F32), held(seq, piece, PAIR, dtype=F32),
-            dma((4, flights)), dma((4, flights)), dma((rows, seq - 1)), dma((rows, seq - 1)),
-            dma((4,)), dma((6,)), dma, dma((3,)),
+            dma((2 + 2 * columns, flights)), dma((2 + 2 * columns, flights)), dma((rows, seq - 1)), dma((rows, seq - 1)),
+            dma((2 + 2 * columns, dp)), dma((7,)), dma((2,)), dma((3,)),
             dma((seq - 1,)), dma((rows, seq - 1)), dma((sums,)), dma((sums,)),
         ],
         compiler_params=pltpu.CompilerParams(

time: 283 us -> 257 us (0.908)
  Pallas kernels: 274 us -> 249 us
    pallas_call x1, Pallas kernels: 274 us -> 249 us  [run_block(): pl.pallas_call(partial(block_kernel, plane, seq, rows, block), in_specs=[...]
where the time goes in v6:
time: 257 us
  Pallas kernels  249 us (97%)
  local copies, waits for them, and re-layouts  5.96 us (2%)
    pallas_call x1, Pallas kernels, run_block(): pl.pallas_call(partial(block_kernel, plane, seq, rows, block), in_specs=[...  249 us

profile of v6, /device:TPU:0, one launch (start us, length us, event | category | flops | bytes accessed | tf_op | source)
XLA Modules:
  0.0 257.2 jit_solution(2267425066080598284)
XLA Ops:
  0.6 1.4 pad_maximum_fusion.small_in
  2.0 249.2 %block.1 = (bf16[3,256,1024]{2,1,0:T(8,128)(2,1)}, f32[3,256,1024]{2,1,0:T(8,128)}, f32[8,16,128]{2,1,0:T(8,128)}, bf16[3,256,1024]{2,1,0:T(8,128)(2,1)}, bf16[3...) custom-call(bf16[3,256,1024]{2,1,0:T(8,128)(2,1)} %x_in.1, ...), custom_call_target="tpu_custom_call" | custom-call | tf_op jit(solution)/shard_map/block/pallas_call | solution.py:695
  251.2 1.5 slice_bitcast_fusion
  252.7 0.0 copy-start
  252.7 2.8 %copy.30 = bf16[3,256,1024]{2,1,0:T(8,128)(2,1)} copy(bf16[3,256,1024]{2,1,0:T(8,128)(2,1)} %get-tuple-element.22) | data formatting | bytes 3145728
  255.5 0.0 copy-done
  255.5 1.7 copy.31
Async XLA Ops:
  252.7 2.8 %copy-start = (f32[3,256,1024]{2,1,0:T(8,128)S(1)}, f32[3,256,1024]{2,1,0:T(8,128)}, u32[]{:S(2)}) copy-start(f32[3,256,1024]{2,1,0:T(8,128)} %get-tuple-element.23) | copy-start | bytes 9437188

commit v7 on v6

--- a/solution.py
+++ b/solution.py
@@ -65,13 +65,13 @@
     plane, seq, rows, block,
     x_in, seg_in, small_in, gain1_in, shift1_in, bias_q_in, bias_v_in, out_bias_in, gain2_in, shift2_in, proj_bias_in,
     fc_bias_in, shard_in, wo_in, fc_in, proj_in, gout_in,
-    out_out, grad_out, sum_out, q_spill, k_spill, v_spill, mix_spill,
+    out_out, grad_out, sum_out, q_spill, k_spill, v_spill, mix_spill, gmix_spill, dq_spill,
     x_ref, seg_ref, small_ref, gain1, shift1, bias_q, bias_v, out_bias, gain2, shift2, proj_bias, fc_bias, input_sems,
     w_held, wo_held, fc_held, proj_held, hidden, q_held, k_held, v_held, mix_row, mix_held, gout_held,
     gmix_ref, h2_ref, acc_ref, back_ref, gmid_ref, own_ref, mask_ref, delta_ref, dq_ref, dkv_ref,
     leaving, arriving, begin_ref, bias_held, lse_ref, down_ref, up_sum, reduce_sum,
     part_ref, plane_ref, line_ref,
-    send_sems, recv_sems, hop_send, hop_recv, own_sems, spill_sems, load_sems, store_sems,
+    send_sems, recv_sems, hop_send, hop_recv, own_sems, spill_sems, load_sems, late_sems, store_sems,
     leave_sems, arrive_sems, sum_send, sum_recv,
 ):
     nx, ny = plane
@@ -91,7 +91,8 @@
     columns, chunk_units = fc_held.shape[0], fc_held.shape[2]
     per_chunk = chunk_units // block
     steps = columns * per_chunk
-    early = (columns - 1) * per_chunk
+    last = rows - 1
+    late_slot = 1 - last % 2
     top = seq - 1
     mesh_type = pl.DeviceIdType.MESH
     me, place = lax.axis_index("dp"), lax.axis_index("seq")
@@ -340,9 +341,42 @@
     def out_store(row):
         return pltpu.make_async_copy(h2_ref, out_out.at[row], store_sems.at[0])
 
-    def grad_store(row):
-        slot = lax.rem(row, 2)
+    def grad_store(row, slot):
         return pltpu.make_async_copy(gmid_ref.at[slot], grad_out.at[row], store_sems.at[1 + slot])
+
+    def late_spills(row):
+        return [
+            pltpu.make_async_copy(gmix_ref, gmix_spill.at[row], late_sems.at[0]),
+            pltpu.make_async_copy(acc_ref, dq_spill.at[row], late_sems.at[1]),
+        ]
+
+    def late_loads(row):
+        q_room, gmix_room = ((mix_row, mix_held), (gout_held, h2_ref))[row]
+        lines = slice((2 + row) * tokens, (3 + row) * tokens)
+        return [
+            pltpu.make_async_copy(gmix_spill.at[row], gmix_room, late_sems.at[2 + 4 * row]),
+            pltpu.make_async_copy(q_spill.at[row], q_room, late_sems.at[3 + 4 * row]),
+            pltpu.make_async_copy(k_spill.at[row, :tokens, :], k_held.at[lines, :], late_sems.at[4 + 4 * row]),
+            pltpu.make_async_copy(v_spill.at[row, :tokens, :], v_held.at[lines, :], late_sems.at[5 + 4 * row]),
+        ]
+
+    def dq_load(row):
+        return pltpu.make_async_copy(dq_spill.at[row], acc_ref, late_sems.at[10])
+
+    def gmid_load(row):
+        return pltpu.make_async_copy(grad_out.at[row], gmid_ref.at[late_slot], late_sems.at[11])
+
+    def late_ready(row):
+        for copy in late_loads(row):
+            copy.wait()
+        dq_load(row).wait()
+        q_room, gmix_room = ((mix_row, mix_held), (gout_held, h2_ref))[row]
+        lines = slice((2 + row) * tokens, (3 + row) * tokens)
+        q_held[...] = q_room[...]
+        gmix_ref[...] = gmix_room[...]
+        k_held[:tokens, :] = k_held[lines, :]
+        v_held[:tokens, :] = v_held[lines, :]
+        dq_ref[...] = acc_ref[...].T
 
     def leave(row, s):
         return pltpu.make_async_remote_copy(
@@ -358,35 +392,45 @@
             leaving[s - 1] = (leaving[s - 1].astype(F32) + arriving[row, s].astype(F32)).astype(BF16)
             leave(row, s).start()
 
-    def chain_end(row):
+    def chain_end(row, slot, own):
         @pl.when(place < top)
         def _():
             leave(row, 1).wait_recv()
-            own_ref[...] += arriving[row, 0].astype(F32)
-
-        slot = lax.rem(row, 2)
+            own[...] += arriving[row, 0].astype(F32)
+
         normed, inverse = norm_parts(x_ref[row].astype(F32))
-        gmid_ref[slot] = gmid_ref[slot] + norm_backward(own_ref[...], normed, inverse, gain1[...])
-        grad_store(row).start()
+        gmid_ref[slot] = gmid_ref[slot] + norm_backward(own[...], normed, inverse, gain1[...])
+        grad_store(row, slot).start()
 
     def feed_begin(row):
         gout_load(row).wait()
-        mix_load(row).wait()
+
+        @pl.when(row < 2)
+        def _():
+            mix_load(row).wait()
 
         @pl.when(row >= 1)
         def _():
             out_store(row - 1).wait()
+
+        @pl.when(row == 1)
+        def _():
             for copy in reloads(row):
                 copy.start()
 
         @pl.when(row >= 2)
         def _():
-            grad_store(row - 2).wait()
+            grad_store(row - 2, lax.rem(row, 2)).wait()
 
         middle = x_ref[row].astype(F32) + dot_nn(mix_held[...], wo_held[...]) + out_bias[...]
         gmid_ref[lax.rem(row, 2)] = middle
         normed, _ = norm_parts(middle)
         h2_ref[...] = (normed * gain2[...] + shift2[...]).astype(BF16)
+
+        @pl.when(row > 0)
+        def _():
+            late_spills(row - 1)[1].wait()
+
         acc_ref[...] = jnp.zeros_like(acc_ref)
         back_ref[...] = jnp.zeros_like(back_ref)
 
@@ -411,19 +455,31 @@
         normed, inverse = norm_parts(middle)
         g_middle = gout_held[...].astype(F32) + norm_backward(back_ref[...], normed, inverse, gain2[...])
         gmid_ref[slot] = g_middle
+
+        @pl.when(row < last)
+        def _():
+            grad_store(row, slot).start()
+
+        @pl.when(row > 0)
+        def _():
+            late_spills(row - 1)[0].wait()
+
         gmix_ref[...] = dot_nt(g_middle.astype(BF16), wo_held[...]).astype(BF16)
         for pair in range(width // PAIR):
             span = slice(pair * PAIR, (pair + 1) * PAIR)
             product = (gmix_ref[:, span].astype(F32) * mix_held[:, span].astype(F32)).T
             for half in range(2):
                 head = pair * 2 + half
-                delta_ref[head // 4, head % 4 : head % 4 + 1, :] = jnp.sum(
+                delta_ref[row, head // 4, head % 4 : head % 4 + 1, :] = jnp.sum(
                     product[half * HEAD : (half + 1) * HEAD], axis=0, keepdims=True
                 )
 
         @pl.when(row < rows - 1)
         def _():
             gout_load(row + 1).start()
+
+        @pl.when(row == 0)
+        def _():
             mix_load(row + 1).start()
 
     def attend_chunk(row, s):
@@ -441,7 +497,7 @@
             head = 2 * (pair % 2)
             lse, inner = [
                 jnp.concatenate([ref[head : head + 1, :], ref[head + 1 : head + 2, :]], axis=1)
-                for ref in (lse_ref.at[row, pair // 2], delta_ref.at[pair // 2])
+                for ref in (lse_ref.at[row, pair // 2], delta_ref.at[row, pair // 2])
             ]
             prob = jnp.exp(dot_nt(k_pair, q_both) + mask_ref[:, : 2 * tokens] - lse)
             g_score = (prob * (dot_nt(v_pair, g_both) - inner)).astype(BF16)
@@ -486,8 +542,11 @@
         def _():
             chain(row - 1, seq - 3)
 
-        for copy in reloads(row):
-            copy.wait()
+        @pl.when(row < 2)
+        def _():
+            for copy in reloads(row):
+                copy.wait()
+
         dq_ref[...] = jnp.zeros_like(dq_ref)
 
         @pl.loop(0, seq - 1)
@@ -504,11 +563,11 @@
 
         chain(row, seq - 2)
 
-        @pl.when(row > 0)
-        def _():
-            chain_end(row - 1)
-
-        attend_chunk(row, 0)
+        @pl.when(row < last)
+        def _():
+            acc_ref[...] = dq_ref[...].T
+            for copy in late_spills(row):
+                copy.start()
 
     def both(action, j):
         if j < columns:
@@ -543,81 +602,105 @@
         both(wave_two, 2)
         both(wave_three, 1)
 
-    def before_third():
+    def before_feed():
         arrive(2, 1)
         wave_end(1)
         both(wave_two, 3)
-
-    def amid_early(step):
-        for j in range(columns - 1):
+        for copy in spills(1):
+            copy.wait()
+        for copy in reloads(0):
+            copy.start()
+
+    def amid_feed(step):
+        for j in range(columns):
             @pl.when(step == j * per_chunk)
             def _():
-                if j == 1:
+                if j == min(1, columns - 1):
                     for s in range(2, seq - 1):
                         arrive(2, s)
-                if j >= 2:
+                if j >= 2 or j == columns - 1:
                     both(wave_three, j)
                 both(wave_end, j)
 
-    def after_early():
-        for s in range(2, seq):
-            if columns < 3 or s == seq - 1:
-                arrive(2, s)
-
-    def amid_third():
-        if columns > 2:
-            both(wave_three, columns - 1)
+    def before_third():
+        arrive(2, seq - 1)
 
     def before_later(row):
         for s in range(1, seq):
             arrive(row, s)
 
-    last = rows - 1
-
     @pl.loop(0, 2 * rows)
     def _(turn):
-        row = jnp.maximum(turn - rows, 0)
+        attending = (turn < 2) | ((turn >= 4) & (lax.rem(turn, 2) == 0))
+        attend_row = jnp.where(turn < 2, turn, turn // 2)
+        row = jnp.where(turn < 4, jnp.maximum(turn - 2, 0), (turn - 1) // 2)
         for index in range(rows):
             befores = (before_first, before_second, before_third)
-            pl.when(turn == index)(befores[index] if index < 3 else partial(before_later, index))
-
-        @pl.when((turn > 0) & (turn <= rows))
-        def _():
-            for copy in spills(turn - 1):
+            action = befores[index] if index < 3 else partial(before_later, index)
+            pl.when(turn == (index if index < 2 else 2 * index))(action)
+
+        pl.when(turn == 2)(before_feed)
+
+        @pl.when(turn == 1)
+        def _():
+            for copy in spills(0):
                 copy.wait()
-
+            mix_load(0).start()
+
+        @pl.when(attending)
+        def _():
+            attend(attend_row, lambda: pl.when(turn == 1)(amid_second))
+
+            @pl.when(turn < 2)
+            def _():
+                for copy in spills(turn):
+                    copy.start()
+
+            @pl.when(turn >= 2)
+            def _():
+                mix_held[...] = mix_row[...]
+
+        @pl.when(jnp.logical_not(attending))
+        def _():
+            feed_begin(row)
+
+            @pl.loop(0, steps)
+            def _(step):
+                pl.when(turn == 2)(partial(amid_feed, step))
+                feed_step(step)
+
+            backward(row)
+
+    grad_store(last - 1, late_slot).wait()
+    out_store(last).wait()
+    for copy in [gmid_load(0), dq_load(0)] + late_loads(0) + late_loads(1):
+        copy.start()
+
+    @pl.loop(0, 3)
+    def _(turn):
         @pl.when(turn == 1)
         def _():
-            mix_load(0).start()
-
-        @pl.when(turn == rows)
-        def _():
-            for copy in reloads(0):
-                copy.start()
-            both(wave_end, columns - 1)
-
-        pl.when((turn == last) | (turn > rows))(partial(feed_begin, row))
-
-        @pl.when(turn >= last)
-        def _():
-            @pl.loop(jnp.where(turn == rows, early, 0), jnp.where(turn == last, early, steps))
-            def _(step):
-                pl.when(turn == last)(partial(amid_early, step))
-                feed_step(step)
-
-        pl.when(turn == 2)(after_early)
-
-        def middle():
-            pl.when(turn == 1)(amid_second)
-            pl.when(turn == 2)(amid_third)
-
-        @pl.when(turn < rows)
-        def _():
-            attend(turn, middle)
-            for copy in spills(turn):
-                copy.start()
-
-        pl.when(turn >= rows)(partial(backward, row))
+            late_ready(0)
+            dq_load(1).start()
+
+        @pl.when(turn == 2)
+        def _():
+            late_ready(1)
+            grad_store(0, late_slot).wait()
+            gmid_load(1).start()
+
+        attend_chunk(jnp.where(turn == 0, last, turn - 1), 0)
+
+        @pl.when(turn == 0)
+        def _():
+            back_ref[...] = own_ref[...]
+
+        @pl.when(turn > 0)
+        def _():
+            gmid_load(turn - 1).wait()
+            chain_end(turn - 1, late_slot, own_ref)
+
+        pl.when(turn == 1)(partial(chain, last, seq - 3))
 
     def send(source, target, slot, device):
         copy = pltpu.make_async_remote_copy(
@@ -635,7 +718,6 @@
             line = (half * lanes + block_lane) * 8
             part_ref[line // piece, line % piece : line % piece + 8, :] = total[:, block_lane * PAIR : (block_lane + 1) * PAIR]
     copies = [send(part_ref.at[lax.rem(me + delta, dp)], plane_ref.at[delta], delta, peer(delta)) for delta in range(1, dp)]
-    chain(last, seq - 3)
     total = part_ref[me]
     for delta in range(1, dp):
         copies[delta - 1].wait()
@@ -651,7 +733,7 @@
     copies = [send(sum_out.at[me], sum_out.at[me], dp + seq + delta, peer(delta)) for delta in range(1, dp)]
     for s in range(seq - 4, 0, -1):
         chain(last, s)
-    chain_end(last)
+    chain_end(last, last % 2, back_ref)
     for copy in copies:
         copy.wait()
     for copy in flights.values():
@@ -665,13 +747,13 @@
         @pl.when(place >= s)
         def _():
             leave(last, s).wait_send()
-    out_store(last).wait()
-    for row in range(max(0, rows - 2), rows):
-        grad_store(row).wait()
+    grad_store(last - 1, late_slot).wait()
+    grad_store(last, last % 2).wait()
 
 
 def run_block(plane, seq, x, seg, small, vectors, shards, gout):
     rows, tokens, width = x.shape
+    assert rows == 3
     length = seq * tokens
     dp = plane[0] * plane[1] * 2
     hidden_units = shards[2].shape[1]
@@ -695,11 +777,11 @@
     result = pl.pallas_call(
         partial(block_kernel, plane, seq, rows, block),
         in_specs=[anywhere] * 17,
-        out_specs=[anywhere, anywhere, vmem] + [anywhere] * 4,
+        out_specs=[anywhere, anywhere, vmem] + [anywhere] * 6,
         out_shape=[
             shape(rows, tokens, width), shape(rows, tokens, width, dtype=F32), shape(dp, piece, PAIR, dtype=F32),
             shape(rows, tokens, width), shape(rows, length, width), shape(rows, length, width),
-            shape(rows, tokens, width),
+            shape(rows, tokens, width), shape(rows, tokens, width), shape(rows, tokens, width, dtype=F32),
         ],
         scratch_shapes=[
             *(held(*a.shape, dtype=a.dtype) for a in (x, seg, small, *vectors)), dma((12,)),
@@ -708,7 +790,7 @@
             held(tokens, width), held(tokens, width), held(tokens, width),
             held(tokens, width), held(tokens, width),
             held(tokens, width, dtype=F32), held(tokens, width, dtype=F32), held(2, tokens, width, dtype=F32),
-            held(tokens, width, dtype=F32), held(tokens, length, dtype=F32), held(quads, 8, tokens, dtype=F32),
+            held(tokens, width, dtype=F32), held(tokens, length, dtype=F32), held(rows, quads, 8, tokens, dtype=F32),
             held(width, tokens, dtype=F32), held(tokens, 2 * width),
             held(seq - 1, tokens, width), held(rows, seq - 1, tokens, width),
             held(rows, 8, tokens, dtype=F32), held(columns, 8, hidden_units // columns, dtype=F32),
@@ -716,7 +798,7 @@
             held(8, width, dtype=F32), held(8, width, dtype=F32),
             held(dp, piece, PAIR, dtype=F32), held(dp, piece, PAIR, dtype=F32), held(seq, piece, PAIR, dtype=F32),
             dma((2 + 2 * columns, flights)), dma((2 + 2 * columns, flights)), dma((rows, seq - 1)), dma((rows, seq - 1)),
-            dma((2 + 2 * columns, dp)), dma((7,)), dma((2,)), dma((3,)),
+            dma((2 + 2 * columns, dp)), dma((7,)), dma((2,)), dma((12,)), dma((3,)),
             dma((seq - 1,)), dma((rows, seq - 1)), dma((sums,)), dma((sums,)),
         ],
         compiler_params=pltpu.CompilerParams(

time: 257 us -> 251 us (0.977)
  Pallas kernels: 249 us -> 243 us
    pallas_call x1, Pallas kernels: 249 us -> 243 us  [run_block(): pl.pallas_call(partial(block_kernel, plane, seq, rows, block), in_specs=[...]
where the time goes in v7:
time: 251 us
  Pallas kernels  243 us (97%)
  local copies, waits for them, and re-layouts  5.99 us (2%)
    pallas_call x1, Pallas kernels, run_block(): pl.pallas_call(partial(block_kernel, plane, seq, rows, block), in_specs=[...  243 us

profile of v7, /device:TPU:0, one launch (start us, length us, event | category | flops | bytes accessed | tf_op | source)
XLA Modules:
  0.0 251.1 jit_solution(16413954319915160084)
XLA Ops:
  0.6 1.4 pad_maximum_fusion.small_in
  2.0 243.1 %block.1 = (bf16[3,256,1024]{2,1,0:T(8,128)(2,1)}, f32[3,256,1024]{2,1,0:T(8,128)}, f32[8,16,128]{2,1,0:T(8,128)}, bf16[3,256,1024]{2,1,0:T(8,128)(2,1)}, bf16[3...) custom-call(bf16[3,256,1024]{2,1,0:T(8,128)(2,1)} %x_in.1, ...), custom_call_target="tpu_custom_call" | custom-call | tf_op jit(solution)/shard_map/block/pallas_call | solution.py:777
  245.1 1.5 slice_bitcast_fusion
  246.6 0.0 copy-start
  246.6 2.8 %copy.30 = bf16[3,256,1024]{2,1,0:T(8,128)(2,1)} copy(bf16[3,256,1024]{2,1,0:T(8,128)(2,1)} %get-tuple-element.22) | data formatting | bytes 3145728
  249.4 0.0 copy-done
  249.4 1.7 copy.31
Async XLA Ops:
  246.6 2.8 %copy-start = (f32[3,256,1024]{2,1,0:T(8,128)S(1)}, f32[3,256,1024]{2,1,0:T(8,128)}, u32[]{:S(2)}) copy-start(f32[3,256,1024]{2,1,0:T(8,128)} %get-tuple-element.23) | copy-start | bytes 9437188

commit v8 on v7

--- a/solution.py
+++ b/solution.py
@@ -63,10 +63,10 @@
 
 def block_kernel(
     plane, seq, rows, block,
-    x_in, seg_in, small_in, gain1_in, shift1_in, bias_q_in, bias_v_in, out_bias_in, gain2_in, shift2_in, proj_bias_in,
+    x_in, seg_in, reduce_q_in, reduce_v_in, up_q_in, up_v_in, gain1_in, shift1_in, bias_q_in, bias_v_in, out_bias_in, gain2_in, shift2_in, proj_bias_in,
     fc_bias_in, shard_in, wo_in, fc_in, proj_in, gout_in,
     out_out, grad_out, sum_out, q_spill, k_spill, v_spill, mix_spill, gmix_spill, dq_spill,
-    x_ref, seg_ref, small_ref, gain1, shift1, bias_q, bias_v, out_bias, gain2, shift2, proj_bias, fc_bias, input_sems,
+    x_ref, seg_ref, reduce_q, reduce_v, up_q, up_v, gain1, shift1, bias_q, bias_v, out_bias, gain2, shift2, proj_bias, fc_bias, small_ref, input_sems,
     w_held, wo_held, fc_held, proj_held, hidden, q_held, k_held, v_held, mix_row, mix_held, gout_held,
     gmix_ref, h2_ref, acc_ref, back_ref, gmid_ref, own_ref, mask_ref, delta_ref, dq_ref, dkv_ref,
     leaving, arriving, begin_ref, bias_held, lse_ref, down_ref, up_sum, reduce_sum,
@@ -80,7 +80,8 @@
         pltpu.make_async_copy(source, target, input_sems.at[i])
         for i, (source, target) in enumerate(
             (
-                (x_in, x_ref), (gain1_in, gain1), (shift1_in, shift1), (seg_in, seg_ref), (small_in, small_ref),
+                (x_in, x_ref), (gain1_in, gain1), (shift1_in, shift1), (seg_in, seg_ref),
+                (reduce_q_in, reduce_q), (reduce_v_in, reduce_v), (up_q_in, up_q), (up_v_in, up_v),
                 (bias_q_in, bias_q), (bias_v_in, bias_v), (out_bias_in, out_bias), (gain2_in, gain2),
                 (shift2_in, shift2), (proj_bias_in, proj_bias), (fc_bias_in, fc_bias),
             )
@@ -238,15 +239,18 @@
             own_copies.append(pltpu.make_async_copy(source, part, own_sems.at[2 + 2 * j, d]))
         source = proj_in.at[j * cut : (j + 1) * cut, :]
         own_copies.append(pltpu.make_async_copy(source, region(3 + 2 * j, me), own_sems.at[3 + 2 * j, 0]))
-    for copy in inputs[:5]:
+    for copy in inputs[:8]:
         copy.start()
     own_copies[0].start()
-    for copy in inputs[5:]:
+    for copy in inputs[8:]:
         copy.start()
     for copy in inputs[:3]:
         copy.wait()
     first_norm(0)
-    inputs[4].wait()
+    for copy in inputs[4:8]:
+        copy.wait()
+    small_ref[:8, :] = jnp.concatenate([reduce_q[...].astype(F32), reduce_v[...].astype(F32)], axis=0).astype(BF16)
+    small_ref[8:, :] = jnp.concatenate([up_q[...].astype(F32), up_v[...].astype(F32)], axis=0).astype(BF16)
     dq_ref[:, :8] = small_ref[:8, :].astype(F32).T
     pl.semaphore_wait(barrier, dp + seq - 2)
     hop_start(0, 1)
@@ -264,7 +268,7 @@
     for copy in own_copies[1:]:
         copy.start()
     gout_load(0).start()
-    for copy in inputs[5:] + inputs[3:4] + own_copies[1:]:
+    for copy in inputs[8:] + inputs[3:4] + own_copies[1:]:
         copy.wait()
     own_starts(seg_ref, begin_ref, place, seq)
     for row in range(1, rows):
@@ -482,7 +486,7 @@
         def _():
             mix_load(row + 1).start()
 
-    def attend_chunk(row, s):
+    def attend_chunk(row, s, summed=None):
         query = place * tokens + lax.broadcasted_iota(jnp.int32, (tokens, tokens), 1)
         key = (place - s) * tokens + lax.broadcasted_iota(jnp.int32, (tokens, tokens), 0)
         start = begin_ref[row, :1, :].astype(jnp.int32)
@@ -509,31 +513,31 @@
                 part = g_score[:, half * tokens : (half + 1) * tokens]
                 dq_ref[lines, :] += dot_nn(k_turned[half * HEAD : (half + 1) * HEAD], part)
 
-        grad = dot_nt(dkv_ref[...], w_held[:, width:])
         dv = dkv_ref[:, width:]
         up_grad = dot_nn(down_ref[row, :, rows_s], dv)
         g_down = dot_nt(small_ref[8:, :], dv).astype(BF16)
         reduce_grad = dot_nn(g_down, hidden[row, s])
         up_sum[...] += jnp.where(rank_row, 0.0, up_grad)
         reduce_sum[...] += jnp.where(rank_row, 0.0, reduce_grad)
-        if not isinstance(s, int):
+        if summed is None:
             @pl.when(row > 0)
             def _():
                 leave(row - 1, s).wait_send()
 
-            leaving[s - 1] = grad.astype(BF16)
+            leaving[s - 1] = dot_nt(dkv_ref[...], w_held[:, width:]).astype(BF16)
 
             @pl.when(place == top)
             def _():
                 leave(row, s).start()
         else:
             dq = (dq_ref[...].T * (HEAD**-0.5)).astype(BF16)
-            own_ref[...] = grad + dot_nt(dq, w_held[:, :width])
             up_grad = dot_nn(down_ref[row, :, rows_s], dq)
             g_down = dot_nt(small_ref[8:, :], dq).astype(BF16)
             reduce_grad = dot_nn(g_down, hidden[row, s])
             up_sum[...] += jnp.where(rank_row, up_grad, 0.0)
             reduce_sum[...] += jnp.where(rank_row, reduce_grad, 0.0)
+            summed()
+            own_ref[...] = dot_nt(dkv_ref[...], w_held[:, width:]) + dot_nt(dq, w_held[:, :width])
 
     def backward(row):
         feed_end(row)
@@ -671,6 +675,30 @@
 
             backward(row)
 
+    def sum_copy(source, target, slot, device):
+        return pltpu.make_async_remote_copy(
+            src_ref=source, dst_ref=target, send_sem=sum_send.at[slot], recv_sem=sum_recv.at[slot],
+            device_id=device, device_id_type=mesh_type,
+        )
+
+    def piece_copies():
+        return [
+            sum_copy(part_ref.at[lax.rem(me + delta, dp)], plane_ref.at[delta], delta, peer(delta))
+            for delta in range(1, dp)
+        ]
+
+    piece = part_ref.shape[1]
+    lanes = width // PAIR
+
+    def start_sums():
+        part_ref[...] = jnp.zeros_like(part_ref)
+        for half, total in enumerate((reduce_sum[...] * ADAPTER_SCALE, up_sum[...])):
+            for block_lane in range(lanes):
+                line = (half * lanes + block_lane) * 8
+                part_ref[line // piece, line % piece : line % piece + 8, :] = total[:, block_lane * PAIR : (block_lane + 1) * PAIR]
+        for copy in piece_copies():
+            copy.start()
+
     grad_store(last - 1, late_slot).wait()
     out_store(last).wait()
     for copy in [gmid_load(0), dq_load(0)] + late_loads(0) + late_loads(1):
@@ -689,7 +717,7 @@
             grad_store(0, late_slot).wait()
             gmid_load(1).start()
 
-        attend_chunk(jnp.where(turn == 0, last, turn - 1), 0)
+        attend_chunk(jnp.where(turn == 0, last, turn - 1), 0, lambda: pl.when(turn == 2)(start_sums))
 
         @pl.when(turn == 0)
         def _():
@@ -702,35 +730,25 @@
 
         pl.when(turn == 1)(partial(chain, last, seq - 3))
 
-    def send(source, target, slot, device):
-        copy = pltpu.make_async_remote_copy(
-            src_ref=source, dst_ref=target, send_sem=sum_send.at[slot], recv_sem=sum_recv.at[slot],
-            device_id=device, device_id_type=mesh_type,
-        )
+    total = part_ref[me]
+    for delta, copy in enumerate(piece_copies()):
+        copy.wait()
+        total = total + plane_ref[delta + 1]
+    line_ref[place] = total
+    line_copies = [
+        sum_copy(line_ref.at[place], line_ref.at[place], dp + delta, line_peer(delta)) for delta in range(1, seq)
+    ]
+    for copy in line_copies:
         copy.start()
-        return copy
-
-    piece = part_ref.shape[1]
-    lanes = width // PAIR
-    part_ref[...] = jnp.zeros_like(part_ref)
-    for half, total in enumerate((reduce_sum[...] * ADAPTER_SCALE, up_sum[...])):
-        for block_lane in range(lanes):
-            line = (half * lanes + block_lane) * 8
-            part_ref[line // piece, line % piece : line % piece + 8, :] = total[:, block_lane * PAIR : (block_lane + 1) * PAIR]
-    copies = [send(part_ref.at[lax.rem(me + delta, dp)], plane_ref.at[delta], delta, peer(delta)) for delta in range(1, dp)]
-    total = part_ref[me]
-    for delta in range(1, dp):
-        copies[delta - 1].wait()
-        total = total + plane_ref[delta]
-    line_ref[place] = total
-    copies = [send(line_ref.at[place], line_ref.at[place], dp + delta, line_peer(delta)) for delta in range(1, seq)]
-    for copy in copies:
+    for copy in line_copies:
         copy.wait()
     total = line_ref[0]
     for other in range(1, seq):
         total = total + line_ref[other]
     sum_out[me] = total
-    copies = [send(sum_out.at[me], sum_out.at[me], dp + seq + delta, peer(delta)) for delta in range(1, dp)]
+    copies = [sum_copy(sum_out.at[me], sum_out.at[me], dp + seq + delta, peer(delta)) for delta in range(1, dp)]
+    for copy in copies:
+        copy.start()
     for s in range(seq - 4, 0, -1):
         chain(last, s)
     chain_end(last, last % 2, back_ref)
@@ -751,7 +769,7 @@
     grad_store(last, last % 2).wait()
 
 
-def run_block(plane, seq, x, seg, small, vectors, shards, gout):
+def run_block(plane, seq, x, seg, adapters, vectors, shards, gout):
     rows, tokens, width = x.shape
     assert rows == 3
     length = seq * tokens
@@ -776,7 +794,7 @@
 
     result = pl.pallas_call(
         partial(block_kernel, plane, seq, rows, block),
-        in_specs=[anywhere] * 17,
+        in_specs=[anywhere] * 20,
         out_specs=[anywhere, anywhere, vmem] + [anywhere] * 6,
         out_shape=[
             shape(rows, tokens, width), shape(rows, tokens, width, dtype=F32), shape(dp, piece, PAIR, dtype=F32),
@@ -784,7 +802,7 @@
             shape(rows, tokens, width), shape(rows, tokens, width), shape(rows, tokens, width, dtype=F32),
         ],
         scratch_shapes=[
-            *(held(*a.shape, dtype=a.dtype) for a in (x, seg, small, *vectors)), dma((12,)),
+            *(held(*a.shape, dtype=a.dtype) for a in (x, seg, *adapters, *vectors)), held(16, width), dma((15,)),
             held(width, 3 * width), held(width, width), held(columns, width, hidden_units // columns), held(columns, hidden_units // columns, width),
             held(rows, seq, tokens, width), held(tokens, width), held(length, width), held(length, width),
             held(tokens, width), held(tokens, width), held(tokens, width),
@@ -805,7 +823,7 @@
             vmem_limit_bytes=VMEM_BYTES, collective_id=0, has_side_effects=True
         ),
         name="block",
-    )(x, seg, small, *vectors, *shards, gout)
+    )(x, seg, *adapters, *vectors, *shards, gout)
     out, grad, total = result[:3]
     flat = total.reshape(-1, PAIR)[: 16 * width // PAIR]
     return out, grad, flat.reshape(2, width // PAIR, 8, PAIR).transpose(0, 2, 1, 3).reshape(2, 8, width)
@@ -838,7 +856,7 @@
     rows, tokens, width = block_input.shape
     rank = query_up.shape[0]
     side = math.isqrt(dp // 2)
-    small = jnp.concatenate([query_adapter_reduce.T, value_adapter_reduce.T, query_up, value_up], axis=0)
+    adapters = (query_adapter_reduce.T, value_adapter_reduce.T, query_up, value_up)
 
     def as_row(vector):
         return vector.reshape(1, -1)
@@ -848,7 +866,7 @@
         for a in (ln1_gain, ln1_bias, query_bias, value_bias, out_bias, ln2_gain, ln2_bias, proj_bias, fc_bias)
     )
     out, grad, sums = run_block(
-        (side, dp // (2 * side)), seq, block_input, seg_start, small, vectors,
+        (side, dp // (2 * side)), seq, block_input, seg_start, adapters, vectors,
         (qkv_weight, out_weight, fc_weight, proj_weight), grad_out,
     )
     reduce, up = sums[0], sums[1]

time: 251 us -> 248 us (0.988)
  no operation moved by 1% of the time
where the time goes in v8:
time: 248 us
  Pallas kernels  241 us (97%)
  local copies, waits for them, and re-layouts  5.99 us (2%)
    pallas_call x1, Pallas kernels, run_block(): pl.pallas_call(partial(block_kernel, plane, seq, rows, block), in_specs=[...  241 us

profile of v8, /device:TPU:0, one launch (start us, length us, event | category | flops | bytes accessed | tf_op | source)
XLA Modules:
  0.0 248.0 jit_solution(941283477769835288)
XLA Ops:
  0.6 241.4 %block.1 = (bf16[3,256,1024]{2,1,0:T(8,128)(2,1)}, f32[3,256,1024]{2,1,0:T(8,128)}, f32[8,16,128]{2,1,0:T(8,128)}, bf16[3,256,1024]{2,1,0:T(8,128)(2,1)}, bf16[3...) custom-call(bf16[3,256,1024]{2,1,0:T(8,128)(2,1)} %x_in.1, ...), custom_call_target="tpu_custom_call" | custom-call | tf_op jit(solution)/shard_map/block/pallas_call | solution.py:795
  242.0 1.5 slice_bitcast_fusion
  243.5 0.0 copy-start
  243.5 2.8 %copy.30 = bf16[3,256,1024]{2,1,0:T(8,128)(2,1)} copy(bf16[3,256,1024]{2,1,0:T(8,128)(2,1)} %get-tuple-element.22) | data formatting | bytes 3145728
  246.3 0.0 copy-done
  246.3 1.7 copy.31
Async XLA Ops:
  243.5 2.8 %copy-start = (f32[3,256,1024]{2,1,0:T(8,128)S(1)}, f32[3,256,1024]{2,1,0:T(8,128)}, u32[]{:S(2)}) copy-start(f32[3,256,1024]{2,1,0:T(8,128)} %get-tuple-element.23) | copy-start | bytes 9437188

commit v9 on v8

--- a/solution.py
+++ b/solution.py
@@ -80,12 +80,15 @@
         pltpu.make_async_copy(source, target, input_sems.at[i])
         for i, (source, target) in enumerate(
             (
-                (x_in, x_ref), (gain1_in, gain1), (shift1_in, shift1), (seg_in, seg_ref),
+                (x_in.at[0], x_ref.at[0]), (gain1_in, gain1), (shift1_in, shift1), (seg_in, seg_ref),
                 (reduce_q_in, reduce_q), (reduce_v_in, reduce_v), (up_q_in, up_q), (up_v_in, up_v),
                 (bias_q_in, bias_q), (bias_v_in, bias_v), (out_bias_in, out_bias), (gain2_in, gain2),
                 (shift2_in, shift2), (proj_bias_in, proj_bias), (fc_bias_in, fc_bias),
             )
         )
+    ]
+    later_inputs = [
+        pltpu.make_async_copy(x_in.at[row], x_ref.at[row], input_sems.at[14 + row]) for row in range(1, rows)
     ]
     tokens, width = x_ref.shape[1], x_ref.shape[2]
     quads = width // QUAD
@@ -252,8 +255,6 @@
     small_ref[:8, :] = jnp.concatenate([reduce_q[...].astype(F32), reduce_v[...].astype(F32)], axis=0).astype(BF16)
     small_ref[8:, :] = jnp.concatenate([up_q[...].astype(F32), up_v[...].astype(F32)], axis=0).astype(BF16)
     dq_ref[:, :8] = small_ref[:8, :].astype(F32).T
-    pl.semaphore_wait(barrier, dp + seq - 2)
-    hop_start(0, 1)
     own_copies[0].wait()
     size = shard_in.shape[0]
     mine = pl.ds(pl.multiple_of(me * size, size), size)
@@ -264,11 +265,15 @@
         span = slice(column * width, (column + 1) * width)
         change = dot_nn(reduce_own, rank_up) * ADAPTER_SCALE
         w_held[mine, span] = (w_held[mine, span].astype(F32) + change).astype(BF16)
+    pl.semaphore_wait(barrier, dp + seq - 2)
     wave_one(0)
+    hop_start(0, 1)
+    for copy in later_inputs:
+        copy.start()
     for copy in own_copies[1:]:
         copy.start()
     gout_load(0).start()
-    for copy in inputs[8:] + inputs[3:4] + own_copies[1:]:
+    for copy in inputs[8:] + inputs[3:4] + own_copies[1:] + later_inputs:
         copy.wait()
     own_starts(seg_ref, begin_ref, place, seq)
     for row in range(1, rows):
@@ -802,7 +807,7 @@
             shape(rows, tokens, width), shape(rows, tokens, width), shape(rows, tokens, width, dtype=F32),
         ],
         scratch_shapes=[
-            *(held(*a.shape, dtype=a.dtype) for a in (x, seg, *adapters, *vectors)), held(16, width), dma((15,)),
+            *(held(*a.shape, dtype=a.dtype) for a in (x, seg, *adapters, *vectors)), held(16, width), dma((14 + rows,)),
             held(width, 3 * width), held(width, width), held(columns, width, hidden_units // columns), held(columns, hidden_units // columns, width),
             held(rows, seq, tokens, width), held(tokens, width), held(length, width), held(length, width),
             held(tokens, width), held(tokens, width), held(tokens, width),

time: 248 us -> 248 us (level)
  no operation moved by 1% of the time
where the time goes in v9:
time: 248 us
  Pallas kernels  241 us (97%)
  local copies, waits for them, and re-layouts  5.99 us (2%)
    pallas_call x1, Pallas kernels, run_block(): pl.pallas_call(partial(block_kernel, plane, seq, rows, block), in_specs=[...  241 us

profile of v9, /device:TPU:0, one launch (start us, length us, event | category | flops | bytes accessed | tf_op | source)
XLA Modules:
  0.0 247.9 jit_solution(3756753044867461386)
XLA Ops:
  0.6 241.3 %block.1 = (bf16[3,256,1024]{2,1,0:T(8,128)(2,1)}, f32[3,256,1024]{2,1,0:T(8,128)}, f32[8,16,128]{2,1,0:T(8,128)}, bf16[3,256,1024]{2,1,0:T(8,128)(2,1)}, bf16[3...) custom-call(bf16[3,256,1024]{2,1,0:T(8,128)(2,1)} %x_in.1, ...), custom_call_target="tpu_custom_call" | custom-call | tf_op jit(solution)/shard_map/block/pallas_call | solution.py:800
  241.9 1.5 slice_bitcast_fusion
  243.4 0.0 copy-start
  243.4 2.8 %copy.30 = bf16[3,256,1024]{2,1,0:T(8,128)(2,1)} copy(bf16[3,256,1024]{2,1,0:T(8,128)(2,1)} %get-tuple-element.22) | data formatting | bytes 3145728
  246.2 0.0 copy-done
  246.2 1.7 copy.31
Async XLA Ops:
  243.4 2.8 %copy-start = (f32[3,256,1024]{2,1,0:T(8,128)S(1)}, f32[3,256,1024]{2,1,0:T(8,128)}, u32[]{:S(2)}) copy-start(f32[3,256,1024]{2,1,0:T(8,128)} %get-tuple-element.23) | copy-start | bytes 9437188
